TPU v7x, 32 devices: a whole 2x2x4 slice. The times are simulated.
32 devices in a mesh: grp: 1, uly: 8 (over z, y), doc: 4 (over x, core).
Axes of the slice: x: 2, y: 2, z: 4, core: 2. Of those that a mesh axis runs over, the one named last changes fastest.
Arguments:
- queries: bfloat16 [4096, 2048], P(('grp', 'doc', 'uly')), may hold values from -4 to 4
- key_vectors: bfloat16 [4096, 2048], P(('grp', 'doc', 'uly')), may hold values from -4 to 4
- value_vectors: bfloat16 [4096, 2048], P(('grp', 'doc', 'uly')), may hold values from -6 to 6
- layout: int32 [32, 32, 32], P('grp'), may hold values from 0 to 31, as said below
- counts: int32 [32, 32], P('grp'), may hold values from 1 to 32, as said below
Outputs:
- attended: bfloat16 [4096, 2048], P(('grp', 'doc', 'uly'))
Inputs may be any that keep to these rules, and one draw needn't show every extreme that they name: layout[h, b, 0] = b; the first counts[h, b] entries of a row are distinct blocks; later entries name blocks that are not attended.
All inputs are finite; a program needn't handle non-finite values.
Results may differ from a plain program's by a relative error of at most 0.0055.
Values may be sent and summed in bfloat16 or wider, within the bound.
No kernel may reach another device: no remote copies, remote signals or barrier semaphores. Data moves between devices by JAX's collectives and lax.ppermute only.
A program may use at most 64 MiB of HBM per device.

v0:
```python
import jax
import jax.numpy as jnp
from jax import lax
from jax.sharding import PartitionSpec as P

H = 32
DH = 64
BLK = 128
KMAX = 32


def attend_head(head_of_query, key_head, value_head, head_layout, head_counts):
    query_blocks = head_of_query.shape[0]

    def advance(step_index, carry):
        running_max, running_sum, accumulated = carry
        key_ids = lax.dynamic_slice_in_dim(head_layout, step_index * 4, 4, axis=1)
        live_slots = (step_index * 4 + jnp.arange(4, dtype=jnp.int32))[None, :] < head_counts[
            :, None
        ]
        key_block_list = jnp.take(key_head, key_ids, axis=0).reshape(query_blocks, 4 * BLK, DH)
        value_block_list = jnp.take(value_head, key_ids, axis=0).reshape(query_blocks, 4 * BLK, DH)
        logit_scores = jnp.einsum(
            "vth,vlh->vtl", head_of_query, key_block_list, preferred_element_type=jnp.float32
        )
        slot_mask = jnp.repeat(live_slots, BLK, axis=1)[:, None, :]
        logit_scores = jnp.where(slot_mask, logit_scores, -jnp.inf)
        new_max = jnp.maximum(running_max, jnp.max(logit_scores, axis=-1))
        rescale = jnp.exp(running_max - new_max)
        weights = jnp.exp(logit_scores - new_max[..., None])
        running_sum = running_sum * rescale + jnp.sum(weights, axis=-1)
        product = jnp.einsum(
            "hyc,hcr->hyr",
            weights.astype(jnp.bfloat16),
            value_block_list,
            preferred_element_type=jnp.float32,
        )
        accumulated = accumulated * rescale[..., None] + product
        return (new_max, running_sum, accumulated)

    start_max = jnp.full((query_blocks, BLK), -jnp.inf, jnp.float32)
    start_sum = jnp.zeros((query_blocks, BLK), jnp.float32)
    start_acc = jnp.zeros((query_blocks, BLK, DH), jnp.float32)
    count_of_steps = (jnp.max(head_counts) + 3) // 4
    final_max, final_sum, accumulated = lax.fori_loop(
        0, count_of_steps, advance, (start_max, start_sum, start_acc)
    )
    return (accumulated / final_sum[..., None]).astype(jnp.bfloat16)


def shards(queries, key_vectors, value_vectors, layout, counts):
    uly_count = lax.axis_size("uly")
    doc_count = lax.axis_size("doc")
    uly_index = lax.axis_index("uly")
    doc_index = lax.axis_index("doc")
    local_rows = queries.shape[0]
    per_device = H // uly_count
    width = per_device * DH
    slab_rows = local_rows * uly_count
    slab_blocks = slab_rows // BLK
    all_blocks = slab_blocks * doc_count
    head_order = jnp.arange(H, dtype=jnp.int32)

    def arrange(tensor, row_count):
        return tensor.reshape(row_count, uly_count, width)

    query_heads, key_heads, value_heads = (
        lax.all_to_all(
            arrange(queries, local_rows), "uly", split_axis=1, concat_axis=0, tiled=True
        ),
        lax.all_to_all(
            arrange(key_vectors, local_rows), "uly", split_axis=1, concat_axis=0, tiled=True
        ),
        lax.all_to_all(
            arrange(value_vectors, local_rows), "uly", split_axis=1, concat_axis=0, tiled=True
        ),
    )
    key_full, value_full = (
        lax.all_gather(key_heads.reshape(slab_rows, width), "doc", axis=0, tiled=True),
        lax.all_gather(value_heads.reshape(slab_rows, width), "doc", axis=0, tiled=True),
    )
    query_slab = query_heads.reshape(slab_rows, width)
    my_heads = lax.dynamic_slice_in_dim(head_order, uly_index * per_device, per_device)
    pieces = []
    for local_head in range(per_device):
        head_id = my_heads[local_head]
        head_layout = lax.dynamic_slice(
            layout, (head_id, doc_index * slab_blocks, 0), (1, slab_blocks, KMAX)
        )[0]
        head_counts = lax.dynamic_slice(
            counts, (head_id, doc_index * slab_blocks), (1, slab_blocks)
        )[0]
        first_column = local_head * DH
        head_of_query = query_slab[:, first_column : first_column + DH].reshape(
            slab_blocks, BLK, DH
        )
        key_head = key_full[:, first_column : first_column + DH].reshape(all_blocks, BLK, DH)
        value_head = value_full[:, first_column : first_column + DH].reshape(all_blocks, BLK, DH)
        result_head = attend_head(head_of_query, key_head, value_head, head_layout, head_counts)
        pieces.append(result_head.reshape(slab_rows, DH))
    local_output = jnp.concatenate(pieces, axis=1).reshape(slab_rows, 1, width)
    returned = lax.all_to_all(local_output, "uly", split_axis=0, concat_axis=1, tiled=True)
    return returned.reshape(local_rows, H * DH)


def solution(mesh):
    placed = (
        P(("grp", "doc", "uly"), None),
        P(("grp", "doc", "uly"), None),
        P(("grp", "doc", "uly"), None),
        P("grp", None, None),
        P("grp", None),
    )
    return jax.shard_map(
        shards,
        mesh=mesh,
        in_specs=placed,
        out_specs=P(("grp", "doc", "uly"), None),
        check_vma=False,
    )
```

profile of v0, /device:TPU:0, one launch (start us, length us, event | category | flops | bytes accessed | tf_op | source)
XLA Modules:
  0.0 329.0 jit_solution(13724909617248755911)
XLA Ops:
  8.1 21.7 %all_to_all.60 = bf16[128,8,256]{2,0,1:T(8,128)(2,1)} all-to-all(bf16[128,8,256]{2,0,1:T(8,128)(2,1)S(1)} %copy.120), channel_id=1, replica_groups=mesh['grp'=1,'uly'=8,'doc'=4] {'uly'}, dimensions={1} | all-to-all | bytes 1048576 | tf_op jit(solution)/shard_map/all_to_all | solution.py:71
  30.4 17.6 %all_to_all.61 = bf16[128,8,256]{2,0,1:T(8,128)(2,1)} all-to-all(bf16[128,8,256]{2,0,1:T(8,128)(2,1)S(1)} %copy.125), channel_id=1, replica_groups=mesh['grp'=1,'uly'=8,'doc'=4] {'uly'}, dimensions={1} | all-to-all | bytes 1048576 | tf_op jit(solution)/shard_map/all_to_all | solution.py:74
  49.1 3.6 %all-to-all-start.1 = ((bf16[128,8,256]{0,2,1:T(8,128)(2,1)}), bf16[128,8,256]{0,2,1:T(8,128)(2,1)S(1)}, u32[]{:S(2)}, u32[]{:S(2)}) async-start(bf16[128,8,256]{0,2,1:T(8,128)(2,1)} %bitcast.35), calls=%async_computation.1 | async-start | bytes 1048576 | tf_op jit(solution)/shard_map/all_to_all | solution.py:68
  60.6 2.2 fusion.36
  69.8 4.6 %fusion.41 = (bf16[4096,64]{1,0:T(8,128)(2,1)}, bf16[4096,64]{1,0:T(8,128)(2,1)}, bf16[4096,64]{1,0:T(8,128)(2,1)S(1)}, bf16[4096,64]{1,0:T(8,128)(2,1)}) fusion(bf16[4096,256]{1,0:T(8,128)(2,1)} %all-gather.3.cloned.1.call-done), kind=kLoop, calls=%fused_computation.110 | loop fusion | bytes 4194304 | tf_op jit(solution)/shard_map/slice | solution.py:97
  75.8 4.4 %fusion.40 = (bf16[4096,64]{1,0:T(8,128)(2,1)}, bf16[4096,64]{1,0:T(8,128)(2,1)}, bf16[4096,64]{1,0:T(8,128)(2,1)}, bf16[4096,64]{1,0:T(8,128)(2,1)S(1)}) fusion(bf16[4096,256]{1,0:T(8,128)(2,1)} %all-gather.5.cloned.1.call-done), kind=kLoop, calls=%fused_computation.109 | loop fusion | bytes 4194304 | tf_op jit(solution)/shard_map/slice | solution.py:98
  80.3 18.0 %while.57 = (s32[]{:T(128)}, f32[8,128]{1,0:T(8,128)S(1)}, f32[8,128]{1,0:T(8,128)S(1)}, f32[8,128,64]{1,2,0:T(8,128)S(1)}, s32[]{:T(128)}, /*index=5*/s32[1,8]{...) while((s32[]{:T(128)}, f32[8,128]{1,0:T(8,128)S(1)}, ...), condition=%wide.region_9.11_spmd, body=%wide.region_6.10_spmd.sunk | while | flops 139070688 | bytes 16995820 | solution.py:45
  86.8 2.4 convolution_add_fusion.9
  95.8 2.4 convolution_add_fusion.9
  99.1 22.9 %while.56 = (s32[]{:T(128)}, f32[8,128]{1,0:T(8,128)S(1)}, f32[8,128]{1,0:T(8,128)S(1)}, f32[8,128,64]{1,2,0:T(8,128)}, s32[]{:T(128)}, /*index=5*/s32[1,8]{1,0:...) while((s32[]{:T(128)}, f32[8,128]{1,0:T(8,128)S(1)}, ...), condition=%wide.region_4.6_spmd, body=%wide.region_1.5_spmd.sunk | while | flops 139070688 | bytes 14898667 | solution.py:45
  107.4 2.4 convolution_add_fusion.8
  111.9 2.0 gather_fusion
  118.9 2.4 convolution_add_fusion.8
  122.6 86.7 %while.59 = (s32[]{:T(128)}, f32[8,128]{1,0:T(8,128)S(1)}, f32[8,128]{1,0:T(8,128)}, f32[8,128,64]{1,2,0:T(8,128)S(1)}, s32[]{:T(128)}, /*index=5*/s32[1,8]{1,0:...) while((s32[]{:T(128)}, f32[8,128]{1,0:T(8,128)S(1)}, ...), condition=%wide.region_19.21_spmd, body=%wide.region_16.20_spmd.sunk | while | flops 139070688 | bytes 12834283 | solution.py:45
  131.0 2.4 convolution_add_fusion.11
  141.8 2.4 convolution_add_fusion.11
  152.7 2.4 convolution_add_fusion.11
  163.5 2.4 convolution_add_fusion.11
  174.4 2.4 convolution_add_fusion.11
  185.2 2.4 convolution_add_fusion.11
  196.1 2.4 convolution_add_fusion.11
  206.9 2.4 convolution_add_fusion.11
  210.1 76.3 %while.58 = (s32[]{:T(128)}, f32[8,128]{1,0:T(8,128)S(1)}, f32[8,128]{1,0:T(8,128)S(1)}, f32[8,128,64]{1,2,0:T(8,128)S(1)}, s32[]{:T(128)}, /*index=5*/s32[1,8]{...) while((s32[]{:T(128)}, f32[8,128]{1,0:T(8,128)S(1)}, ...), condition=%wide.region_14.16_spmd, body=%wide.region_11.15_spmd.sunk | while | flops 139070688 | bytes 12277143 | solution.py:45
  217.2 2.4 convolution_add_fusion.10
  226.7 2.4 convolution_add_fusion.10
  236.3 2.4 convolution_add_fusion.10
  245.8 2.4 convolution_add_fusion.10
  255.3 2.4 convolution_add_fusion.10
  264.9 2.4 convolution_add_fusion.10
  274.4 2.4 convolution_add_fusion.10
  283.9 2.4 convolution_add_fusion.10
  290.4 29.8 %all_to_all.62 = bf16[8,2,16384]{2,1,0:T(2,128)(2,1)S(1)} all-to-all(bf16[8,2,16384]{2,1,0:T(2,128)(2,1)S(1)} %reshape.281), channel_id=1, replica_groups=mesh['grp'=1,'uly'=8,'doc'=4] {'uly'}, dimensions={0} | all-to-all | bytes 1048576 | tf_op jit(solution)/shard_map/all_to_all | solution.py:102
  (446 shorter events, 168.1 us)
Async XLA Ops:
  6.5 23.4 %copy-start.9 = (bf16[128,2048]{1,0:T(8,128)(2,1)S(1)}, bf16[128,2048]{1,0:T(8,128)(2,1)}, u32[]{:S(2)}) copy-start(bf16[128,2048]{1,0:T(8,128)(2,1)} %param.17) | copy-start | bytes 1572868
  6.5 63.2 %all-gather.3.cloned.1.call-start = ((), (), s32[]{:S(2)}) async-start(), calls=%async_computation.4 | async-start | bytes 2621440 | tf_op jit(solution)/shard_map/all_gather | solution.py:79
  29.9 18.2 %copy-start.10 = (bf16[128,2048]{1,0:T(8,128)(2,1)S(1)}, bf16[128,2048]{1,0:T(8,128)(2,1)}, u32[]{:S(2)}) copy-start(bf16[128,2048]{1,0:T(8,128)(2,1)} %param.15) | copy-start | bytes 1572868
  29.9 45.9 %all-gather.5.cloned.1.call-start = ((), (), s32[]{:S(2)}) async-start(), calls=%async_computation.5 | async-start | bytes 2621440 | tf_op jit(solution)/shard_map/all_gather | solution.py:80
  49.1 17.7 %all-to-all-start.1 = ((bf16[128,8,256]{0,2,1:T(8,128)(2,1)}), bf16[128,8,256]{0,2,1:T(8,128)(2,1)S(1)}, u32[]{:S(2)}, u32[]{:S(2)}) async-start(bf16[128,8,256]{0,2,1:T(8,128)(2,1)} %bitcast.35), calls=%async_computation.1 | async-start | bytes 1048576 | tf_op jit(solution)/shard_map/all_to_all | solution.py:68
  80.3 1.6 copy-start
  86.8 2.5 copy-start.1
  89.3 1.6 copy-start
  95.8 2.5 copy-start.1
  105.6 1.8 copy-start.3
  117.0 1.8 copy-start.3
  128.0 1.1 copy-start.6
  129.1 1.8 copy-start.12
  131.0 2.5 copy-start.13
  138.8 1.1 copy-start.6
  140.0 1.8 copy-start.12
  141.8 2.5 copy-start.13
  149.7 1.1 copy-start.6
  150.8 1.8 copy-start.12
  152.7 2.5 copy-start.13
  160.5 1.1 copy-start.6
  161.7 1.8 copy-start.12
  163.5 2.5 copy-start.13
  172.5 1.8 copy-start.12
  174.4 2.5 copy-start.13
  182.2 1.1 copy-start.6
  183.4 1.8 copy-start.12
  185.2 2.5 copy-start.13
  194.2 1.8 copy-start.12
  196.0 2.5 copy-start.13
  205.1 1.8 copy-start.12
  206.9 2.5 copy-start.13
  (32 other events, 30.6 us)
Sparse Core Ops, SparseCore 0:
  30.0 21.5 all-gather.2
  53.2 22.5 all-gather.4
where the time goes:
time: 331 us; the launch traced here: 329 us
  local copies, waits for them, and re-layouts  93.5 us (28%)
  blocking collectives  69.2 us (21%)
  matrix products  69.1 us (21%)
  other arithmetic  66 us (20%)
  between operations  23.4 us (7%)
  starting transfers between devices  3.68 us (1%)
    dot_general x20, matrix products, advance(): jnp.einsum('hyc,hcr->hyr', weights.astype(jnp.bfloat16), value_block_list...  48.7 us
    gather x20, local copies, waits for them, and re-layouts, advance(): jnp.take(value_head, key_ids, axis=0).reshape(query_blocks, 4 * BLK, DH)  37 us
    all_to_all x1, blocking collectives, shards(): lax.all_to_all(local_output, 'uly', split_axis=0, concat_axis=1, tiled=True)  29.8 us
    gather x20, local copies, waits for them, and re-layouts, advance(): jnp.take(key_head, key_ids, axis=0).reshape(query_blocks, 4 * BLK, DH)  29.7 us
    and x20, other arithmetic, advance(): jnp.take(key_head, key_ids, axis=0).reshape(query_blocks, 4 * BLK, DH)  25.2 us
    all_to_all x1, blocking collectives, shards(): lax.all_to_all(arrange(key_vectors, local_rows), 'uly', split_axis=1, con...  21.7 us
    dot_general x20, matrix products, advance(): jnp.einsum('vth,vlh->vtl', head_of_query, key_block_list, preferred_eleme...  20.3 us
    select_n x20, other arithmetic, advance(): jnp.take(value_head, key_ids, axis=0).reshape(query_blocks, 4 * BLK, DH)  18.4 us
  transfers between devices with their start and end apart: 3, of which 1 were waited for; matrix products, arithmetic and copies ran while one was open for 4% of the time, Pallas kernels for 0%

commit v1 on v0

v1 whole, which is shorter than its diff:
```python
import functools

import jax
import jax.numpy as jnp
from jax import lax
from jax.experimental import pallas as pl
from jax.experimental.pallas import tpu as pltpu
from jax.sharding import PartitionSpec as P

H = 32
DH = 64
BLK = 128
KMAX = 32
UNROLL = 4
BIG = 1e30
VMEM = pl.BlockSpec(memory_space=pltpu.VMEM)
SMEM = pl.BlockSpec(memory_space=pltpu.SMEM)
PARAMS = pltpu.CompilerParams(vmem_limit_bytes=58 << 20)


def pack_kernel(head_ref, place_ref, q_ref, k_ref, v_ref, qt_ref, kp_ref, vt_ref):
    per = kp_ref.shape[2] // DH
    low = lax.broadcasted_iota(jnp.int32, (BLK, 2 * DH), 1) < DH
    for pair in range(H // 2):
        lanes = slice(pair * 2 * DH, (pair + 1) * 2 * DH)
        for source, target in ((q_ref, qt_ref), (v_ref, vt_ref)):
            turned = source[:, lanes].T
            target[place_ref[2 * pair]] = turned[:DH]
            target[place_ref[2 * pair + 1]] = turned[DH:]

        def fetch(place, odd):
            head = head_ref[place]
            start = pl.multiple_of((head // 2) * (2 * DH), 2 * DH)
            block = k_ref[:, pl.ds(start, 2 * DH)]
            swapped = jnp.concatenate([block[:, DH:], block[:, :DH]], axis=1)
            return jnp.where((head % 2) == odd, block, swapped)

        joined = jnp.where(low, fetch(2 * pair, 0), fetch(2 * pair + 1, 1))
        group, slot = divmod(2 * pair, per)
        kp_ref[group, :, slot * DH : slot * DH + 2 * DH] = joined


def attend_kernel(lay_ref, cnt_ref, qt_ref, k_ref, vt_ref, o_ref, unit_ref, qz_ref, m_ref, l_ref, acc_ref):
    slab, width, _ = qt_ref.shape
    per = width // DH
    rows = per * slab

    def place_row(row, base):
        count = cnt_ref[row]
        units = (count + 1) // 2

        def place_unit(step, _):
            first = lay_ref[row * KMAX + 2 * step]
            whole = 2 * step + 1 < count
            second = jnp.where(whole, lay_ref[row * KMAX + 2 * step + 1], first)
            unit_ref[0, base + step] = row
            unit_ref[1, base + step] = first
            unit_ref[2, base + step] = second
            unit_ref[3, base + step] = whole.astype(jnp.int32)
            return 0

        lax.fori_loop(0, units, place_unit, 0)
        return base + units

    total = lax.fori_loop(0, rows, place_row, 0)
    for extra in range(UNROLL):
        unit_ref[0, total + extra] = rows
        unit_ref[1, total + extra] = 0
        unit_ref[2, total + extra] = 0
        unit_ref[3, total + extra] = 1

    zeros = jnp.zeros((DH, BLK), jnp.bfloat16)
    for head in range(per):
        for block in range(slab):
            part = qt_ref[block, head * DH : (head + 1) * DH, :]
            both = [part, zeros] if head % 2 == 0 else [zeros, part]
            qz_ref[head * slab + block] = jnp.concatenate(both, axis=0)
    m_ref[...] = jnp.full(m_ref.shape, -BIG, jnp.float32)
    l_ref[...] = jnp.zeros(l_ref.shape, jnp.float32)
    acc_ref[...] = jnp.zeros(acc_ref.shape, jnp.float32)
    qz_ref[rows] = jnp.zeros((2 * DH, BLK), jnp.bfloat16)

    def one(unit):
        row = unit_ref[0, unit]
        first = unit_ref[1, unit]
        second = unit_ref[2, unit]
        whole = unit_ref[3, unit]
        head = jnp.minimum(row // slab, per - 1)
        lanes = pl.ds(pl.multiple_of((head // 2) * (2 * DH), 2 * DH), 2 * DH)
        weights = qz_ref[row]
        keys = jnp.concatenate([k_ref[first, :, lanes], k_ref[second, :, lanes]], axis=0)
        scores = jnp.dot(keys, weights, preferred_element_type=jnp.float32)
        tiles = scores.reshape(2 * BLK // 8, 8, BLK)
        top = jnp.max(tiles, axis=0)
        top = jnp.max(top, axis=0, keepdims=True)
        limit = jnp.where(whole == 1, top, top + BIG)
        first_w = jnp.exp(scores[:BLK] - top)
        second_w = jnp.exp(scores[BLK:] - limit)
        w = jnp.concatenate([first_w, second_w], axis=0)
        part_sum = jnp.sum(w.reshape(2 * BLK // 8, 8, BLK), axis=0)
        span = pl.ds(pl.multiple_of(head * DH, DH), DH)
        values = jnp.concatenate([vt_ref[first, span, :], vt_ref[second, span, :]], axis=1)
        out = jnp.dot(values, w.astype(jnp.bfloat16), preferred_element_type=jnp.float32)
        return row, top, part_sum, out

    def step(index, _):
        done = [one(index * UNROLL + lane) for lane in range(UNROLL)]
        for row, top, part_sum, out in done:
            old = m_ref[row]
            new = jnp.maximum(old, top)
            a = jnp.exp(old - new)
            b = jnp.exp(top - new)
            m_ref[row] = new
            l_ref[row] = l_ref[row] * a + part_sum * b
            acc_ref[row] = (
                acc_ref[row].reshape(DH // 8, 8, BLK) * a[None] + out.reshape(DH // 8, 8, BLK) * b[None]
            ).reshape(DH, BLK)
        return 0

    lax.fori_loop(0, (total + UNROLL - 1) // UNROLL, step, 0)

    for head in range(per):
        for block in range(slab):
            row = head * slab + block
            total_w = jnp.sum(l_ref[row], axis=0, keepdims=True)
            o_ref[block, head * DH : (head + 1) * DH, :] = (acc_ref[row] / total_w).astype(jnp.bfloat16)


def unpack_kernel(place_ref, o_ref, out_ref):
    for pair in range(H // 2):
        both = jnp.concatenate([o_ref[place_ref[2 * pair]], o_ref[place_ref[2 * pair + 1]]], axis=0)
        out_ref[:, pair * 2 * DH : (pair + 1) * 2 * DH] = both.T


def places_of(counts, groups):
    load = jnp.sum(counts, axis=1)
    ids = jnp.arange(H, dtype=jnp.int32)
    ahead = (load[None, :] > load[:, None]) | ((load[None, :] == load[:, None]) & (ids[None, :] < ids[:, None]))
    rank = jnp.sum(ahead.astype(jnp.int32), axis=1)
    turn, seat = rank // groups, rank % groups
    group = jnp.where(turn % 2 == 0, seat, groups - 1 - seat)
    place = group * (H // groups) + turn
    head_at = jnp.sum(jnp.where(place[None, :] == ids[:, None], ids[None, :], 0), axis=1)
    return head_at, place


def shards(queries, key_vectors, value_vectors, layout, counts):
    uly = lax.axis_size("uly")
    per = H // uly
    width = per * DH
    slab = queries.shape[0] // BLK * uly
    bf16 = jnp.bfloat16
    head_at, place = places_of(counts, uly)
    shape = jax.ShapeDtypeStruct
    qt, kp, vt = pl.pallas_call(
        pack_kernel,
        out_shape=(shape((H, DH, BLK), bf16), shape((uly, BLK, width), bf16), shape((H, DH, BLK), bf16)),
        in_specs=[SMEM, SMEM, VMEM, VMEM, VMEM],
        out_specs=(VMEM, VMEM, VMEM),
        compiler_params=PARAMS,
        name="pack",
    )(head_at, place, queries, key_vectors, value_vectors)
    swap = functools.partial(lax.all_to_all, axis_name="uly", split_axis=0, concat_axis=0, tiled=True)
    kp = swap(kp)
    k_full = lax.all_gather(kp, "doc", axis=0, tiled=True)
    vt = swap(vt.reshape(uly, width, BLK))
    v_full = lax.all_gather(vt, "doc", axis=0, tiled=True)
    qt = swap(qt.reshape(uly, width, BLK))
    mine = lax.dynamic_slice_in_dim(head_at, lax.axis_index("uly") * per, per)
    begin = lax.axis_index("doc") * slab
    lay = jnp.take(lax.dynamic_slice_in_dim(layout, begin, slab, axis=1), mine, axis=0).reshape(-1)
    cnt = jnp.take(lax.dynamic_slice_in_dim(counts, begin, slab, axis=1), mine, axis=0).reshape(-1)
    rows = per * slab
    ot = pl.pallas_call(
        attend_kernel,
        out_shape=shape((slab, width, BLK), bf16),
        in_specs=[SMEM, SMEM, VMEM, VMEM, VMEM],
        out_specs=VMEM,
        scratch_shapes=[
            pltpu.SMEM((4, rows * KMAX // 2 + UNROLL), jnp.int32),
            pltpu.VMEM((rows + 1, 2 * DH, BLK), bf16),
            pltpu.VMEM((rows + 1, 8, BLK), jnp.float32),
            pltpu.VMEM((rows + 1, 8, BLK), jnp.float32),
            pltpu.VMEM((rows + 1, DH, BLK), jnp.float32),
        ],
        compiler_params=PARAMS,
        name="attend",
    )(lay, cnt, qt, k_full, v_full)
    ot = swap(ot)
    return pl.pallas_call(
        unpack_kernel,
        out_shape=shape(queries.shape, bf16),
        in_specs=[SMEM, VMEM],
        out_specs=VMEM,
        compiler_params=PARAMS,
        name="unpack",
    )(place, ot.reshape(H, DH, BLK))


def solution(mesh):
    placed = (
        P(("grp", "doc", "uly"), None),
        P(("grp", "doc", "uly"), None),
        P(("grp", "doc", "uly"), None),
        P("grp", None, None),
        P("grp", None),
    )
    return jax.shard_map(
        shards,
        mesh=mesh,
        in_specs=placed,
        out_specs=P(("grp", "doc", "uly"), None),
        check_vma=False,
    )
```

time: 331 us -> 155 us (0.47)
  local copies, waits for them, and re-layouts: 93.5 us -> 2.57 us
  matrix products: 69.1 us -> 0 us
  other arithmetic: 66 us -> 2.03 us
  Pallas kernels: 0 us -> 56.6 us
  waiting for transfers between devices: 1.5 us -> 21.6 us
  blocking collectives: 69.2 us -> 55.5 us
  between operations: 23.4 us -> 13.5 us
    dot_general x40 -> x0, matrix products: 69.1 us -> none  [the longest x20 48.7 us: advance(): jnp.einsum('hyc,hcr->hyr', weights.astype(jnp.bfloat16), value_block_list...]
    gather x40 -> x2, local copies, waits for them, and re-layouts: 66.7 us -> 1.11 us  [the longest x1 0.56 us: shards(): jnp.take(lax.dynamic_slice_in_dim(counts, begin, slab, axis=1), mine, axi...]
    pallas_call x0 -> x3, Pallas kernels: none -> 56.6 us  [the longest x1 51.3 us: shards(): pl.pallas_call(attend_kernel, out_shape=shape((slab, width, BLK), bf16),...]
    and x20 -> x1, other arithmetic: 25.2 us -> 0.08 us  [shards(): jnp.take(lax.dynamic_slice_in_dim(layout, begin, slab, axis=1), mine, axi...]
    select_n x20 -> x2, other arithmetic: 18.4 us -> 0.15 us  [the longest x1 0.07 us: shards(): jnp.take(lax.dynamic_slice_in_dim(counts, begin, slab, axis=1), mine, axi...]
    all_to_all x3, blocking collectives: 69.2 us -> 55.5 us  [the longest x1 22 us: shards(): kp = swap(kp)]
    reduce_sum x20 -> x3, other arithmetic: 15 us -> 1.78 us  [the longest x1 0.89 us: places_of(): load = jnp.sum(counts, axis=1)]
    all_to_all x1, waiting for transfers between devices: 0.01 us -> 11.2 us  [shards(): qt = swap(qt.reshape(uly, width, BLK))]
  transfers between devices with their start and end apart: 3 -> 3, of which waited for: 1 -> 2; matrix products, arithmetic and copies ran while one was open for 4% -> 2% of each run, Pallas kernels for 0% -> 0%
where the time goes in v1:
time: 155 us
  Pallas kernels  56.6 us (37%)
  blocking collectives  55.5 us (36%)
  waiting for transfers between devices  21.6 us (14%)
  between operations  13.5 us (9%)
  starting transfers between devices  3.69 us (2%)
  local copies, waits for them, and re-layouts  2.57 us (2%)
  other arithmetic  2.03 us (1%)
    pallas_call x1, Pallas kernels, shards(): pl.pallas_call(attend_kernel, out_shape=shape((slab, width, BLK), bf16),...  51.3 us
    all_to_all x1, blocking collectives, shards(): kp = swap(kp)  22 us
    all_to_all x1, blocking collectives, shards(): vt = swap(vt.reshape(uly, width, BLK))  17.8 us
    all_to_all x1, blocking collectives, shards(): ot = swap(ot)  15.6 us
    all_to_all x1, waiting for transfers between devices, shards(): qt = swap(qt.reshape(uly, width, BLK))  11.2 us
    all_gather x1, waiting for transfers between devices, shards(): v_full = lax.all_gather(vt, 'doc', axis=0, tiled=True)  10.3 us
    all_to_all x1, starting transfers between devices, shards(): qt = swap(qt.reshape(uly, width, BLK))  3.65 us
    pallas_call x1, Pallas kernels, shards(): pl.pallas_call(pack_kernel, out_shape=(shape((H, DH, BLK), bf16), shape((...  3.27 us
  transfers between devices with their start and end apart: 3, of which 2 were waited for; matrix products, arithmetic and copies ran while one was open for 2% of the time, Pallas kernels for 0%

profile of v1, /device:TPU:0, one launch (start us, length us, event | category | flops | bytes accessed | tf_op | source)
XLA Modules:
  0.0 155.4 jit_solution(17140115614974115992)
XLA Ops:
  6.5 0.0 copy-start
  6.5 0.0 all-gather.3.cloned.1.call-start
  6.5 0.9 reduce_sum.27
  7.4 0.2 convert_reduce_fusion
  7.6 0.0 copy-start.3
  7.7 0.7 select_reduce_fusion.head_ref
  8.4 0.0 copy-done.3
  8.4 3.3 %pack.1 = (bf16[32,64,128]{2,1,0:T(8,128)(2,1)}, bf16[8,128,256]{2,1,0:T(8,128)(2,1)}, bf16[32,64,128]{2,1,0:T(8,128)(2,1)}) custom-call(s32[32]{0:T(128)} %select_reduce_fusion.head_ref, s32[32]{0:T(128)} %copy-done.3, bf16[128,2048]{1,0:T(8,128)(2,1)} %q_ref.1, bf16[128,2048]{1,0:T(8,128)(2,1)} %k_ref.1, bf16[128,2048]{1,0:T(8,128)(2,1)} %v_ref.1), custom_call_target="tpu_custom_call" | custom-call | tf_op jit(solution)/shard_map/pack/pallas_call | solution.py:155
  11.6 0.0 copy-start.4
  11.6 22.0 %all_to_all.20 = bf16[8,128,256]{2,1,0:T(8,128)(2,1)} all-to-all(bf16[8,128,256]{2,1,0:T(8,128)(2,1)} %get-tuple-element.9), channel_id=1, replica_groups=mesh['grp'=1,'uly'=8,'doc'=4] {'uly'}, dimensions={0} | all-to-all | bytes 1048576 | tf_op jit(solution)/shard_map/all_to_all | solution.py:164
  33.7 0.0 all-gather.3.cloned.1.call-update
  33.7 0.0 all-gather.5.cloned.1.call-start
  33.8 17.8 %all_to_all.21 = bf16[8,256,128]{2,1,0:T(8,128)(2,1)} all-to-all(bf16[8,256,128]{2,1,0:T(8,128)(2,1)} %bitcast.4), channel_id=1, replica_groups=mesh['grp'=1,'uly'=8,'doc'=4] {'uly'}, dimensions={0} | all-to-all | bytes 1048576 | tf_op jit(solution)/shard_map/all_to_all | solution.py:166
  51.6 0.0 all-gather.5.cloned.1.call-update
  51.6 3.6 %all-to-all-start = ((bf16[8,256,128]{2,1,0:T(8,128)(2,1)}), bf16[8,256,128]{2,1,0:T(8,128)(2,1)S(1)}, u32[]{:S(2)}, u32[]{:S(2)}) async-start(bf16[8,256,128]{2,1,0:T(8,128)(2,1)} %bitcast), calls=%async_computation | async-start | bytes 1048576 | tf_op jit(solution)/shard_map/all_to_all | solution.py:168
  55.3 0.0 copy-done.4
  55.3 0.1 compare_and_fusion
  55.4 0.0 copy-done.2
  55.4 0.1 constant_dynamic-slice_fusion.1
  55.5 0.6 gather_fusion.1
  56.0 0.1 broadcast_select_fusion.1
  56.1 0.7 select_n.80.cnt_ref
  56.8 0.0 copy-done
  56.8 0.6 gather_fusion
  57.4 0.1 broadcast_select_fusion
  57.4 0.7 select_n.78.lay_ref
  58.1 11.2 %all-to-all-done.qt_ref = bf16[8,256,128]{2,1,0:T(8,128)(2,1)S(1)} async-done(((bf16[8,256,128]{2,1,0:T(8,128)(2,1)}), bf16[8,256,128]{2,1,0:T(8,128)(2,1)S(1)}, u32[]{:S(2)}, u32[]{:S(2)}) %all-to-all-start) | async-done | bytes 524320 | tf_op jit(solution)/shard_map/all_to_all | solution.py:168
  69.3 10.3 %all-gather.5.cloned.1.call-done.vt_ref = bf16[32,256,128]{2,1,0:T(8,128)(2,1)} async-done(((bf16[8,256,128]{2,1,0:T(8,128)(2,1)}), bf16[32,256,128]{2,1,0:T(8,128)(2,1)}) %all-gather.5.cloned.1.call-update) | async-done | bytes 2097168 | tf_op jit(solution)/shard_map/all_gather | solution.py:167
  79.6 0.0 copy-done.1
  79.6 51.3 %attend.1 = bf16[8,256,128]{2,1,0:T(8,128)(2,1)} custom-call(s32[1024]{0:T(1024)} %select_n.78.lay_ref, s32[32]{0:T(128)} %select_n.80.cnt_ref, bf16[8,256,128]{2,1,0:T(8,128)(2,1)} %copy-done.1, bf16[32,128,256]{2,1,0:T(8,128)(2,1)} %all-gather.3.cloned.1.call-done.k_ref, bf16[32,256,128]{2,1,0:T(8,128)(2,1)} %all-gather.5.cloned.1.call-done.vt_ref), custom_call_target="tpu_custom_call" | custom-call | tf_op jit(solution)/shard_map/attend/pallas_call | solution.py:174
  131.0 15.6 %all_to_all.22 = bf16[8,256,128]{2,1,0:T(8,128)(2,1)} all-to-all(bf16[8,256,128]{2,1,0:T(8,128)(2,1)} %attend.1), channel_id=1, replica_groups=mesh['grp'=1,'uly'=8,'doc'=4] {'uly'}, dimensions={0} | all-to-all | bytes 1048576 | tf_op jit(solution)/shard_map/all_to_all | solution.py:189
  146.6 2.0 %unpack.1 = bf16[128,2048]{1,0:T(8,128)(2,1)} custom-call(s32[32]{0:T(128)} %copy-done.3, bf16[32,64,128]{2,1,0:T(8,128)(2,1)} %bitcast.3), custom_call_target="tpu_custom_call" | custom-call | tf_op jit(solution)/shard_map/unpack/pallas_call | solution.py:190
  (6 shorter events, 0.1 us)
Async XLA Ops:
  6.5 50.2 %copy-start = (s32[32,32,32]{2,1,0:T(8,128)S(1)}, s32[32,32,32]{2,1,0:T(8,128)}, u32[]{:S(2)}) copy-start(s32[32,32,32]{2,1,0:T(8,128)} %param.8) | copy-start | bytes 393220
  6.5 62.8 %all-gather.3.cloned.1.call-start = ((), (), s32[]{:S(2)}) async-start(), calls=%async_computation.4 | async-start | bytes 2621440 | tf_op jit(solution)/shard_map/all_gather | solution.py:165
  7.6 0.7 copy-start.3
  11.6 43.6 %copy-start.4 = (s32[32]{0:T(128)S(1)}, s32[32]{0:T(128)}, u32[]{:S(2)}) copy-start(s32[32]{0:T(128)} %select_reduce_fusion.head_ref) | copy-start | bytes 388
  11.6 43.7 %copy-start.2 = (s32[32,32]{1,0:T(8,128)S(1)}, s32[32,32]{1,0:T(8,128)}, u32[]{:S(2)}) copy-start(s32[32,32]{1,0:T(8,128)} %param.9) | copy-start | bytes 12292
  33.7 45.9 %all-gather.5.cloned.1.call-start = ((), (), s32[]{:S(2)}) async-start(), calls=%async_computation.5 | async-start | bytes 2621440 | tf_op jit(solution)/shard_map/all_gather | solution.py:167
  51.6 17.7 %all-to-all-start = ((bf16[8,256,128]{2,1,0:T(8,128)(2,1)}), bf16[8,256,128]{2,1,0:T(8,128)(2,1)S(1)}, u32[]{:S(2)}, u32[]{:S(2)}) async-start(bf16[8,256,128]{2,1,0:T(8,128)(2,1)} %bitcast), calls=%async_computation | async-start | bytes 1048576 | tf_op jit(solution)/shard_map/all_to_all | solution.py:168
  69.3 10.3 %copy-start.1 = (bf16[8,256,128]{2,1,0:T(8,128)(2,1)}, bf16[8,256,128]{2,1,0:T(8,128)(2,1)S(1)}, u32[]{:S(2)}) copy-start(bf16[8,256,128]{2,1,0:T(8,128)(2,1)S(1)} %all-to-all-done.qt_ref) | copy-start | bytes 1572868
Sparse Core Ops, SparseCore 0:
  33.8 21.5 all-gather.2
  57.0 22.5 all-gather.4

commit v2 on v0

v2 whole, which is shorter than its diff:
```python
import functools

import jax
import jax.numpy as jnp
from jax import lax
from jax.experimental import pallas as pl
from jax.experimental.pallas import tpu as pltpu
from jax.sharding import PartitionSpec as P

H = 32
DH = 64
BLK = 128
KMAX = 32
UNROLL = 4
BIG = 1e30
F32 = jnp.float32
BF16 = jnp.bfloat16
VMEM = pl.BlockSpec(memory_space=pltpu.VMEM)
SMEM = pl.BlockSpec(memory_space=pltpu.SMEM)
ANY = pl.BlockSpec(memory_space=pl.ANY)
PARAMS = pltpu.CompilerParams(vmem_limit_bytes=58 << 20)


def pack_kernel(head_ref, q_ref, k_ref, v_ref, *refs):
    pairs = (len(refs) - 1) // 2
    kv_refs, qt_refs, turned = refs[:pairs], refs[pairs : 2 * pairs], refs[-1]
    groups = qt_refs[0].shape[0]
    low = lax.broadcasted_iota(jnp.int32, (BLK, 2 * DH), 1) < DH
    for pair in range(H // 2):
        lanes = slice(pair * 2 * DH, (pair + 1) * 2 * DH)
        for which, source in enumerate((q_ref, v_ref)):
            tile = source[:, lanes].T
            turned[which, 2 * pair] = tile[:DH]
            turned[which, 2 * pair + 1] = tile[DH:]

    def fetch(head, odd):
        start = pl.multiple_of((head // 2) * (2 * DH), 2 * DH)
        block = k_ref[:, pl.ds(start, 2 * DH)]
        swapped = jnp.concatenate([block[:, DH:], block[:, :DH]], axis=1)
        return jnp.where((head % 2) == odd, block, swapped)

    for pair in range(pairs):
        for group in range(groups):
            place = (pair * groups + group) * 2
            left, right = head_ref[place], head_ref[place + 1]
            kv_refs[pair][group, 0] = jnp.where(low, fetch(left, 0), fetch(right, 1))
            kv_refs[pair][group, 1] = jnp.concatenate([turned[1, left], turned[1, right]], axis=0)
            qt_refs[pair][group] = jnp.concatenate([turned[0, left], turned[0, right]], axis=0)


def plan_kernel(groups, me_ref, lay_ref, cnt_ref, unit_ref, total_ref):
    pairs = total_ref.shape[0]
    rows = cnt_ref.shape[0] // pairs
    own = me_ref[0]

    def local(block):
        return ((block // groups) ^ own) * groups + block % groups

    for pair in range(pairs):

        def idle(base, many):
            for extra in range(many):
                unit_ref[pair, 0, base + extra] = rows
                unit_ref[pair, 1, base + extra] = 0
                unit_ref[pair, 2, base + extra] = 0
                unit_ref[pair, 3, base + extra] = 1

        def place_row(row, base):
            count = cnt_ref[pair * rows + row]
            start = (pair * rows + row) * KMAX

            def place_unit(step, _):
                first = lay_ref[start + 2 * step]
                whole = 2 * step + 1 < count
                second = jnp.where(whole, lay_ref[start + 2 * step + 1], first)
                unit_ref[pair, 0, base + step] = row
                unit_ref[pair, 1, base + step] = local(first)
                unit_ref[pair, 2, base + step] = local(second)
                unit_ref[pair, 3, base + step] = whole.astype(jnp.int32)
                return 0

            units = (count + 1) // 2
            lax.fori_loop(0, units, place_unit, 0)
            return base + units

        idle(0, 2 * UNROLL)
        total = lax.fori_loop(0, rows, place_row, jnp.int32(2 * UNROLL))
        idle(total, 4 * UNROLL)
        total_ref[pair] = total


def attend_kernel(pair, slabs, unit_ref, total_ref, qt_ref, *refs):
    kv_hbm, o_ref = refs[:slabs], refs[slabs]
    kv_ref, qz_ref, m_ref, l_ref, acc_ref, sem = refs[slabs + 1 : slabs + 7]
    score, top_of, out_of, sum_of = (refs[slabs + 7 + 2 * at : slabs + 9 + 2 * at] for at in range(4))
    slab = qt_ref.shape[0]
    rows = 2 * slab
    copies = [
        pltpu.make_async_copy(source, kv_ref.at[pl.ds(at * slab, slab)], sem.at[at])
        for at, source in enumerate(kv_hbm)
    ]
    for copy in copies:
        copy.start()
    zeros = jnp.zeros((DH, BLK), BF16)
    for head in range(2):
        for block in range(slab):
            part = qt_ref[block, head * DH : (head + 1) * DH, :]
            up = jnp.concatenate([part, zeros], axis=0)
            down = jnp.concatenate([zeros, part], axis=0)
            qz_ref[head * slab + block] = jnp.concatenate([up, down], axis=1)
    qz_ref[rows] = jnp.zeros((2 * DH, 2 * BLK), BF16)
    m_ref[...] = jnp.full(m_ref.shape, -BIG, F32)
    for ref in (l_ref, acc_ref, *score, *top_of, *out_of, *sum_of):
        ref[...] = jnp.zeros(ref.shape, F32)
    for copy in copies:
        copy.wait()
    low = lax.broadcasted_iota(jnp.int32, (BLK, 2 * DH), 1) < DH

    def read(unit):
        row = unit_ref[pair, 0, unit]
        odd = jnp.where((row >= slab) & (row < rows), 1, 0)
        return row, odd, unit_ref[pair, 1, unit], unit_ref[pair, 2, unit]

    def make_scores(unit, lane, side):
        row, odd, first, second = read(unit)
        plain = kv_ref[jnp.where(odd == 1, second, first), 0]
        other = kv_ref[jnp.where(odd == 1, first, second), 0]
        other = jnp.concatenate([other[:, DH:], other[:, :DH]], axis=1)
        keys = jnp.where(low == (odd == 0), plain, other)
        scores = jnp.dot(keys, qz_ref[row], preferred_element_type=F32)
        score[side][lane] = scores
        top = jnp.max(scores.reshape(BLK // 8, 8, 2 * BLK), axis=0)
        top = jnp.maximum(top[:, :BLK], top[:, BLK:])
        top_of[side][lane] = jnp.broadcast_to(jnp.max(top, axis=0, keepdims=True), (8, BLK))

    def make_output(unit, lane, side):
        _, odd, first, second = read(unit)
        top = top_of[side][lane]
        limit = jnp.where(unit_ref[pair, 3, unit] == 1, top, top + BIG)
        scores = score[side][lane]
        left = jnp.exp(scores[:, :BLK].reshape(BLK // 8, 8, BLK) - top[None])
        right = jnp.exp(scores[:, BLK:].reshape(BLK // 8, 8, BLK) - limit[None])
        sum_of[side][lane] = jnp.sum(left, axis=0) + jnp.sum(right, axis=0)
        weights = jnp.concatenate([left.reshape(BLK, BLK), right.reshape(BLK, BLK)], axis=0)
        span = pl.ds(pl.multiple_of(odd * DH, DH), DH)
        values = jnp.concatenate([kv_ref[first, 1, span, :], kv_ref[second, 1, span, :]], axis=1)
        out_of[side][lane] = jnp.dot(values, weights.astype(BF16), preferred_element_type=F32)

    def merge(unit, lane, side):
        row = unit_ref[pair, 0, unit]
        top, old = top_of[side][lane], m_ref[row]
        new = jnp.maximum(old, top)
        a, b = jnp.exp(old - new), jnp.exp(top - new)
        m_ref[row] = new
        l_ref[row] = l_ref[row] * a + sum_of[side][lane] * b
        tiles = (DH // 8, 8, BLK)
        acc_ref[row] = (acc_ref[row].reshape(tiles) * a[None] + out_of[side][lane].reshape(tiles) * b[None]).reshape(
            DH, BLK
        )

    def step(index, _):
        for side in range(2):
            chunk = 2 * index + side
            for lane in range(UNROLL):
                merge(chunk * UNROLL + lane, lane, side)
            for lane in range(UNROLL):
                make_scores((chunk + 2) * UNROLL + lane, lane, side)
                make_output((chunk + 1) * UNROLL + lane, lane, 1 - side)
        return 0

    chunks = (total_ref[pair] + UNROLL - 1) // UNROLL
    lax.fori_loop(0, (chunks + 1) // 2, step, 0)
    for head in range(2):
        for block in range(slab):
            row = head * slab + block
            total_w = jnp.sum(l_ref[row], axis=0, keepdims=True)
            o_ref[block, head * DH : (head + 1) * DH, :] = (acc_ref[row] / total_w).astype(BF16)


def unpack_kernel(place_ref, *refs):
    ins, out_ref, held = refs[:-2], refs[-2], refs[-1]
    groups = ins[0].shape[0]
    for pair, source in enumerate(ins):
        for group in range(groups):
            place = (pair * groups + group) * 2
            held[place] = source[group, :DH]
            held[place + 1] = source[group, DH:]
    for pair in range(H // 2):
        both = jnp.concatenate([held[place_ref[2 * pair]], held[place_ref[2 * pair + 1]]], axis=0)
        out_ref[:, pair * 2 * DH : (pair + 1) * 2 * DH] = both.T


def places_of(counts, groups):
    load = jnp.sum(counts, axis=1)
    ids = jnp.arange(H, dtype=jnp.int32)
    ahead = (load[None, :] > load[:, None]) | ((load[None, :] == load[:, None]) & (ids[None, :] < ids[:, None]))
    rank = jnp.sum(ahead.astype(jnp.int32), axis=1)
    turn, seat = rank // groups, rank % groups
    group = jnp.where(turn % 2 == 0, seat, groups - 1 - seat)
    place = ((turn // 2) * groups + group) * 2 + turn % 2
    head_at = jnp.sum(jnp.where(place[None, :] == ids[:, None], ids[None, :], 0), axis=1)
    return head_at, place


def shards(queries, key_vectors, value_vectors, layout, counts):
    groups, slabs = lax.axis_size("uly"), lax.axis_size("doc")
    per = H // groups
    pairs = per // 2
    slab = groups
    rows = 2 * slab
    shape = jax.ShapeDtypeStruct
    head_at, place = places_of(counts, groups)
    packed = pl.pallas_call(
        pack_kernel,
        out_shape=(shape((groups, 2, BLK, BLK), BF16),) * pairs + (shape((groups, BLK, BLK), BF16),) * pairs,
        in_specs=[SMEM, VMEM, VMEM, VMEM],
        out_specs=(VMEM,) * (2 * pairs),
        scratch_shapes=[pltpu.VMEM((2, H, DH, BLK), BF16)],
        compiler_params=PARAMS,
        name="pack",
    )(head_at, queries, key_vectors, value_vectors)
    swap = functools.partial(lax.all_to_all, axis_name="uly", split_axis=0, concat_axis=0, tiled=True)

    def flip(array, bit):
        return lax.ppermute(array, "doc", [(at, at ^ bit) for at in range(slabs)])

    own = lax.axis_index("doc")
    mine = head_at.reshape(pairs, groups, 2)
    mine = lax.dynamic_index_in_dim(mine, lax.axis_index("uly"), 1, keepdims=False).reshape(-1)
    lay = jnp.take(lax.dynamic_slice_in_dim(layout, own * slab, slab, axis=1), mine, axis=0).reshape(-1)
    cnt = jnp.take(lax.dynamic_slice_in_dim(counts, own * slab, slab, axis=1), mine, axis=0).reshape(-1)
    units, totals = pl.pallas_call(
        functools.partial(plan_kernel, groups),
        out_shape=(
            shape((pairs, 4, rows * KMAX // 2 + 8 * UNROLL), jnp.int32),
            shape((pairs,), jnp.int32),
        ),
        in_specs=[SMEM, SMEM, SMEM],
        out_specs=(SMEM, SMEM),
        compiler_params=PARAMS,
        name="plan",
    )(own.reshape(1), lay, cnt)

    returned = []
    for pair in range(pairs):
        kv = swap(packed[pair])
        qt = swap(packed[pairs + pair])
        gathered = {0: kv}
        bit = slabs // 2
        while bit:
            gathered.update({at ^ bit: flip(array, bit) for at, array in list(gathered.items())})
            bit //= 2
        both = [pltpu.VMEM((UNROLL, BLK, 2 * BLK), F32)] * 2 + [pltpu.VMEM((UNROLL, 8, BLK), F32)] * 2
        both += [pltpu.VMEM((UNROLL, DH, BLK), F32)] * 2 + [pltpu.VMEM((UNROLL, 8, BLK), F32)] * 2
        out = pl.pallas_call(
            functools.partial(attend_kernel, pair, slabs),
            out_shape=shape((slab, BLK, BLK), BF16),
            in_specs=[SMEM, SMEM, VMEM] + [ANY] * slabs,
            out_specs=VMEM,
            scratch_shapes=[
                pltpu.VMEM((slabs * slab, 2, BLK, BLK), BF16),
                pltpu.VMEM((rows + 1, 2 * DH, 2 * BLK), BF16),
                pltpu.VMEM((rows + 1, 8, BLK), F32),
                pltpu.VMEM((rows + 1, 8, BLK), F32),
                pltpu.VMEM((rows + 1, DH, BLK), F32),
                pltpu.SemaphoreType.DMA((slabs,)),
                *both,
            ],
            compiler_params=PARAMS,
            name="attend",
        )(units, totals, qt, *[gathered[at] for at in range(slabs)])
        returned.append(swap(out))
    return pl.pallas_call(
        unpack_kernel,
        out_shape=shape(queries.shape, BF16),
        in_specs=[SMEM] + [VMEM] * pairs,
        out_specs=VMEM,
        scratch_shapes=[pltpu.VMEM((H, DH, BLK), BF16)],
        compiler_params=PARAMS,
        name="unpack",
    )(place, *returned)


def solution(mesh):
    placed = (
        P(("grp", "doc", "uly"), None),
        P(("grp", "doc", "uly"), None),
        P(("grp", "doc", "uly"), None),
        P("grp", None, None),
        P("grp", None),
    )
    return jax.shard_map(
        shards,
        mesh=mesh,
        in_specs=placed,
        out_specs=P(("grp", "doc", "uly"), None),
        check_vma=False,
    )
```

time: 331 us -> 113 us (0.34)
  local copies, waits for them, and re-layouts: 93.5 us -> 6.55 us
  matrix products: 69.1 us -> 0 us
  other arithmetic: 66 us -> 1.92 us
  blocking collectives: 69.2 us -> 36.2 us
  Pallas kernels: 0 us -> 30.3 us
  between operations: 23.4 us -> 0.19 us
  starting transfers between devices: 3.68 us -> 20.3 us
  waiting for transfers between devices: 1.5 us -> 17 us
    dot_general x40 -> x0, matrix products: 69.1 us -> none  [the longest x20 48.7 us: advance(): jnp.einsum('hyc,hcr->hyr', weights.astype(jnp.bfloat16), value_block_list...]
    gather x40 -> x2, local copies, waits for them, and re-layouts: 66.7 us -> 1.11 us  [the longest x1 0.56 us: shards(): jnp.take(lax.dynamic_slice_in_dim(counts, own * slab, slab, axis=1), mine...]
    all_to_all x3 -> x2, blocking collectives: 69.2 us -> 36.2 us  [the longest x1 21.8 us: shards(): kv = swap(packed[pair])]
    pallas_call x0 -> x5, Pallas kernels: none -> 30.3 us  [the longest x2 19.3 us: shards(): pl.pallas_call(functools.partial(attend_kernel, pair, slabs), out_shape=s...]
    and x20 -> x1, other arithmetic: 25.2 us -> 0.01 us  [shards(): jnp.take(lax.dynamic_slice_in_dim(layout, own * slab, slab, axis=1), mine...]
    select_n x20 -> x3, other arithmetic: 18.4 us -> 0.15 us  [the longest x2 0.08 us: shards(): jnp.take(lax.dynamic_slice_in_dim(layout, own * slab, slab, axis=1), mine...]
    all_to_all x1 -> x4, waiting for transfers between devices: 0.01 us -> 16.7 us  [the longest x1 11.2 us: shards(): kv = swap(packed[pair])]
    reduce_sum x20 -> x3, other arithmetic: 15 us -> 1.73 us  [the longest x1 0.89 us: places_of(): load = jnp.sum(counts, axis=1)]
  transfers between devices with their start and end apart: 3 -> 10, of which waited for: 1 -> 3; matrix products, arithmetic and copies ran while one was open for 4% -> 4% of each run, Pallas kernels for 0% -> 22%
where the time goes in v2:
time: 113 us; the launch traced here: 112 us
  blocking collectives  36.2 us (32%)
  Pallas kernels  30.3 us (27%)
  starting transfers between devices  20.3 us (18%)
  waiting for transfers between devices  17 us (15%)
  local copies, waits for them, and re-layouts  6.55 us (6%)
  other arithmetic  1.92 us (2%)
    all_to_all x1, blocking collectives, shards(): kv = swap(packed[pair])  21.8 us
    pallas_call x2, Pallas kernels, shards(): pl.pallas_call(functools.partial(attend_kernel, pair, slabs), out_shape=s...  19.3 us
    all_to_all x1, blocking collectives, shards(): returned.append(swap(out))  14.3 us
    all_to_all x1, waiting for transfers between devices, shards(): kv = swap(packed[pair])  11.2 us
    all_to_all x2, starting transfers between devices, shards(): qt = swap(packed[pairs + pair])  7.22 us
    all_to_all x1, starting transfers between devices, shards(): returned.append(swap(out))  5.75 us
    pallas_call x1, Pallas kernels, shards(): pl.pallas_call(functools.partial(plan_kernel, groups), out_shape=(shape((...  5.6 us
    all_to_all x2, waiting for transfers between devices, shards(): qt = swap(packed[pairs + pair])  5.48 us
  transfers between devices with their start and end apart: 10, of which 3 were waited for; matrix products, arithmetic and copies ran while one was open for 4% of the time, Pallas kernels for 22%

profile of v2, /device:TPU:0, one launch (start us, length us, event | category | flops | bytes accessed | tf_op | source)
XLA Modules:
  0.0 112.4 jit_solution(7240275879673368643)
XLA Ops:
  0.0 0.9 reduce_sum.27
  0.9 0.2 convert_reduce_fusion
  1.1 0.7 select_reduce_fusion.head_ref
  1.8 3.3 %pack.1 = (bf16[8,2,128,128]{3,2,1,0:T(8,128)(2,1)}, bf16[8,2,128,128]{3,2,1,0:T(8,128)(2,1)}, bf16[8,128,128]{2,1,0:T(8,128)(2,1)}, bf16[8,128,128]{2,1,0:T(8,128)(2,1)}) custom-call(s32[32]{0:T(128)} %select_reduce_fusion.head_ref, bf16[128,2048]{1,0:T(8,128)(2,1)} %q_ref.1, bf16[128,2048]{1,0:T(8,128)(2,1)} %k_ref.1, bf16[128,2048]{1,0:T(8,128)(2,1)} %v_ref.1), custom_call_target="tpu_custom_call" | custom-call | tf_op jit(solution)/shard_map/pack/pallas_call | solution.py:213
  5.1 21.8 %all_to_all.30.refs_0_ = bf16[8,2,128,128]{3,2,1,0:T(8,128)(2,1)S(1)} all-to-all(bf16[8,2,128,128]{3,2,1,0:T(8,128)(2,1)} %get-tuple-element.16), channel_id=1, replica_groups=mesh['grp'=1,'uly'=8,'doc'=4] {'uly'}, dimensions={0} | all-to-all | bytes 1048576 | tf_op jit(solution)/shard_map/all_to_all | solution.py:246
  26.9 3.6 %all-to-all-start.1 = ((bf16[8,2,128,128]{3,2,1,0:T(8,128)(2,1)}), bf16[8,2,128,128]{3,2,1,0:T(8,128)(2,1)S(1)}, u32[]{:S(2)}, u32[]{:S(2)}) async-start(bf16[8,2,128,128]{3,2,1,0:T(8,128)(2,1)} %get-tuple-element.14), calls=%async_computation.1 | async-start | bytes 1048576 | tf_op jit(solution)/shard_map/all_to_all | solution.py:246
  30.5 0.6 copy-done.9
  31.2 0.6 copy-done.8
  31.9 1.6 %collective-permute-start.4 = (bf16[8,2,128,128]{3,2,1,0:T(8,128)(2,1)S(1)}, bf16[8,2,128,128]{3,2,1,0:T(8,128)(2,1)S(1)}, u32[]{:S(2)}, u32[]{:S(2)}) collective-permute-start(bf16[8,2,128,128]{3,2,1,0:T(8,128)(2,1)S(1)} %all_to_all.30.refs_0_), channel_id=1, source_target_pairs={{0,2},{1,3},{2,0},{3,1},{4,6},{5,7},{6,4},{7,5},{8,10},{9,11},{10,... | collective-permute-start | bytes 1572872 | tf_op jit(solution)/shard_map/ppermute | solution.py:225
  33.5 11.2 %all-to-all-done.1.refs_0_ = bf16[8,2,128,128]{3,2,1,0:T(8,128)(2,1)S(1)} async-done(((bf16[8,2,128,128]{3,2,1,0:T(8,128)(2,1)}), bf16[8,2,128,128]{3,2,1,0:T(8,128)(2,1)S(1)}, u32[]{:S(2)}, u32[]{:S(2)}) %all-to-all-start.1) | async-done | bytes 524320 | tf_op jit(solution)/shard_map/all_to_all | solution.py:246
  44.7 3.6 %all-to-all-start.3 = ((bf16[8,128,128]{2,1,0:T(8,128)(2,1)}), bf16[8,128,128]{2,1,0:T(8,128)(2,1)S(1)}, u32[]{:S(2)}, u32[]{:S(2)}) async-start(bf16[8,128,128]{2,1,0:T(8,128)(2,1)} %get-tuple-element.15), calls=%async_computation.3 | async-start | bytes 524288 | tf_op jit(solution)/shard_map/all_to_all | solution.py:247
  48.3 0.5 broadcast.191
  48.8 0.6 fusion.4
  49.5 0.1 reshape.121
  49.7 1.5 %collective-permute-start.1 = (bf16[8,2,128,128]{3,2,1,0:T(8,128)(2,1)S(1)}, bf16[8,2,128,128]{3,2,1,0:T(8,128)(2,1)S(1)}, u32[]{:S(2)}, u32[]{:S(2)}) collective-permute-start(bf16[8,2,128,128]{3,2,1,0:T(8,128)(2,1)S(1)} %all-to-all-done.1.refs_0_), channel_id=1, source_target_pairs={{0,2},{1,3},{2,0},{3,1},{4,6},{5,7},{6,4},{7,5},{8,10},{9,11},{10,... | collective-permute-start | bytes 1572872 | tf_op jit(solution)/shard_map/ppermute | solution.py:225
  51.2 0.5 collective-permute-start.5
  51.7 5.5 %all-to-all-done.3.qt_ref = bf16[8,128,128]{2,1,0:T(8,128)(2,1)S(1)} async-done(((bf16[8,128,128]{2,1,0:T(8,128)(2,1)}), bf16[8,128,128]{2,1,0:T(8,128)(2,1)S(1)}, u32[]{:S(2)}, u32[]{:S(2)}) %all-to-all-start.3) | async-done | bytes 262176 | tf_op jit(solution)/shard_map/all_to_all | solution.py:247
  57.2 0.7 copy-done.3
  57.9 3.6 %all-to-all-start = ((bf16[8,128,128]{2,1,0:T(8,128)(2,1)}), bf16[8,128,128]{2,1,0:T(8,128)(2,1)S(1)}, u32[]{:S(2)}, u32[]{:S(2)}) async-start(bf16[8,128,128]{2,1,0:T(8,128)(2,1)} %get-tuple-element.13), calls=%async_computation | async-start | bytes 524288 | tf_op jit(solution)/shard_map/all_to_all | solution.py:247
  61.5 0.6 gather_fusion.1
  62.0 0.5 gather_fusion
  62.7 0.3 collective-permute-done.1.refs_2_
  63.0 0.2 collective-permute-start.2
  63.3 0.6 select_n.103.cnt_ref
  63.9 0.7 select_n.101.lay_ref
  64.5 5.6 %plan.1 = (s32[2,4,288]{2,1,0:T(4,128)}, s32[2]{0:T(128)}) custom-call(s32[1]{0:T(128)} %bitcast.me_ref, s32[1024]{0:T(1024)} %select_n.101.lay_ref, s32[32]{0:T(128)} %select_n.103.cnt_ref), custom_call_target="tpu_custom_call" | custom-call | tf_op jit(solution)/shard_map/plan/pallas_call | solution.py:232
  70.2 6.6 %attend.3 = bf16[8,128,128]{2,1,0:T(8,128)(2,1)} custom-call(s32[2,4,288]{2,1,0:T(4,128)} %get-tuple-element.11.unit_ref, s32[2]{0:T(128)} %get-tuple-element.12.total_ref, bf16[8,128,128]{2,1,0:T(8,128)(2,1)} %copy-done.3, bf16[8,2,128,128]{3,2,1,0:T(8,128)(2,1)} %copy-done.2, bf16[8,2,128,128]{3,2,1,0:T(8,128)(2,1)} %collective-permute-done.3.refs_1_, ...), custom_call_target="tpu_custom_call" | custom-call | tf_op jit(solution)/shard_map/attend/pallas_call | solution.py:255
  76.8 0.7 copy-done.4
  77.5 5.8 %all-to-all-start.5 = ((bf16[8,128,128]{2,1,0:T(8,128)(2,1)}), bf16[8,128,128]{2,1,0:T(8,128)(2,1)S(1)}, u32[]{:S(2)}, u32[]{:S(2)}) async-start(bf16[8,128,128]{2,1,0:T(8,128)(2,1)} %attend.3), calls=%async_computation.5 | async-start | bytes 524288 | tf_op jit(solution)/shard_map/all_to_all | solution.py:272
  83.2 12.8 %attend.2 = bf16[8,128,128]{2,1,0:T(8,128)(2,1)} custom-call(s32[2,4,288]{2,1,0:T(4,128)} %get-tuple-element.11.unit_ref, s32[2]{0:T(128)} %get-tuple-element.12.total_ref, bf16[8,128,128]{2,1,0:T(8,128)(2,1)} %copy-done.4, bf16[8,2,128,128]{3,2,1,0:T(8,128)(2,1)} %copy-done.1, bf16[8,2,128,128]{3,2,1,0:T(8,128)(2,1)} %collective-permute-done.refs_1_, ...), custom_call_target="tpu_custom_call" | custom-call | tf_op jit(solution)/shard_map/attend/pallas_call | solution.py:255
  96.0 14.3 %all_to_all.31.refs_0_ = bf16[8,128,128]{2,1,0:T(8,128)(2,1)} all-to-all(bf16[8,128,128]{2,1,0:T(8,128)(2,1)} %attend.2), channel_id=1, replica_groups=mesh['grp'=1,'uly'=8,'doc'=4] {'uly'}, dimensions={0} | all-to-all | bytes 524288 | tf_op jit(solution)/shard_map/all_to_all | solution.py:272
  110.4 2.1 %unpack.1 = bf16[128,2048]{1,0:T(8,128)(2,1)} custom-call(s32[32]{0:T(128)} %copy-done.10, bf16[8,128,128]{2,1,0:T(8,128)(2,1)} %all_to_all.31.refs_0_, bf16[8,128,128]{2,1,0:T(8,128)(2,1)} %copy-done.5), custom_call_target="tpu_custom_call" | custom-call | tf_op jit(solution)/shard_map/unpack/pallas_call | solution.py:273
  (37 shorter events, 0.5 us)
Async XLA Ops:
  0.0 31.9 %copy-start = (s32[32,32,32]{2,1,0:T(8,128)S(1)}, s32[32,32,32]{2,1,0:T(8,128)}, u32[]{:S(2)}) copy-start(s32[32,32,32]{2,1,0:T(8,128)} %param.8) | copy-start | bytes 393220
  1.1 0.7 copy-start.10
  26.9 24.3 %copy-start.2 = (bf16[8,2,128,128]{3,2,1,0:T(8,128)(2,1)}, bf16[8,2,128,128]{3,2,1,0:T(8,128)(2,1)S(1)}, u32[]{:S(2)}) copy-start(bf16[8,2,128,128]{3,2,1,0:T(8,128)(2,1)S(1)} %all_to_all.30.refs_0_) | copy-start | bytes 1572868
  26.9 17.8 %all-to-all-start.1 = ((bf16[8,2,128,128]{3,2,1,0:T(8,128)(2,1)}), bf16[8,2,128,128]{3,2,1,0:T(8,128)(2,1)S(1)}, u32[]{:S(2)}, u32[]{:S(2)}) async-start(bf16[8,2,128,128]{3,2,1,0:T(8,128)(2,1)} %get-tuple-element.14), calls=%async_computation.1 | async-start | bytes 1048576 | tf_op jit(solution)/shard_map/all_to_all | solution.py:246
  30.5 0.6 copy-start.9
  31.1 0.7 copy-start.8
  31.9 19.2 %collective-permute-start.4 = (bf16[8,2,128,128]{3,2,1,0:T(8,128)(2,1)S(1)}, bf16[8,2,128,128]{3,2,1,0:T(8,128)(2,1)S(1)}, u32[]{:S(2)}, u32[]{:S(2)}) collective-permute-start(bf16[8,2,128,128]{3,2,1,0:T(8,128)(2,1)S(1)} %all_to_all.30.refs_0_), channel_id=1, source_target_pairs={{0,2},{1,3},{2,0},{3,1},{4,6},{5,7},{6,4},{7,5},{8,10},{9,11},{10,... | collective-permute-start | bytes 1572872 | tf_op jit(solution)/shard_map/ppermute | solution.py:225
  44.7 18.0 %copy-start.1 = (bf16[8,2,128,128]{3,2,1,0:T(8,128)(2,1)}, bf16[8,2,128,128]{3,2,1,0:T(8,128)(2,1)S(1)}, u32[]{:S(2)}) copy-start(bf16[8,2,128,128]{3,2,1,0:T(8,128)(2,1)S(1)} %all-to-all-done.1.refs_0_) | copy-start | bytes 1572868
  44.7 12.5 %all-to-all-start.3 = ((bf16[8,128,128]{2,1,0:T(8,128)(2,1)}), bf16[8,128,128]{2,1,0:T(8,128)(2,1)S(1)}, u32[]{:S(2)}, u32[]{:S(2)}) async-start(bf16[8,128,128]{2,1,0:T(8,128)(2,1)} %get-tuple-element.15), calls=%async_computation.3 | async-start | bytes 524288 | tf_op jit(solution)/shard_map/all_to_all | solution.py:247
  49.7 13.4 %collective-permute-start.1 = (bf16[8,2,128,128]{3,2,1,0:T(8,128)(2,1)S(1)}, bf16[8,2,128,128]{3,2,1,0:T(8,128)(2,1)S(1)}, u32[]{:S(2)}, u32[]{:S(2)}) collective-permute-start(bf16[8,2,128,128]{3,2,1,0:T(8,128)(2,1)S(1)} %all-to-all-done.1.refs_0_), channel_id=1, source_target_pairs={{0,2},{1,3},{2,0},{3,1},{4,6},{5,7},{6,4},{7,5},{8,10},{9,11},{10,... | collective-permute-start | bytes 1572872 | tf_op jit(solution)/shard_map/ppermute | solution.py:225
  51.2 19.0 %collective-permute-start.3 = (bf16[8,2,128,128]{3,2,1,0:T(8,128)(2,1)S(1)}, bf16[8,2,128,128]{3,2,1,0:T(8,128)(2,1)}, u32[]{:S(2)}, u32[]{:S(2)}) collective-permute-start(bf16[8,2,128,128]{3,2,1,0:T(8,128)(2,1)S(1)} %all_to_all.30.refs_0_), channel_id=1, source_target_pairs={{0,1},{1,0},{2,3},{3,2},{4,5},{5,4},{6,7},{7,6},{8,9},{9,8},{10,11... | collective-permute-start | bytes 1572872 | tf_op jit(solution)/shard_map/ppermute | solution.py:225
  51.2 19.0 %copy-start.6 = (bf16[8,2,128,128]{3,2,1,0:T(8,128)(2,1)}, bf16[8,2,128,128]{3,2,1,0:T(8,128)(2,1)S(1)}, u32[]{:S(2)}) copy-start(bf16[8,2,128,128]{3,2,1,0:T(8,128)(2,1)S(1)} %collective-permute-done.4.refs_2_) | copy-start | bytes 1572868
  51.2 18.9 %collective-permute-start.5 = (bf16[8,2,128,128]{3,2,1,0:T(8,128)(2,1)S(1)}, bf16[8,2,128,128]{3,2,1,0:T(8,128)(2,1)}, u32[]{:S(2)}, u32[]{:S(2)}) collective-permute-start(bf16[8,2,128,128]{3,2,1,0:T(8,128)(2,1)S(1)} %collective-permute-done.4.refs_2_), channel_id=1, source_target_pairs={{0,1},{1,0},{2,3},{3,2},{4,5},{5,4},{6,7},{7,6},{8,9},{9,8},{10,11... | collective-permute-start | bytes 1572872 | tf_op jit(solution)/shard_map/ppermute | solution.py:225
  57.2 0.7 copy-start.3
  57.9 18.9 %all-to-all-start = ((bf16[8,128,128]{2,1,0:T(8,128)(2,1)}), bf16[8,128,128]{2,1,0:T(8,128)(2,1)S(1)}, u32[]{:S(2)}, u32[]{:S(2)}) async-start(bf16[8,128,128]{2,1,0:T(8,128)(2,1)} %get-tuple-element.13), calls=%async_computation | async-start | bytes 524288 | tf_op jit(solution)/shard_map/all_to_all | solution.py:247
  62.6 20.6 %collective-permute-start = (bf16[8,2,128,128]{3,2,1,0:T(8,128)(2,1)S(1)}, bf16[8,2,128,128]{3,2,1,0:T(8,128)(2,1)}, u32[]{:S(2)}, u32[]{:S(2)}) collective-permute-start(bf16[8,2,128,128]{3,2,1,0:T(8,128)(2,1)S(1)} %all-to-all-done.1.refs_0_), channel_id=1, source_target_pairs={{0,1},{1,0},{2,3},{3,2},{4,5},{5,4},{6,7},{7,6},{8,9},{9,8},{10,11... | collective-permute-start | bytes 1572872 | tf_op jit(solution)/shard_map/ppermute | solution.py:225
  63.0 13.8 %copy-start.7 = (bf16[8,2,128,128]{3,2,1,0:T(8,128)(2,1)}, bf16[8,2,128,128]{3,2,1,0:T(8,128)(2,1)S(1)}, u32[]{:S(2)}) copy-start(bf16[8,2,128,128]{3,2,1,0:T(8,128)(2,1)S(1)} %collective-permute-done.1.refs_2_) | copy-start | bytes 1572868
  63.0 20.2 %collective-permute-start.2 = (bf16[8,2,128,128]{3,2,1,0:T(8,128)(2,1)S(1)}, bf16[8,2,128,128]{3,2,1,0:T(8,128)(2,1)}, u32[]{:S(2)}, u32[]{:S(2)}) collective-permute-start(bf16[8,2,128,128]{3,2,1,0:T(8,128)(2,1)S(1)} %collective-permute-done.1.refs_2_), channel_id=1, source_target_pairs={{0,1},{1,0},{2,3},{3,2},{4,5},{5,4},{6,7},{7,6},{8,9},{9,8},{10,11... | collective-permute-start | bytes 1572872 | tf_op jit(solution)/shard_map/ppermute | solution.py:225
  76.8 0.7 copy-start.4
  77.5 18.5 %all-to-all-start.5 = ((bf16[8,128,128]{2,1,0:T(8,128)(2,1)}), bf16[8,128,128]{2,1,0:T(8,128)(2,1)S(1)}, u32[]{:S(2)}, u32[]{:S(2)}) async-start(bf16[8,128,128]{2,1,0:T(8,128)(2,1)} %attend.3), calls=%async_computation.5 | async-start | bytes 524288 | tf_op jit(solution)/shard_map/all_to_all | solution.py:272
  96.0 14.4 %copy-start.5 = (bf16[8,128,128]{2,1,0:T(8,128)(2,1)}, bf16[8,128,128]{2,1,0:T(8,128)(2,1)S(1)}, u32[]{:S(2)}) copy-start(bf16[8,128,128]{2,1,0:T(8,128)(2,1)S(1)} %all-to-all-done.5.refs_1_) | copy-start | bytes 786436

commit v3 on v2

--- a/solution.py
+++ b/solution.py
@@ -21,40 +21,30 @@
 PARAMS = pltpu.CompilerParams(vmem_limit_bytes=58 << 20)
 
 
-def pack_kernel(head_ref, q_ref, k_ref, v_ref, *refs):
-    pairs = (len(refs) - 1) // 2
-    kv_refs, qt_refs, turned = refs[:pairs], refs[pairs : 2 * pairs], refs[-1]
-    groups = qt_refs[0].shape[0]
+def pack_kernel(groups, me_ref, head_ref, q_ref, k_ref, v_ref, *out_refs):
     low = lax.broadcasted_iota(jnp.int32, (BLK, 2 * DH), 1) < DH
-    for pair in range(H // 2):
-        lanes = slice(pair * 2 * DH, (pair + 1) * 2 * DH)
-        for which, source in enumerate((q_ref, v_ref)):
-            tile = source[:, lanes].T
-            turned[which, 2 * pair] = tile[:DH]
-            turned[which, 2 * pair + 1] = tile[DH:]
-
-    def fetch(head, odd):
+
+    def fetch(source, head, odd):
         start = pl.multiple_of((head // 2) * (2 * DH), 2 * DH)
-        block = k_ref[:, pl.ds(start, 2 * DH)]
+        block = source[:, pl.ds(start, 2 * DH)]
         swapped = jnp.concatenate([block[:, DH:], block[:, :DH]], axis=1)
         return jnp.where((head % 2) == odd, block, swapped)
 
-    for pair in range(pairs):
-        for group in range(groups):
-            place = (pair * groups + group) * 2
-            left, right = head_ref[place], head_ref[place + 1]
-            kv_refs[pair][group, 0] = jnp.where(low, fetch(left, 0), fetch(right, 1))
-            kv_refs[pair][group, 1] = jnp.concatenate([turned[1, left], turned[1, right]], axis=0)
-            qt_refs[pair][group] = jnp.concatenate([turned[0, left], turned[0, right]], axis=0)
+    for at, out in enumerate(out_refs):
+        pair, step = divmod(at, groups)
+        place = (pair * groups + (me_ref[0] ^ step)) * 2
+        left, right = head_ref[place], head_ref[place + 1]
+        joined = [jnp.where(low, fetch(source, left, 0), fetch(source, right, 1)) for source in (k_ref, v_ref, q_ref)]
+        out[0], out[1], out[2] = joined[0], joined[1].T, joined[2].T
 
 
 def plan_kernel(groups, me_ref, lay_ref, cnt_ref, unit_ref, total_ref):
     pairs = total_ref.shape[0]
     rows = cnt_ref.shape[0] // pairs
-    own = me_ref[0]
+    slab, group = me_ref[1], me_ref[0]
 
     def local(block):
-        return ((block // groups) ^ own) * groups + block % groups
+        return ((block // groups) ^ slab) * groups + ((block % groups) ^ group)
 
     for pair in range(pairs):
 
@@ -89,18 +79,24 @@
         total_ref[pair] = total
 
 
-def attend_kernel(pair, slabs, unit_ref, total_ref, qt_ref, *refs):
-    kv_hbm, o_ref = refs[:slabs], refs[slabs]
-    kv_ref, qz_ref, m_ref, l_ref, acc_ref, sem = refs[slabs + 1 : slabs + 7]
-    score, top_of, out_of, sum_of = (refs[slabs + 7 + 2 * at : slabs + 9 + 2 * at] for at in range(4))
-    slab = qt_ref.shape[0]
+def attend_kernel(pair, slabs, slab, unit_ref, total_ref, *refs):
+    pieces, others, outs = refs[:slab], refs[slab : slab + slabs - 1], refs[slab + slabs - 1 : 2 * slab + slabs - 1]
+    refs = refs[2 * slab + slabs - 1 :]
+    kv_ref, qt_ref, qz_ref, m_ref, l_ref, acc_ref, sem = refs[:7]
+    score, top_of, out_of, sum_of = (refs[7 + 2 * at : 9 + 2 * at] for at in range(4))
     rows = 2 * slab
-    copies = [
-        pltpu.make_async_copy(source, kv_ref.at[pl.ds(at * slab, slab)], sem.at[at])
-        for at, source in enumerate(kv_hbm)
+    first = [pltpu.make_async_copy(piece.at[2], qt_ref.at[at], sem.at[at]) for at, piece in enumerate(pieces)]
+    rest = [
+        pltpu.make_async_copy(piece.at[pl.ds(0, 2)], kv_ref.at[at], sem.at[slab + at]) for at, piece in enumerate(pieces)
     ]
-    for copy in copies:
+    rest += [
+        pltpu.make_async_copy(other, kv_ref.at[pl.ds((at + 1) * slab, slab)], sem.at[2 * slab + at])
+        for at, other in enumerate(others)
+    ]
+    for copy in first + rest:
         copy.start()
+    for copy in first:
+        copy.wait()
     zeros = jnp.zeros((DH, BLK), BF16)
     for head in range(2):
         for block in range(slab):
@@ -110,9 +106,9 @@
             qz_ref[head * slab + block] = jnp.concatenate([up, down], axis=1)
     qz_ref[rows] = jnp.zeros((2 * DH, 2 * BLK), BF16)
     m_ref[...] = jnp.full(m_ref.shape, -BIG, F32)
-    for ref in (l_ref, acc_ref, *score, *top_of, *out_of, *sum_of):
+    for ref in (l_ref, acc_ref):
         ref[...] = jnp.zeros(ref.shape, F32)
-    for copy in copies:
+    for copy in rest:
         copy.wait()
     low = lax.broadcasted_iota(jnp.int32, (BLK, 2 * DH), 1) < DH
 
@@ -174,23 +170,20 @@
         for block in range(slab):
             row = head * slab + block
             total_w = jnp.sum(l_ref[row], axis=0, keepdims=True)
-            o_ref[block, head * DH : (head + 1) * DH, :] = (acc_ref[row] / total_w).astype(BF16)
-
-
-def unpack_kernel(place_ref, *refs):
+            outs[block][head * DH : (head + 1) * DH, :] = (acc_ref[row] / total_w).astype(BF16)
+
+
+def unpack_kernel(spot_ref, *refs):
     ins, out_ref, held = refs[:-2], refs[-2], refs[-1]
-    groups = ins[0].shape[0]
-    for pair, source in enumerate(ins):
-        for group in range(groups):
-            place = (pair * groups + group) * 2
-            held[place] = source[group, :DH]
-            held[place + 1] = source[group, DH:]
+    for at, source in enumerate(ins):
+        held[2 * at] = source[:DH]
+        held[2 * at + 1] = source[DH:]
     for pair in range(H // 2):
-        both = jnp.concatenate([held[place_ref[2 * pair]], held[place_ref[2 * pair + 1]]], axis=0)
+        both = jnp.concatenate([held[spot_ref[2 * pair]], held[spot_ref[2 * pair + 1]]], axis=0)
         out_ref[:, pair * 2 * DH : (pair + 1) * 2 * DH] = both.T
 
 
-def places_of(counts, groups):
+def places_of(counts, groups, me):
     load = jnp.sum(counts, axis=1)
     ids = jnp.arange(H, dtype=jnp.int32)
     ahead = (load[None, :] > load[:, None]) | ((load[None, :] == load[:, None]) & (ids[None, :] < ids[:, None]))
@@ -199,7 +192,8 @@
     group = jnp.where(turn % 2 == 0, seat, groups - 1 - seat)
     place = ((turn // 2) * groups + group) * 2 + turn % 2
     head_at = jnp.sum(jnp.where(place[None, :] == ids[:, None], ids[None, :], 0), axis=1)
-    return head_at, place
+    spot = ((turn // 2) * groups + (group ^ me)) * 2 + turn % 2
+    return head_at, spot
 
 
 def shards(queries, key_vectors, value_vectors, layout, counts):
@@ -209,26 +203,28 @@
     slab = groups
     rows = 2 * slab
     shape = jax.ShapeDtypeStruct
-    head_at, place = places_of(counts, groups)
+    me, own = lax.axis_index("uly"), lax.axis_index("doc")
+    where = jnp.stack([me, own])
+    head_at, spot = places_of(counts, groups, me)
     packed = pl.pallas_call(
-        pack_kernel,
-        out_shape=(shape((groups, 2, BLK, BLK), BF16),) * pairs + (shape((groups, BLK, BLK), BF16),) * pairs,
-        in_specs=[SMEM, VMEM, VMEM, VMEM],
-        out_specs=(VMEM,) * (2 * pairs),
-        scratch_shapes=[pltpu.VMEM((2, H, DH, BLK), BF16)],
+        functools.partial(pack_kernel, groups),
+        out_shape=(shape((3, BLK, BLK), BF16),) * (pairs * groups),
+        in_specs=[SMEM, SMEM, VMEM, VMEM, VMEM],
+        out_specs=(VMEM,) * (pairs * groups),
         compiler_params=PARAMS,
         name="pack",
-    )(head_at, queries, key_vectors, value_vectors)
-    swap = functools.partial(lax.all_to_all, axis_name="uly", split_axis=0, concat_axis=0, tiled=True)
-
-    def flip(array, bit):
-        return lax.ppermute(array, "doc", [(at, at ^ bit) for at in range(slabs)])
-
-    own = lax.axis_index("doc")
-    mine = head_at.reshape(pairs, groups, 2)
-    mine = lax.dynamic_index_in_dim(mine, lax.axis_index("uly"), 1, keepdims=False).reshape(-1)
-    lay = jnp.take(lax.dynamic_slice_in_dim(layout, own * slab, slab, axis=1), mine, axis=0).reshape(-1)
-    cnt = jnp.take(lax.dynamic_slice_in_dim(counts, own * slab, slab, axis=1), mine, axis=0).reshape(-1)
+    )(where, head_at, queries, key_vectors, value_vectors)
+
+    def flip(array, axis, size, bit):
+        return lax.ppermute(array, axis, [(at, at ^ bit) for at in range(size)])
+
+    def exchange(pieces):
+        return [piece if step == 0 else flip(piece, "uly", groups, step) for step, piece in enumerate(pieces)]
+
+    mine = lax.dynamic_index_in_dim(head_at.reshape(pairs, groups, 2), me, 1, keepdims=False).reshape(-1)
+    order = jnp.arange(groups, dtype=jnp.int32) ^ me
+    lay = jnp.take(jnp.take(layout, mine, axis=0), own * slab + order, axis=1).reshape(-1)
+    cnt = jnp.take(jnp.take(counts, mine, axis=0), own * slab + order, axis=1).reshape(-1)
     units, totals = pl.pallas_call(
         functools.partial(plan_kernel, groups),
         out_shape=(
@@ -239,46 +235,46 @@
         out_specs=(SMEM, SMEM),
         compiler_params=PARAMS,
         name="plan",
-    )(own.reshape(1), lay, cnt)
+    )(where, lay, cnt)
 
     returned = []
     for pair in range(pairs):
-        kv = swap(packed[pair])
-        qt = swap(packed[pairs + pair])
-        gathered = {0: kv}
+        pieces = exchange(packed[pair * groups : (pair + 1) * groups])
+        gathered = {0: jnp.stack([piece[:2] for piece in pieces])}
         bit = slabs // 2
         while bit:
-            gathered.update({at ^ bit: flip(array, bit) for at, array in list(gathered.items())})
+            gathered.update({at ^ bit: flip(array, "doc", slabs, bit) for at, array in list(gathered.items())})
             bit //= 2
         both = [pltpu.VMEM((UNROLL, BLK, 2 * BLK), F32)] * 2 + [pltpu.VMEM((UNROLL, 8, BLK), F32)] * 2
         both += [pltpu.VMEM((UNROLL, DH, BLK), F32)] * 2 + [pltpu.VMEM((UNROLL, 8, BLK), F32)] * 2
         out = pl.pallas_call(
-            functools.partial(attend_kernel, pair, slabs),
-            out_shape=shape((slab, BLK, BLK), BF16),
-            in_specs=[SMEM, SMEM, VMEM] + [ANY] * slabs,
-            out_specs=VMEM,
+            functools.partial(attend_kernel, pair, slabs, slab),
+            out_shape=(shape((BLK, BLK), BF16),) * slab,
+            in_specs=[SMEM, SMEM] + [ANY] * (slab + slabs - 1),
+            out_specs=(VMEM,) * slab,
             scratch_shapes=[
                 pltpu.VMEM((slabs * slab, 2, BLK, BLK), BF16),
+                pltpu.VMEM((slab, BLK, BLK), BF16),
                 pltpu.VMEM((rows + 1, 2 * DH, 2 * BLK), BF16),
                 pltpu.VMEM((rows + 1, 8, BLK), F32),
                 pltpu.VMEM((rows + 1, 8, BLK), F32),
                 pltpu.VMEM((rows + 1, DH, BLK), F32),
-                pltpu.SemaphoreType.DMA((slabs,)),
+                pltpu.SemaphoreType.DMA((2 * slab + slabs - 1,)),
                 *both,
             ],
             compiler_params=PARAMS,
             name="attend",
-        )(units, totals, qt, *[gathered[at] for at in range(slabs)])
-        returned.append(swap(out))
+        )(units, totals, *pieces, *[gathered[at] for at in range(1, slabs)])
+        returned += exchange(out)
     return pl.pallas_call(
         unpack_kernel,
         out_shape=shape(queries.shape, BF16),
-        in_specs=[SMEM] + [VMEM] * pairs,
+        in_specs=[SMEM] + [VMEM] * len(returned),
         out_specs=VMEM,
         scratch_shapes=[pltpu.VMEM((H, DH, BLK), BF16)],
         compiler_params=PARAMS,
         name="unpack",
-    )(place, *returned)
+    )(spot, *returned)
 
 
 def solution(mesh):

time: 113 us -> 127 us (1.12)
  blocking collectives: 36.2 us -> 0 us
  starting transfers between devices: 20.3 us -> 50.4 us
  local copies, waits for them, and re-layouts: 6.55 us -> 19.6 us
  Pallas kernels: 30.3 us -> 34.5 us
  other arithmetic: 1.92 us -> 3.85 us
    ppermute x6 -> x34, starting transfers between devices: 3.76 us -> 50.4 us  [flip(): return lax.ppermute(array, axis, [(at, at ^ bit) for at in range(size)])]
    all_to_all x2 -> x0, blocking collectives: 36.2 us -> none  [the longest x1 21.8 us: shards(): kv = swap(packed[pair])]
    all_to_all x4 -> x0, waiting for transfers between devices: 16.7 us -> none  [the longest x1 11.2 us: shards(): kv = swap(packed[pair])]
    all_to_all x4 -> x0, starting transfers between devices: 16.6 us -> none  [the longest x2 7.22 us: shards(): qt = swap(packed[pairs + pair])]
    ppermute x6 -> x34, waiting for transfers between devices: 0.34 us -> 16.6 us  [flip(): return lax.ppermute(array, axis, [(at, at ^ bit) for at in range(size)])]
    unnamed x22 -> x112, local copies, waits for them, and re-layouts: 2.67 us -> 13.2 us
    pallas_call x3, Pallas kernels: 22.6 us -> 26.5 us  [the longest x2 21.9 us: shards(): pl.pallas_call(functools.partial(attend_kernel, pair, slabs, slab), out_s...]
  transfers between devices with their start and end apart: 10 -> 34, of which waited for: 3 -> 4; matrix products, arithmetic and copies ran while one was open for 4% -> 14% of each run, Pallas kernels for 22% -> 22%
where the time goes in v3:
time: 127 us; the launch traced here: 125 us
  starting transfers between devices  50.4 us (40%)
  Pallas kernels  34.5 us (27%)
  local copies, waits for them, and re-layouts  19.6 us (15%)
  waiting for transfers between devices  16.6 us (13%)
  other arithmetic  3.85 us (3%)
    ppermute x34, starting transfers between devices, flip(): return lax.ppermute(array, axis, [(at, at ^ bit) for at in range(size)])  50.4 us
    pallas_call x2, Pallas kernels, shards(): pl.pallas_call(functools.partial(attend_kernel, pair, slabs, slab), out_s...  21.9 us
    ppermute x34, waiting for transfers between devices, flip(): return lax.ppermute(array, axis, [(at, at ^ bit) for at in range(size)])  16.6 us
    unnamed x112, local copies, waits for them, and re-layouts  13.2 us
    pallas_call x1, Pallas kernels, shards(): pl.pallas_call(functools.partial(plan_kernel, groups), out_shape=(shape((...  5.93 us
    pallas_call x1, Pallas kernels, shards(): pl.pallas_call(functools.partial(pack_kernel, groups), out_shape=(shape((...  4.59 us
  transfers between devices with their start and end apart: 34, of which 4 were waited for; matrix products, arithmetic and copies ran while one was open for 14% of the time, Pallas kernels for 22%

profile of v3, /device:TPU:0, one launch (start us, length us, event | category | flops | bytes accessed | tf_op | source)
XLA Modules:
  0.0 125.5 jit_solution(2645869201301106200)
XLA Ops:
  0.0 0.9 reduce_sum.27
  3.0 4.6 %pack.1 = (bf16[3,128,128]{2,1,0:T(8,128)(2,1)}, bf16[3,128,128]{2,1,0:T(8,128)(2,1)}, bf16[3,128,128]{2,1,0:T(8,128)(2,1)}, bf16[3,128,128]{2,1,0:T(8,128)(2,1)...) custom-call(s32[2]{0:T(128)} %pad_add_fusion.me_ref, ...), custom_call_target="tpu_custom_call" | custom-call | tf_op jit(solution)/shard_map/pack/pallas_call | solution.py:209
  7.5 3.0 %collective-permute-start = (bf16[3,128,128]{2,1,0:T(8,128)(2,1)}, bf16[3,128,128]{2,1,0:T(8,128)(2,1)S(1)}, u32[]{:S(2)}, u32[]{:S(2)}) collective-permute-start(bf16[3,128,128]{2,1,0:T(8,128)(2,1)} %get-tuple-element.42), channel_id=1, source_target_pairs={{0,4},{4,0},{8,12},{12,8},{16,20},{20,16},{24,28},{28,24},{1,5},{5... | collective-permute-start | bytes 294920 | tf_op jit(solution)/shard_map/ppermute | solution.py:219
  10.6 1.6 %collective-permute-start.1 = (bf16[3,128,128]{2,1,0:T(8,128)(2,1)}, bf16[3,128,128]{2,1,0:T(8,128)(2,1)S(1)}, u32[]{:S(2)}, u32[]{:S(2)}) collective-permute-start(bf16[3,128,128]{2,1,0:T(8,128)(2,1)} %get-tuple-element.43), channel_id=1, source_target_pairs={{0,8},{4,12},{8,0},{12,4},{16,24},{20,28},{24,16},{28,20},{1,9},{5... | collective-permute-start | bytes 294920 | tf_op jit(solution)/shard_map/ppermute | solution.py:219
  12.2 3.0 %collective-permute-start.3 = (bf16[3,128,128]{2,1,0:T(8,128)(2,1)}, bf16[3,128,128]{2,1,0:T(8,128)(2,1)S(1)}, u32[]{:S(2)}, u32[]{:S(2)}) collective-permute-start(bf16[3,128,128]{2,1,0:T(8,128)(2,1)} %get-tuple-element.45), channel_id=1, source_target_pairs={{0,16},{4,20},{8,24},{12,28},{16,0},{20,4},{24,8},{28,12},{1,17},{... | collective-permute-start | bytes 294920 | tf_op jit(solution)/shard_map/ppermute | solution.py:219
  15.1 1.3 %collective-permute-start.4 = (bf16[3,128,128]{2,1,0:T(8,128)(2,1)}, bf16[3,128,128]{2,1,0:T(8,128)(2,1)S(1)}, u32[]{:S(2)}, u32[]{:S(2)}) collective-permute-start(bf16[3,128,128]{2,1,0:T(8,128)(2,1)} %get-tuple-element.46), channel_id=1, source_target_pairs={{0,20},{4,16},{8,28},{12,24},{16,4},{20,0},{24,12},{28,8},{1,21},{... | collective-permute-start | bytes 294920 | tf_op jit(solution)/shard_map/ppermute | solution.py:219
  17.9 1.5 %bitcast_dynamic-update-slice_fusion.1 = bf16[8,2,128,128]{3,2,1,0:T(8,128)(2,1)} fusion(bf16[3,128,128]{2,1,0:T(8,128)(2,1)} %get-tuple-element.41.refs_0_), kind=kLoop, calls=%fused_computation.33 | loop fusion | bytes 131072
  20.9 3.6 %collective-permute-start.5 = (bf16[3,128,128]{2,1,0:T(8,128)(2,1)S(1)}, bf16[3,128,128]{2,1,0:T(8,128)(2,1)S(1)}, u32[]{:S(2)}, u32[]{:S(2)}) collective-permute-start(bf16[3,128,128]{2,1,0:T(8,128)(2,1)S(1)} %copy-done.46), channel_id=1, source_target_pairs={{0,24},{4,28},{8,16},{12,20},{16,8},{20,12},{24,0},{28,4},{1,25},{... | collective-permute-start | bytes 294920 | tf_op jit(solution)/shard_map/ppermute | solution.py:219
  26.0 1.6 %collective-permute-start.17 = (bf16[3,128,128]{2,1,0:T(8,128)(2,1)S(1)}, bf16[3,128,128]{2,1,0:T(8,128)(2,1)S(1)}, u32[]{:S(2)}, u32[]{:S(2)}) collective-permute-start(bf16[3,128,128]{2,1,0:T(8,128)(2,1)S(1)} %copy-done.44), channel_id=1, source_target_pairs={{0,4},{4,0},{8,12},{12,8},{16,20},{20,16},{24,28},{28,24},{1,5},{5... | collective-permute-start | bytes 294920 | tf_op jit(solution)/shard_map/ppermute | solution.py:219
  29.2 1.8 %collective-permute-start.19 = (bf16[3,128,128]{2,1,0:T(8,128)(2,1)S(1)}, bf16[3,128,128]{2,1,0:T(8,128)(2,1)S(1)}, u32[]{:S(2)}, u32[]{:S(2)}) collective-permute-start(bf16[3,128,128]{2,1,0:T(8,128)(2,1)S(1)} %copy-done.42), channel_id=1, source_target_pairs={{0,12},{4,8},{8,4},{12,0},{16,28},{20,24},{24,20},{28,16},{1,13},{... | collective-permute-start | bytes 294920 | tf_op jit(solution)/shard_map/ppermute | solution.py:219
  31.6 2.6 %collective-permute-start.20 = (bf16[3,128,128]{2,1,0:T(8,128)(2,1)S(1)}, bf16[3,128,128]{2,1,0:T(8,128)(2,1)S(1)}, u32[]{:S(2)}, u32[]{:S(2)}) collective-permute-start(bf16[3,128,128]{2,1,0:T(8,128)(2,1)S(1)} %copy-done.41), channel_id=1, source_target_pairs={{0,16},{4,20},{8,24},{12,28},{16,0},{20,4},{24,8},{28,12},{1,17},{... | collective-permute-start | bytes 294920 | tf_op jit(solution)/shard_map/ppermute | solution.py:219
  34.9 1.6 %collective-permute-start.21 = (bf16[3,128,128]{2,1,0:T(8,128)(2,1)S(1)}, bf16[3,128,128]{2,1,0:T(8,128)(2,1)S(1)}, u32[]{:S(2)}, u32[]{:S(2)}) collective-permute-start(bf16[3,128,128]{2,1,0:T(8,128)(2,1)S(1)} %copy-done.40), channel_id=1, source_target_pairs={{0,20},{4,16},{8,28},{12,24},{16,4},{20,0},{24,12},{28,8},{1,21},{... | collective-permute-start | bytes 294920 | tf_op jit(solution)/shard_map/ppermute | solution.py:219
  37.2 3.5 %collective-permute-start.22 = (bf16[3,128,128]{2,1,0:T(8,128)(2,1)S(1)}, bf16[3,128,128]{2,1,0:T(8,128)(2,1)S(1)}, u32[]{:S(2)}, u32[]{:S(2)}) collective-permute-start(bf16[3,128,128]{2,1,0:T(8,128)(2,1)S(1)} %copy-done.39), channel_id=1, source_target_pairs={{0,24},{4,28},{8,16},{12,20},{16,8},{20,12},{24,0},{28,4},{1,25},{... | collective-permute-start | bytes 294920 | tf_op jit(solution)/shard_map/ppermute | solution.py:219
  41.3 1.2 collective-permute-start.23
  43.1 1.6 %collective-permute-start.8 = (bf16[8,2,128,128]{3,2,1,0:T(8,128)(2,1)}, bf16[8,2,128,128]{3,2,1,0:T(8,128)(2,1)S(1)}, u32[]{:S(2)}, u32[]{:S(2)}) collective-permute-start(bf16[8,2,128,128]{3,2,1,0:T(8,128)(2,1)} %fusion.7), channel_id=1, source_target_pairs={{0,2},{1,3},{2,0},{3,1},{4,6},{5,7},{6,4},{7,5},{8,10},{9,11},{10,... | collective-permute-start | bytes 1572872 | tf_op jit(solution)/shard_map/ppermute | solution.py:219
  46.0 1.7 %collective-permute-done.21.refs_5_ = bf16[3,128,128]{2,1,0:T(8,128)(2,1)S(1)} collective-permute-done((bf16[3,128,128]{2,1,0:T(8,128)(2,1)S(1)}, bf16[3,128,128]{2,1,0:T(8,128)(2,1)S(1)}, u32[]{:S(2)}, u32[]{:S(2)}) %collective-permute-start.21) | collective-permute-done | bytes 98336 | tf_op jit(solution)/shard_map/ppermute | solution.py:219
  50.3 1.5 %collective-permute-start.25 = (bf16[8,2,128,128]{3,2,1,0:T(8,128)(2,1)}, bf16[8,2,128,128]{3,2,1,0:T(8,128)(2,1)S(1)}, u32[]{:S(2)}, u32[]{:S(2)}) collective-permute-start(bf16[8,2,128,128]{3,2,1,0:T(8,128)(2,1)} %fusion), channel_id=1, source_target_pairs={{0,2},{1,3},{2,0},{3,1},{4,6},{5,7},{6,4},{7,5},{8,10},{9,11},{10,... | collective-permute-start | bytes 1572872 | tf_op jit(solution)/shard_map/ppermute | solution.py:219
  53.1 5.2 %collective-permute-done.8.refs_9_ = bf16[8,2,128,128]{3,2,1,0:T(8,128)(2,1)S(1)} collective-permute-done((bf16[8,2,128,128]{3,2,1,0:T(8,128)(2,1)}, bf16[8,2,128,128]{3,2,1,0:T(8,128)(2,1)S(1)}, u32[]{:S(2)}, u32[]{:S(2)}) %collective-permute-start.8) | collective-permute-done | bytes 524320 | tf_op jit(solution)/shard_map/ppermute | solution.py:219
  58.3 7.9 %collective-permute-done.25.refs_9_ = bf16[8,2,128,128]{3,2,1,0:T(8,128)(2,1)S(1)} collective-permute-done((bf16[8,2,128,128]{3,2,1,0:T(8,128)(2,1)}, bf16[8,2,128,128]{3,2,1,0:T(8,128)(2,1)S(1)}, u32[]{:S(2)}, u32[]{:S(2)}) %collective-permute-start.25) | collective-permute-done | bytes 524320 | tf_op jit(solution)/shard_map/ppermute | solution.py:219
  69.1 5.9 %plan.1 = (s32[2,4,288]{2,1,0:T(4,128)}, s32[2]{0:T(128)}) custom-call(s32[2]{0:T(128)} %pad_add_fusion.me_ref, s32[1024]{0:T(1024)} %select_n.128.lay_ref, s32[32]{0:T(128)} %select_n.131.cnt_ref), custom_call_target="tpu_custom_call" | custom-call | tf_op jit(solution)/shard_map/plan/pallas_call | solution.py:228
  75.8 14.2 %attend.2 = (bf16[128,128]{1,0:T(8,128)(2,1)}, bf16[128,128]{1,0:T(8,128)(2,1)}, bf16[128,128]{1,0:T(8,128)(2,1)}, bf16[128,128]{1,0:T(8,128)(2,1)}, bf16[128,12...) custom-call(s32[2,4,288]{2,1,0:T(4,128)} %get-tuple-element.39.unit_ref, ...), custom_call_target="tpu_custom_call" | custom-call | tf_op jit(solution)/shard_map/attend/pallas_call | solution.py:250
  90.2 3.4 %collective-permute-start.12 = (bf16[128,128]{1,0:T(8,128)(2,1)}, bf16[128,128]{1,0:T(8,128)(2,1)S(1)}, u32[]{:S(2)}, u32[]{:S(2)}) collective-permute-start(bf16[128,128]{1,0:T(8,128)(2,1)} %get-tuple-element.52), channel_id=1, source_target_pairs={{0,12},{4,8},{8,4},{12,0},{16,28},{20,24},{24,20},{28,16},{1,13},{... | collective-permute-start | bytes 98312 | tf_op jit(solution)/shard_map/ppermute | solution.py:219
  93.7 2.5 %collective-permute-start.14 = (bf16[128,128]{1,0:T(8,128)(2,1)}, bf16[128,128]{1,0:T(8,128)(2,1)S(1)}, u32[]{:S(2)}, u32[]{:S(2)}) collective-permute-start(bf16[128,128]{1,0:T(8,128)(2,1)} %get-tuple-element.54), channel_id=1, source_target_pairs={{0,20},{4,16},{8,28},{12,24},{16,4},{20,0},{24,12},{28,8},{1,21},{... | collective-permute-start | bytes 98312 | tf_op jit(solution)/shard_map/ppermute | solution.py:219
  96.2 7.7 %attend.3 = (bf16[128,128]{1,0:T(8,128)(2,1)}, bf16[128,128]{1,0:T(8,128)(2,1)}, bf16[128,128]{1,0:T(8,128)(2,1)}, bf16[128,128]{1,0:T(8,128)(2,1)}, bf16[128,12...) custom-call(s32[2,4,288]{2,1,0:T(4,128)} %get-tuple-element.39.unit_ref, ...), custom_call_target="tpu_custom_call" | custom-call | tf_op jit(solution)/shard_map/attend/pallas_call | solution.py:250
  103.9 0.9 collective-permute-start.15
  104.8 3.8 %collective-permute-start.16 = (bf16[128,128]{1,0:T(8,128)(2,1)S(1)}, bf16[128,128]{1,0:T(8,128)(2,1)S(1)}, u32[]{:S(2)}, u32[]{:S(2)}) collective-permute-start(bf16[128,128]{1,0:T(8,128)(2,1)S(1)} %copy-done.47), channel_id=1, source_target_pairs={{0,28},{4,24},{8,20},{12,16},{16,12},{20,8},{24,4},{28,0},{1,29},{... | collective-permute-start | bytes 98312 | tf_op jit(solution)/shard_map/ppermute | solution.py:219
  109.3 2.8 %collective-permute-start.29 = (bf16[128,128]{1,0:T(8,128)(2,1)}, bf16[128,128]{1,0:T(8,128)(2,1)S(1)}, u32[]{:S(2)}, u32[]{:S(2)}) collective-permute-start(bf16[128,128]{1,0:T(8,128)(2,1)} %get-tuple-element.68), channel_id=1, source_target_pairs={{0,12},{4,8},{8,4},{12,0},{16,28},{20,24},{24,20},{28,16},{1,13},{... | collective-permute-start | bytes 98312 | tf_op jit(solution)/shard_map/ppermute | solution.py:219
  112.1 3.0 %collective-permute-start.31 = (bf16[128,128]{1,0:T(8,128)(2,1)}, bf16[128,128]{1,0:T(8,128)(2,1)S(1)}, u32[]{:S(2)}, u32[]{:S(2)}) collective-permute-start(bf16[128,128]{1,0:T(8,128)(2,1)} %get-tuple-element.70), channel_id=1, source_target_pairs={{0,20},{4,16},{8,28},{12,24},{16,4},{20,0},{24,12},{28,8},{1,21},{... | collective-permute-start | bytes 98312 | tf_op jit(solution)/shard_map/ppermute | solution.py:219
  115.2 0.8 collective-permute-start.32
  116.0 3.7 %collective-permute-start.33 = (bf16[128,128]{1,0:T(8,128)(2,1)}, bf16[128,128]{1,0:T(8,128)(2,1)S(1)}, u32[]{:S(2)}, u32[]{:S(2)}) collective-permute-start(bf16[128,128]{1,0:T(8,128)(2,1)} %get-tuple-element.72), channel_id=1, source_target_pairs={{0,28},{4,24},{8,20},{12,16},{16,12},{20,8},{24,4},{28,0},{1,29},{... | collective-permute-start | bytes 98312 | tf_op jit(solution)/shard_map/ppermute | solution.py:219
  121.1 1.8 %collective-permute-done.33.refs_15_ = bf16[128,128]{1,0:T(8,128)(2,1)S(1)} collective-permute-done((bf16[128,128]{1,0:T(8,128)(2,1)}, bf16[128,128]{1,0:T(8,128)(2,1)S(1)}, u32[]{:S(2)}, u32[]{:S(2)}) %collective-permute-start.33) | collective-permute-done | bytes 32800 | tf_op jit(solution)/shard_map/ppermute | solution.py:219
  123.5 2.0 %unpack.1 = bf16[128,2048]{1,0:T(8,128)(2,1)} custom-call(s32[32]{0:T(128)} %multiply_add_fusion.1.spot_ref, bf16[128,128]{1,0:T(8,128)(2,1)} %get-tuple-element.49.refs_0_, bf16[128,128]{1,0:T(8,128)(2,1)} %copy-done.22, bf16[128,128]{1,0:T(8,128)(2,1)} %copy-done.23, bf16[128,128]{1,0:T(8,128)(2,1)} %copy-done.24, bf16[128,128]{1,0:T(8,128)(2,1)} %copy-done.25, ...), custom_call_target="tpu_custom_call" | custom-call | tf_op jit(solution)/shard_map/unpack/pallas_call | solution.py:269
  (185 shorter events, 22.8 us)
Async XLA Ops:
  7.5 13.0 %collective-permute-start = (bf16[3,128,128]{2,1,0:T(8,128)(2,1)}, bf16[3,128,128]{2,1,0:T(8,128)(2,1)S(1)}, u32[]{:S(2)}, u32[]{:S(2)}) collective-permute-start(bf16[3,128,128]{2,1,0:T(8,128)(2,1)} %get-tuple-element.42), channel_id=1, source_target_pairs={{0,4},{4,0},{8,12},{12,8},{16,20},{20,16},{24,28},{28,24},{1,5},{5... | collective-permute-start | bytes 294920 | tf_op jit(solution)/shard_map/ppermute | solution.py:219
  10.6 14.5 %collective-permute-start.1 = (bf16[3,128,128]{2,1,0:T(8,128)(2,1)}, bf16[3,128,128]{2,1,0:T(8,128)(2,1)S(1)}, u32[]{:S(2)}, u32[]{:S(2)}) collective-permute-start(bf16[3,128,128]{2,1,0:T(8,128)(2,1)} %get-tuple-element.43), channel_id=1, source_target_pairs={{0,8},{4,12},{8,0},{12,4},{16,24},{20,28},{24,16},{28,20},{1,9},{5... | collective-permute-start | bytes 294920 | tf_op jit(solution)/shard_map/ppermute | solution.py:219
  12.2 13.7 %collective-permute-start.2 = (bf16[3,128,128]{2,1,0:T(8,128)(2,1)}, bf16[3,128,128]{2,1,0:T(8,128)(2,1)S(1)}, u32[]{:S(2)}, u32[]{:S(2)}) collective-permute-start(bf16[3,128,128]{2,1,0:T(8,128)(2,1)} %get-tuple-element.44), channel_id=1, source_target_pairs={{0,12},{4,8},{8,4},{12,0},{16,28},{20,24},{24,20},{28,16},{1,13},{... | collective-permute-start | bytes 294920 | tf_op jit(solution)/shard_map/ppermute | solution.py:219
  12.2 16.1 %collective-permute-start.3 = (bf16[3,128,128]{2,1,0:T(8,128)(2,1)}, bf16[3,128,128]{2,1,0:T(8,128)(2,1)S(1)}, u32[]{:S(2)}, u32[]{:S(2)}) collective-permute-start(bf16[3,128,128]{2,1,0:T(8,128)(2,1)} %get-tuple-element.45), channel_id=1, source_target_pairs={{0,16},{4,20},{8,24},{12,28},{16,0},{20,4},{24,8},{28,12},{1,17},{... | collective-permute-start | bytes 294920 | tf_op jit(solution)/shard_map/ppermute | solution.py:219
  15.1 13.8 %collective-permute-start.4 = (bf16[3,128,128]{2,1,0:T(8,128)(2,1)}, bf16[3,128,128]{2,1,0:T(8,128)(2,1)S(1)}, u32[]{:S(2)}, u32[]{:S(2)}) collective-permute-start(bf16[3,128,128]{2,1,0:T(8,128)(2,1)} %get-tuple-element.46), channel_id=1, source_target_pairs={{0,20},{4,16},{8,28},{12,24},{16,4},{20,0},{24,12},{28,8},{1,21},{... | collective-permute-start | bytes 294920 | tf_op jit(solution)/shard_map/ppermute | solution.py:219
  20.9 10.7 %collective-permute-start.5 = (bf16[3,128,128]{2,1,0:T(8,128)(2,1)S(1)}, bf16[3,128,128]{2,1,0:T(8,128)(2,1)S(1)}, u32[]{:S(2)}, u32[]{:S(2)}) collective-permute-start(bf16[3,128,128]{2,1,0:T(8,128)(2,1)S(1)} %copy-done.46), channel_id=1, source_target_pairs={{0,24},{4,28},{8,16},{12,20},{16,8},{20,12},{24,0},{28,4},{1,25},{... | collective-permute-start | bytes 294920 | tf_op jit(solution)/shard_map/ppermute | solution.py:219
  25.1 9.7 %collective-permute-start.6 = (bf16[3,128,128]{2,1,0:T(8,128)(2,1)S(1)}, bf16[3,128,128]{2,1,0:T(8,128)(2,1)S(1)}, u32[]{:S(2)}, u32[]{:S(2)}) collective-permute-start(bf16[3,128,128]{2,1,0:T(8,128)(2,1)S(1)} %copy-done.45), channel_id=1, source_target_pairs={{0,28},{4,24},{8,20},{12,16},{16,12},{20,8},{24,4},{28,0},{1,29},{... | collective-permute-start | bytes 294920 | tf_op jit(solution)/shard_map/ppermute | solution.py:219
  26.0 11.1 %collective-permute-start.17 = (bf16[3,128,128]{2,1,0:T(8,128)(2,1)S(1)}, bf16[3,128,128]{2,1,0:T(8,128)(2,1)S(1)}, u32[]{:S(2)}, u32[]{:S(2)}) collective-permute-start(bf16[3,128,128]{2,1,0:T(8,128)(2,1)S(1)} %copy-done.44), channel_id=1, source_target_pairs={{0,4},{4,0},{8,12},{12,8},{16,20},{20,16},{24,28},{28,24},{1,5},{5... | collective-permute-start | bytes 294920 | tf_op jit(solution)/shard_map/ppermute | solution.py:219
  28.3 13.0 %collective-permute-start.18 = (bf16[3,128,128]{2,1,0:T(8,128)(2,1)S(1)}, bf16[3,128,128]{2,1,0:T(8,128)(2,1)S(1)}, u32[]{:S(2)}, u32[]{:S(2)}) collective-permute-start(bf16[3,128,128]{2,1,0:T(8,128)(2,1)S(1)} %copy-done.43), channel_id=1, source_target_pairs={{0,8},{4,12},{8,0},{12,4},{16,24},{20,28},{24,16},{28,20},{1,9},{5... | collective-permute-start | bytes 294920 | tf_op jit(solution)/shard_map/ppermute | solution.py:219
  29.2 14.0 %collective-permute-start.19 = (bf16[3,128,128]{2,1,0:T(8,128)(2,1)S(1)}, bf16[3,128,128]{2,1,0:T(8,128)(2,1)S(1)}, u32[]{:S(2)}, u32[]{:S(2)}) collective-permute-start(bf16[3,128,128]{2,1,0:T(8,128)(2,1)S(1)} %copy-done.42), channel_id=1, source_target_pairs={{0,12},{4,8},{8,4},{12,0},{16,28},{20,24},{24,20},{28,16},{1,13},{... | collective-permute-start | bytes 294920 | tf_op jit(solution)/shard_map/ppermute | solution.py:219
  31.6 13.7 %collective-permute-start.20 = (bf16[3,128,128]{2,1,0:T(8,128)(2,1)S(1)}, bf16[3,128,128]{2,1,0:T(8,128)(2,1)S(1)}, u32[]{:S(2)}, u32[]{:S(2)}) collective-permute-start(bf16[3,128,128]{2,1,0:T(8,128)(2,1)S(1)} %copy-done.41), channel_id=1, source_target_pairs={{0,16},{4,20},{8,24},{12,28},{16,0},{20,4},{24,8},{28,12},{1,17},{... | collective-permute-start | bytes 294920 | tf_op jit(solution)/shard_map/ppermute | solution.py:219
  34.9 12.8 %collective-permute-start.21 = (bf16[3,128,128]{2,1,0:T(8,128)(2,1)S(1)}, bf16[3,128,128]{2,1,0:T(8,128)(2,1)S(1)}, u32[]{:S(2)}, u32[]{:S(2)}) collective-permute-start(bf16[3,128,128]{2,1,0:T(8,128)(2,1)S(1)} %copy-done.40), channel_id=1, source_target_pairs={{0,20},{4,16},{8,28},{12,24},{16,4},{20,0},{24,12},{28,8},{1,21},{... | collective-permute-start | bytes 294920 | tf_op jit(solution)/shard_map/ppermute | solution.py:219
  37.2 11.2 %collective-permute-start.22 = (bf16[3,128,128]{2,1,0:T(8,128)(2,1)S(1)}, bf16[3,128,128]{2,1,0:T(8,128)(2,1)S(1)}, u32[]{:S(2)}, u32[]{:S(2)}) collective-permute-start(bf16[3,128,128]{2,1,0:T(8,128)(2,1)S(1)} %copy-done.39), channel_id=1, source_target_pairs={{0,24},{4,28},{8,16},{12,20},{16,8},{20,12},{24,0},{28,4},{1,25},{... | collective-permute-start | bytes 294920 | tf_op jit(solution)/shard_map/ppermute | solution.py:219
  41.3 7.7 %collective-permute-start.23 = (bf16[3,128,128]{2,1,0:T(8,128)(2,1)S(1)}, bf16[3,128,128]{2,1,0:T(8,128)(2,1)S(1)}, u32[]{:S(2)}, u32[]{:S(2)}) collective-permute-start(bf16[3,128,128]{2,1,0:T(8,128)(2,1)S(1)} %copy-done.38), channel_id=1, source_target_pairs={{0,28},{4,24},{8,20},{12,16},{16,12},{20,8},{24,4},{28,0},{1,29},{... | collective-permute-start | bytes 294920 | tf_op jit(solution)/shard_map/ppermute | solution.py:219
  43.1 15.1 %collective-permute-start.8 = (bf16[8,2,128,128]{3,2,1,0:T(8,128)(2,1)}, bf16[8,2,128,128]{3,2,1,0:T(8,128)(2,1)S(1)}, u32[]{:S(2)}, u32[]{:S(2)}) collective-permute-start(bf16[8,2,128,128]{3,2,1,0:T(8,128)(2,1)} %fusion.7), channel_id=1, source_target_pairs={{0,2},{1,3},{2,0},{3,1},{4,6},{5,7},{6,4},{7,5},{8,10},{9,11},{10,... | collective-permute-start | bytes 1572872 | tf_op jit(solution)/shard_map/ppermute | solution.py:219
  50.3 15.9 %collective-permute-start.25 = (bf16[8,2,128,128]{3,2,1,0:T(8,128)(2,1)}, bf16[8,2,128,128]{3,2,1,0:T(8,128)(2,1)S(1)}, u32[]{:S(2)}, u32[]{:S(2)}) collective-permute-start(bf16[8,2,128,128]{3,2,1,0:T(8,128)(2,1)} %fusion), channel_id=1, source_target_pairs={{0,2},{1,3},{2,0},{3,1},{4,6},{5,7},{6,4},{7,5},{8,10},{9,11},{10,... | collective-permute-start | bytes 1572872 | tf_op jit(solution)/shard_map/ppermute | solution.py:219
  52.5 22.5 %collective-permute-start.7 = (bf16[8,2,128,128]{3,2,1,0:T(8,128)(2,1)}, bf16[8,2,128,128]{3,2,1,0:T(8,128)(2,1)S(1)}, u32[]{:S(2)}, u32[]{:S(2)}) collective-permute-start(bf16[8,2,128,128]{3,2,1,0:T(8,128)(2,1)} %fusion.7), channel_id=1, source_target_pairs={{0,1},{1,0},{2,3},{3,2},{4,5},{5,4},{6,7},{7,6},{8,9},{9,8},{10,11... | collective-permute-start | bytes 1572872 | tf_op jit(solution)/shard_map/ppermute | solution.py:219
  52.6 41.0 %collective-permute-start.24 = (bf16[8,2,128,128]{3,2,1,0:T(8,128)(2,1)}, bf16[8,2,128,128]{3,2,1,0:T(8,128)(2,1)S(1)}, u32[]{:S(2)}, u32[]{:S(2)}) collective-permute-start(bf16[8,2,128,128]{3,2,1,0:T(8,128)(2,1)} %fusion), channel_id=1, source_target_pairs={{0,1},{1,0},{2,3},{3,2},{4,5},{5,4},{6,7},{7,6},{8,9},{9,8},{10,11... | collective-permute-start | bytes 1572872 | tf_op jit(solution)/shard_map/ppermute | solution.py:219
  58.3 16.7 %collective-permute-start.9 = (bf16[8,2,128,128]{3,2,1,0:T(8,128)(2,1)S(1)}, bf16[8,2,128,128]{3,2,1,0:T(8,128)(2,1)}, u32[]{:S(2)}, u32[]{:S(2)}) collective-permute-start(bf16[8,2,128,128]{3,2,1,0:T(8,128)(2,1)S(1)} %collective-permute-done.8.refs_9_), channel_id=1, source_target_pairs={{0,1},{1,0},{2,3},{3,2},{4,5},{5,4},{6,7},{7,6},{8,9},{9,8},{10,11... | collective-permute-start | bytes 1572872 | tf_op jit(solution)/shard_map/ppermute | solution.py:219
  66.2 27.4 %collective-permute-start.26 = (bf16[8,2,128,128]{3,2,1,0:T(8,128)(2,1)S(1)}, bf16[8,2,128,128]{3,2,1,0:T(8,128)(2,1)S(1)}, u32[]{:S(2)}, u32[]{:S(2)}) collective-permute-start(bf16[8,2,128,128]{3,2,1,0:T(8,128)(2,1)S(1)} %collective-permute-done.25.refs_9_), channel_id=1, source_target_pairs={{0,1},{1,0},{2,3},{3,2},{4,5},{5,4},{6,7},{7,6},{8,9},{9,8},{10,11... | collective-permute-start | bytes 1572872 | tf_op jit(solution)/shard_map/ppermute | solution.py:219
  90.1 13.8 %collective-permute-start.10 = (bf16[128,128]{1,0:T(8,128)(2,1)}, bf16[128,128]{1,0:T(8,128)(2,1)S(1)}, u32[]{:S(2)}, u32[]{:S(2)}) collective-permute-start(bf16[128,128]{1,0:T(8,128)(2,1)} %get-tuple-element.50), channel_id=1, source_target_pairs={{0,4},{4,0},{8,12},{12,8},{16,20},{20,16},{24,28},{28,24},{1,5},{5... | collective-permute-start | bytes 98312 | tf_op jit(solution)/shard_map/ppermute | solution.py:219
  90.1 14.6 %collective-permute-start.11 = (bf16[128,128]{1,0:T(8,128)(2,1)}, bf16[128,128]{1,0:T(8,128)(2,1)S(1)}, u32[]{:S(2)}, u32[]{:S(2)}) collective-permute-start(bf16[128,128]{1,0:T(8,128)(2,1)} %get-tuple-element.51), channel_id=1, source_target_pairs={{0,8},{4,12},{8,0},{12,4},{16,24},{20,28},{24,16},{28,20},{1,9},{5... | collective-permute-start | bytes 98312 | tf_op jit(solution)/shard_map/ppermute | solution.py:219
  90.2 18.4 %collective-permute-start.12 = (bf16[128,128]{1,0:T(8,128)(2,1)}, bf16[128,128]{1,0:T(8,128)(2,1)S(1)}, u32[]{:S(2)}, u32[]{:S(2)}) collective-permute-start(bf16[128,128]{1,0:T(8,128)(2,1)} %get-tuple-element.52), channel_id=1, source_target_pairs={{0,12},{4,8},{8,4},{12,0},{16,28},{20,24},{24,20},{28,16},{1,13},{... | collective-permute-start | bytes 98312 | tf_op jit(solution)/shard_map/ppermute | solution.py:219
  93.6 15.7 %collective-permute-start.13 = (bf16[128,128]{1,0:T(8,128)(2,1)}, bf16[128,128]{1,0:T(8,128)(2,1)S(1)}, u32[]{:S(2)}, u32[]{:S(2)}) collective-permute-start(bf16[128,128]{1,0:T(8,128)(2,1)} %get-tuple-element.53), channel_id=1, source_target_pairs={{0,16},{4,20},{8,24},{12,28},{16,0},{20,4},{24,8},{28,12},{1,17},{... | collective-permute-start | bytes 98312 | tf_op jit(solution)/shard_map/ppermute | solution.py:219
  93.7 15.6 %collective-permute-start.14 = (bf16[128,128]{1,0:T(8,128)(2,1)}, bf16[128,128]{1,0:T(8,128)(2,1)S(1)}, u32[]{:S(2)}, u32[]{:S(2)}) collective-permute-start(bf16[128,128]{1,0:T(8,128)(2,1)} %get-tuple-element.54), channel_id=1, source_target_pairs={{0,20},{4,16},{8,28},{12,24},{16,4},{20,0},{24,12},{28,8},{1,21},{... | collective-permute-start | bytes 98312 | tf_op jit(solution)/shard_map/ppermute | solution.py:219
  103.9 8.2 %collective-permute-start.15 = (bf16[128,128]{1,0:T(8,128)(2,1)S(1)}, bf16[128,128]{1,0:T(8,128)(2,1)S(1)}, u32[]{:S(2)}, u32[]{:S(2)}) collective-permute-start(bf16[128,128]{1,0:T(8,128)(2,1)S(1)} %copy-done.48), channel_id=1, source_target_pairs={{0,24},{4,28},{8,16},{12,20},{16,8},{20,12},{24,0},{28,4},{1,25},{... | collective-permute-start | bytes 98312 | tf_op jit(solution)/shard_map/ppermute | solution.py:219
  104.8 7.3 %collective-permute-start.16 = (bf16[128,128]{1,0:T(8,128)(2,1)S(1)}, bf16[128,128]{1,0:T(8,128)(2,1)S(1)}, u32[]{:S(2)}, u32[]{:S(2)}) collective-permute-start(bf16[128,128]{1,0:T(8,128)(2,1)S(1)} %copy-done.47), channel_id=1, source_target_pairs={{0,28},{4,24},{8,20},{12,16},{16,12},{20,8},{24,4},{28,0},{1,29},{... | collective-permute-start | bytes 98312 | tf_op jit(solution)/shard_map/ppermute | solution.py:219
  109.3 6.7 %collective-permute-start.28 = (bf16[128,128]{1,0:T(8,128)(2,1)}, bf16[128,128]{1,0:T(8,128)(2,1)S(1)}, u32[]{:S(2)}, u32[]{:S(2)}) collective-permute-start(bf16[128,128]{1,0:T(8,128)(2,1)} %get-tuple-element.67), channel_id=1, source_target_pairs={{0,8},{4,12},{8,0},{12,4},{16,24},{20,28},{24,16},{28,20},{1,9},{5... | collective-permute-start | bytes 98312 | tf_op jit(solution)/shard_map/ppermute | solution.py:219
  109.3 11.7 %collective-permute-start.29 = (bf16[128,128]{1,0:T(8,128)(2,1)}, bf16[128,128]{1,0:T(8,128)(2,1)S(1)}, u32[]{:S(2)}, u32[]{:S(2)}) collective-permute-start(bf16[128,128]{1,0:T(8,128)(2,1)} %get-tuple-element.68), channel_id=1, source_target_pairs={{0,12},{4,8},{8,4},{12,0},{16,28},{20,24},{24,20},{28,16},{1,13},{... | collective-permute-start | bytes 98312 | tf_op jit(solution)/shard_map/ppermute | solution.py:219
  112.1 8.9 %collective-permute-start.30 = (bf16[128,128]{1,0:T(8,128)(2,1)}, bf16[128,128]{1,0:T(8,128)(2,1)S(1)}, u32[]{:S(2)}, u32[]{:S(2)}) collective-permute-start(bf16[128,128]{1,0:T(8,128)(2,1)} %get-tuple-element.69), channel_id=1, source_target_pairs={{0,16},{4,20},{8,24},{12,28},{16,0},{20,4},{24,8},{28,12},{1,17},{... | collective-permute-start | bytes 98312 | tf_op jit(solution)/shard_map/ppermute | solution.py:219
  112.1 8.9 %collective-permute-start.31 = (bf16[128,128]{1,0:T(8,128)(2,1)}, bf16[128,128]{1,0:T(8,128)(2,1)S(1)}, u32[]{:S(2)}, u32[]{:S(2)}) collective-permute-start(bf16[128,128]{1,0:T(8,128)(2,1)} %get-tuple-element.70), channel_id=1, source_target_pairs={{0,20},{4,16},{8,28},{12,24},{16,4},{20,0},{24,12},{28,8},{1,21},{... | collective-permute-start | bytes 98312 | tf_op jit(solution)/shard_map/ppermute | solution.py:219
  116.0 6.8 %collective-permute-start.33 = (bf16[128,128]{1,0:T(8,128)(2,1)}, bf16[128,128]{1,0:T(8,128)(2,1)S(1)}, u32[]{:S(2)}, u32[]{:S(2)}) collective-permute-start(bf16[128,128]{1,0:T(8,128)(2,1)} %get-tuple-element.72), channel_id=1, source_target_pairs={{0,28},{4,24},{8,20},{12,16},{16,12},{20,8},{24,4},{28,0},{1,29},{... | collective-permute-start | bytes 98312 | tf_op jit(solution)/shard_map/ppermute | solution.py:219
  (51 other events, 336.2 us)

commit v4 on v2

v4 whole, which is shorter than its diff:
```python
import functools

import jax
import jax.numpy as jnp
from jax import lax
from jax.experimental import pallas as pl
from jax.experimental.pallas import tpu as pltpu
from jax.sharding import PartitionSpec as P

H = 32
DH = 64
BLK = 128
KMAX = 32
UNROLL = 4
BIG = 1e30
F32 = jnp.float32
BF16 = jnp.bfloat16
VMEM = pl.BlockSpec(memory_space=pltpu.VMEM)
SMEM = pl.BlockSpec(memory_space=pltpu.SMEM)
PARAMS = pltpu.CompilerParams(vmem_limit_bytes=58 << 20)


def rank_heads(counts_ref, table_ref, groups, me):
    counts = counts_ref[...].astype(BF16)
    blocks = counts.shape[1]
    over = (((1,), (1,)), ((), ()))
    mine = lax.dot_general(counts, jnp.ones((H, blocks), BF16), over, preferred_element_type=F32)
    theirs = lax.dot_general(jnp.ones((H, blocks), BF16), counts, over, preferred_element_type=F32)
    row = lax.broadcasted_iota(jnp.int32, (H, H), 0)
    lane = lax.broadcasted_iota(jnp.int32, (H, H), 1)
    bits = groups.bit_length() - 1

    def place_of(rank, own_group):
        turn, seat = rank >> bits, rank & (groups - 1)
        group = jnp.where((turn & 1) == 0, seat, groups - 1 - seat) ^ own_group
        return (((turn >> 1) * groups + group) << 1) + (turn & 1)

    behind = (theirs > mine) | ((theirs == mine) & (lane < row))
    rank_down = jnp.sum(jnp.where(behind, 1.0, 0.0), axis=1, keepdims=True).astype(jnp.int32)
    ahead = (mine > theirs) | ((theirs == mine) & (row < lane))
    rank_along = jnp.sum(jnp.where(ahead, 1.0, 0.0), axis=0, keepdims=True).astype(jnp.int32)
    here = place_of(jnp.broadcast_to(rank_down, (H, H)), 0) == lane
    head_at = jnp.sum(jnp.where(here, row.astype(F32), 0.0), axis=0, keepdims=True).astype(jnp.int32)
    table_ref[0:1, 0:H] = head_at
    table_ref[1:2, 0:H] = place_of(rank_along, me)


def pack_kernel(groups, counts_ref, q_ref, k_ref, v_ref, table_ref, qt_ref, *refs):
    kv_refs, turned, table_vmem, sem = refs[:-3], refs[-3], refs[-2], refs[-1]
    pairs = qt_ref.shape[1]
    me = lax.axis_index("uly")
    rank_heads(counts_ref, table_vmem, groups, me)
    copy = pltpu.make_async_copy(table_vmem, table_ref, sem)
    copy.start()
    low = lax.broadcasted_iota(jnp.int32, (BLK, 2 * DH), 1) < DH
    for pair in range(H // 2):
        lanes = slice(pair * 2 * DH, (pair + 1) * 2 * DH)
        for which, source in enumerate((q_ref, v_ref)):
            tile = source[:, lanes].T
            turned[which, 2 * pair] = tile[:DH]
            turned[which, 2 * pair + 1] = tile[DH:]
    copy.wait()

    def fetch(head, odd):
        start = pl.multiple_of((head // 2) * (2 * DH), 2 * DH)
        block = k_ref[:, pl.ds(start, 2 * DH)]
        swapped = jnp.concatenate([block[:, DH:], block[:, :DH]], axis=1)
        return jnp.where((head % 2) == odd, block, swapped)

    for step, kv_ref in enumerate(kv_refs):
        group = me ^ step
        for pair in range(pairs):
            place = (pair * groups + group) * 2
            left, right = table_ref[0, place], table_ref[0, place + 1]
            kv_ref[pair, 0] = jnp.where(low, fetch(left, 0), fetch(right, 1))
            kv_ref[pair, 1] = jnp.concatenate([turned[1, left], turned[1, right]], axis=0)
            qt_ref[group, pair] = jnp.concatenate([turned[0, left], turned[0, right]], axis=0)


def join_kernel(*refs):
    *pieces, out_ref = refs[1:]
    for at, piece in enumerate(pieces):
        out_ref[at] = piece[...]


def plan_kernel(groups, slabs, table_ref, counts_ref, layout_ref, unit_ref, total_ref, lay_ref, sem):
    per = H // groups
    group, slab = lax.axis_index("uly"), lax.axis_index("doc")
    rows = per * groups

    def head_of(slot):
        return table_ref[0, ((slot // 2) * groups + group) * 2 + slot % 2]

    copies = [
        pltpu.make_async_copy(layout_ref.at[head_of(slot), pl.ds(slab * groups, groups)], lay_ref.at[slot], sem.at[slot])
        for slot in range(per)
    ]
    for copy in copies:
        copy.start()

    def local(block):
        return block ^ (slab * groups + group)

    def idle(base, many):
        for extra in range(many):
            unit_ref[0, base + extra] = rows
            unit_ref[1, base + extra] = 0
            unit_ref[2, base + extra] = 0
            unit_ref[3, base + extra] = 1

    idle(0, 2 * UNROLL)
    for copy in copies:
        copy.wait()
    base = jnp.int32(2 * UNROLL)
    for slot in range(per):
        head = head_of(slot)

        def place_row(block, base, slot=slot, head=head):
            count = counts_ref[head, slab * groups + block]

            def place_unit(step, _):
                first = lay_ref[slot, block, 2 * step]
                whole = 2 * step + 1 < count
                second = jnp.where(whole, lay_ref[slot, block, jnp.minimum(2 * step + 1, KMAX - 1)], first)
                unit_ref[0, base + step] = slot * groups + block
                unit_ref[1, base + step] = local(first)
                unit_ref[2, base + step] = local(second)
                unit_ref[3, base + step] = whole.astype(jnp.int32)
                return 0

            units = (count + 1) // 2
            lax.fori_loop(0, units, place_unit, 0)
            return base + units

        base = lax.fori_loop(0, groups, place_row, base)
    idle(base, 4 * UNROLL)
    total_ref[0] = base


def attend_kernel(sizes, unit_ref, total_ref, qt_ref, *refs):
    many = sum(size > 0 for size in sizes)
    kv_hbm, o_ref = refs[:many], refs[many]
    kv_ref, qz_ref, m_ref, l_ref, acc_ref, sem = refs[many + 1 : many + 7]
    score, top_of, out_of, sum_of = (refs[many + 7 + 2 * at : many + 9 + 2 * at] for at in range(4))
    slab, pairs = qt_ref.shape[:2]
    rows = 2 * pairs * slab
    start, copies = 0, []
    for at, source in enumerate(kv_hbm):
        copies.append(pltpu.make_async_copy(source, kv_ref.at[pl.ds(start, sizes[at])], sem.at[at]))
        copies[-1].start()
        start += sizes[at]
    zeros = jnp.zeros((DH, BLK), BF16)
    for head in range(2 * pairs):
        for block in range(slab):
            part = qt_ref[block, head // 2, (head % 2) * DH : (head % 2 + 1) * DH, :]
            up = jnp.concatenate([part, zeros], axis=0)
            down = jnp.concatenate([zeros, part], axis=0)
            qz_ref[head * slab + block] = jnp.concatenate([up, down], axis=1)
    qz_ref[rows] = jnp.zeros((2 * DH, 2 * BLK), BF16)
    m_ref[...] = jnp.full(m_ref.shape, -BIG, F32)
    for ref in (l_ref, acc_ref):
        ref[...] = jnp.zeros(ref.shape, F32)
    for copy in copies:
        copy.wait()
    low = lax.broadcasted_iota(jnp.int32, (BLK, 2 * DH), 1) < DH

    def read(unit):
        row = unit_ref[0, unit]
        head = jnp.minimum(row // slab, 2 * pairs - 1)
        return row, head // 2, head % 2, unit_ref[1, unit], unit_ref[2, unit]

    def make_scores(unit, lane, side):
        row, pair, odd, first, second = read(unit)
        plain = kv_ref[jnp.where(odd == 1, second, first), pair, 0]
        other = kv_ref[jnp.where(odd == 1, first, second), pair, 0]
        other = jnp.concatenate([other[:, DH:], other[:, :DH]], axis=1)
        keys = jnp.where(low == (odd == 0), plain, other)
        scores = jnp.dot(keys, qz_ref[row], preferred_element_type=F32)
        score[side][lane] = scores
        top = jnp.max(scores.reshape(BLK // 8, 8, 2 * BLK), axis=0)
        top = jnp.maximum(top[:, :BLK], top[:, BLK:])
        top_of[side][lane] = jnp.broadcast_to(jnp.max(top, axis=0, keepdims=True), (8, BLK))

    def make_output(unit, lane, side):
        _, pair, odd, first, second = read(unit)
        top = top_of[side][lane]
        limit = jnp.where(unit_ref[3, unit] == 1, top, top + BIG)
        scores = score[side][lane]
        left = jnp.exp(scores[:, :BLK].reshape(BLK // 8, 8, BLK) - top[None])
        right = jnp.exp(scores[:, BLK:].reshape(BLK // 8, 8, BLK) - limit[None])
        sum_of[side][lane] = jnp.sum(left, axis=0) + jnp.sum(right, axis=0)
        weights = jnp.concatenate([left.reshape(BLK, BLK), right.reshape(BLK, BLK)], axis=0)
        span = pl.ds(pl.multiple_of(odd * DH, DH), DH)
        values = jnp.concatenate([kv_ref[first, pair, 1, span, :], kv_ref[second, pair, 1, span, :]], axis=1)
        out_of[side][lane] = jnp.dot(values, weights.astype(BF16), preferred_element_type=F32)

    def merge(unit, lane, side):
        row = unit_ref[0, unit]
        top, old = top_of[side][lane], m_ref[row]
        new = jnp.maximum(old, top)
        a, b = jnp.exp(old - new), jnp.exp(top - new)
        m_ref[row] = new
        l_ref[row] = l_ref[row] * a + sum_of[side][lane] * b
        tiles = (DH // 8, 8, BLK)
        acc_ref[row] = (acc_ref[row].reshape(tiles) * a[None] + out_of[side][lane].reshape(tiles) * b[None]).reshape(
            DH, BLK
        )

    def step(index, _):
        for side in range(2):
            chunk = 2 * index + side
            for lane in range(UNROLL):
                merge(chunk * UNROLL + lane, lane, side)
            for lane in range(UNROLL):
                make_scores((chunk + 2) * UNROLL + lane, lane, side)
                make_output((chunk + 1) * UNROLL + lane, lane, 1 - side)
        return 0

    chunks = (total_ref[0] + UNROLL - 1) // UNROLL
    lax.fori_loop(0, (chunks + 1) // 2, step, 0)
    for head in range(2 * pairs):
        for block in range(slab):
            row = head * slab + block
            total_w = jnp.sum(l_ref[row], axis=0, keepdims=True)
            o_ref[block, head // 2, (head % 2) * DH : (head % 2 + 1) * DH, :] = (acc_ref[row] / total_w).astype(BF16)


def unpack_kernel(table_ref, o_ref, out_ref):
    groups = o_ref.shape[0]
    me = lax.axis_index("uly")

    def fetch(head):
        spot = table_ref[1, head]
        span = pl.ds(pl.multiple_of((spot % 2) * DH, DH), DH)
        return o_ref[((spot // 2) % groups) ^ me, spot // (2 * groups), span, :]

    for pair in range(H // 2):
        both = jnp.concatenate([fetch(2 * pair), fetch(2 * pair + 1)], axis=0)
        out_ref[:, pair * 2 * DH : (pair + 1) * 2 * DH] = both.T


def shards(queries, key_vectors, value_vectors, layout, counts):
    groups, slabs = lax.axis_size("uly"), lax.axis_size("doc")
    per = H // groups
    pairs = per // 2
    rows = per * groups
    shape = jax.ShapeDtypeStruct
    piece = (pairs, 2, BLK, BLK)
    table, qt, *pieces = pl.pallas_call(
        functools.partial(pack_kernel, groups),
        out_shape=(shape((8, 128), jnp.int32), shape((groups, pairs, BLK, BLK), BF16)) + (shape(piece, BF16),) * groups,
        in_specs=[VMEM] * 4,
        out_specs=(SMEM, VMEM) + (VMEM,) * groups,
        scratch_shapes=[
            pltpu.VMEM((2, H, DH, BLK), BF16),
            pltpu.VMEM((8, 128), jnp.int32),
            pltpu.SemaphoreType.DMA,
        ],
        compiler_params=PARAMS,
        name="pack",
    )(counts, queries, key_vectors, value_vectors)

    def flip(array, axis, size, bit):
        return lax.ppermute(array, axis, [(at, at ^ bit) for at in range(size)])

    swap = functools.partial(lax.all_to_all, axis_name="uly", split_axis=0, concat_axis=0, tiled=True)
    units, total = pl.pallas_call(
        functools.partial(plan_kernel, groups, slabs),
        out_shape=(shape((4, rows * KMAX // 2 + 8 * UNROLL), jnp.int32), shape((1,), jnp.int32)),
        in_specs=[SMEM, SMEM, VMEM],
        out_specs=(SMEM, SMEM),
        scratch_shapes=[pltpu.SMEM((per, groups, KMAX), jnp.int32), pltpu.SemaphoreType.DMA((per,))],
        compiler_params=PARAMS,
        name="plan",
    )(table, counts, layout)

    pieces = [piece if step == 0 else flip(piece, "uly", groups, step) for step, piece in enumerate(pieces)]
    bounds = [0, groups // 2, 3 * groups // 4, groups]
    parts = []
    for at, (begin, end) in enumerate(zip(bounds, bounds[1:])):
        some = pieces[begin:end]
        joined = pl.pallas_call(
            join_kernel,
            out_shape=shape((len(some),) + piece, BF16),
            in_specs=[SMEM] + [VMEM] * len(some),
            out_specs=VMEM,
            compiler_params=PARAMS,
            name="join",
        )(total if at == 1 else jnp.zeros((1,), jnp.int32), *some)
        if at == 2:
            joined, qt = lax.optimization_barrier((joined, qt))
            qt = swap(qt)
        gathered = {0: joined}
        bit = slabs // 2
        while bit:
            gathered.update({at ^ bit: flip(array, "doc", slabs, bit) for at, array in list(gathered.items())})
            bit //= 2
        parts.append(gathered)
    order = [(at, part) for at in range(slabs) for part in parts]
    sizes = [part[at].shape[0] for at, part in order]
    both = [pltpu.VMEM((UNROLL, BLK, 2 * BLK), F32)] * 2 + [pltpu.VMEM((UNROLL, 8, BLK), F32)] * 2
    both += [pltpu.VMEM((UNROLL, DH, BLK), F32)] * 2 + [pltpu.VMEM((UNROLL, 8, BLK), F32)] * 2
    out = pl.pallas_call(
        functools.partial(attend_kernel, sizes),
        out_shape=shape(qt.shape, BF16),
        in_specs=[SMEM, SMEM, VMEM] + [VMEM] * len(order),
        out_specs=VMEM,
        scratch_shapes=[
            pltpu.VMEM((slabs * groups,) + piece, BF16),
            pltpu.VMEM((rows + 1, 2 * DH, 2 * BLK), BF16),
            pltpu.VMEM((rows + 1, 8, BLK), F32),
            pltpu.VMEM((rows + 1, 8, BLK), F32),
            pltpu.VMEM((rows + 1, DH, BLK), F32),
            pltpu.SemaphoreType.DMA((len(order),)),
            *both,
        ],
        compiler_params=PARAMS,
        cost_estimate=pl.CostEstimate(flops=8 * 10**9, transcendentals=5 * 10**6, bytes_accessed=6 * 10**6),
        name="attend",
    )(units, total, qt, *[part[at] for at, part in order])
    return pl.pallas_call(
        unpack_kernel,
        out_shape=shape(queries.shape, BF16),
        in_specs=[SMEM, VMEM],
        out_specs=VMEM,
        compiler_params=PARAMS,
        name="unpack",
    )(table, swap(out))


def solution(mesh):
    placed = (
        P(("grp", "doc", "uly"), None),
        P(("grp", "doc", "uly"), None),
        P(("grp", "doc", "uly"), None),
        P("grp", None, None),
        P("grp", None),
    )
    return jax.shard_map(
        shards,
        mesh=mesh,
        in_specs=placed,
        out_specs=P(("grp", "doc", "uly"), None),
        check_vma=False,
    )
```

time: 113 us -> 113 us (level)
  blocking collectives: 36.2 us -> 19.8 us
  waiting for transfers between devices: 17 us -> 26.4 us
  starting transfers between devices: 20.3 us -> 27.3 us
  Pallas kernels: 30.3 us -> 35 us
  local copies, waits for them, and re-layouts: 6.55 us -> 3.78 us
  other arithmetic: 1.92 us -> 0 us
    ppermute x6 -> x16, waiting for transfers between devices: 0.34 us -> 26.4 us  [flip(): return lax.ppermute(array, axis, [(at, at ^ bit) for at in range(size)])]
    all_to_all x4 -> x1, waiting for transfers between devices: 16.7 us -> 0.01 us  [shards(): qt = swap(qt)]
    all_to_all x2 -> x1, blocking collectives: 36.2 us -> 19.8 us  [shards(): swap(out)]
    ppermute x6 -> x16, starting transfers between devices: 3.76 us -> 18.7 us  [flip(): return lax.ppermute(array, axis, [(at, at ^ bit) for at in range(size)])]
    all_to_all x4 -> x1, starting transfers between devices: 16.6 us -> 8.57 us  [shards(): qt = swap(qt)]
    pallas_call x4 -> x6, Pallas kernels: 28.2 us -> 32.6 us  [the longest x1 17.1 us: shards(): pl.pallas_call(functools.partial(attend_kernel, sizes), out_shape=shape(q...]
    reduce_sum x3 -> x0, other arithmetic: 1.73 us -> none  [the longest x1 0.89 us: places_of(): load = jnp.sum(counts, axis=1)]
    select_n x2 -> x0, local copies, waits for them, and re-layouts: 1.27 us -> none  [the longest x1 0.66 us: shards(): jnp.take(lax.dynamic_slice_in_dim(layout, own * slab, slab, axis=1), mine...]
  transfers between devices with their start and end apart: 10 -> 17, of which waited for: 3 -> 8; matrix products, arithmetic and copies ran while one was open for 4% -> 0% of each run, Pallas kernels for 22% -> 10%
where the time goes in v4:
time: 113 us; the launch traced here: 112 us
  Pallas kernels  35 us (31%)
  starting transfers between devices  27.3 us (24%)
  waiting for transfers between devices  26.4 us (23%)
  blocking collectives  19.8 us (18%)
  local copies, waits for them, and re-layouts  3.78 us (3%)
    ppermute x16, waiting for transfers between devices, flip(): return lax.ppermute(array, axis, [(at, at ^ bit) for at in range(size)])  26.4 us
    all_to_all x1, blocking collectives, shards(): swap(out)  19.8 us
    ppermute x16, starting transfers between devices, flip(): return lax.ppermute(array, axis, [(at, at ^ bit) for at in range(size)])  18.7 us
    pallas_call x1, Pallas kernels, shards(): pl.pallas_call(functools.partial(attend_kernel, sizes), out_shape=shape(q...  17.1 us
    all_to_all x1, starting transfers between devices, shards(): qt = swap(qt)  8.57 us
    pallas_call x3, Pallas kernels, shards(): pl.pallas_call(join_kernel, out_shape=shape((len(some),) + piece, BF16),...  6.03 us
    pallas_call x1, Pallas kernels, shards(): pl.pallas_call(functools.partial(plan_kernel, groups, slabs), out_shape=(...  5.56 us
    pallas_call x1, Pallas kernels, shards(): pl.pallas_call(functools.partial(pack_kernel, groups), out_shape=(shape((...  3.99 us
  transfers between devices with their start and end apart: 17, of which 8 were waited for; matrix products, arithmetic and copies ran while one was open for 0% of the time, Pallas kernels for 10%

profile of v4, /device:TPU:0, one launch (start us, length us, event | category | flops | bytes accessed | tf_op | source)
XLA Modules:
  0.0 112.4 jit_solution(6848916328606158583)
XLA Ops:
  0.0 4.0 %pack.1 = (s32[8,128]{1,0:T(8,128)}, bf16[8,2,128,128]{3,2,1,0:T(8,128)(2,1)}, bf16[2,2,128,128]{3,2,1,0:T(8,128)(2,1)}, bf16[2,2,128,128]{3,2,1,0:T(8,128)(2,1)...) custom-call(s32[32,32]{1,0:T(8,128)} %counts_ref.3, ...), custom_call_target="tpu_custom_call" | custom-call | tf_op jit(solution)/shard_map/pack/pallas_call | solution.py:249
  4.0 3.0 %collective-permute-start.2 = (bf16[2,2,128,128]{3,2,1,0:T(8,128)(2,1)}, bf16[2,2,128,128]{3,2,1,0:T(8,128)(2,1)S(1)}, u32[]{:S(2)}, u32[]{:S(2)}) collective-permute-start(bf16[2,2,128,128]{3,2,1,0:T(8,128)(2,1)} %get-tuple-element.27), channel_id=1, source_target_pairs={{0,4},{4,0},{8,12},{12,8},{16,20},{20,16},{24,28},{28,24},{1,5},{5... | collective-permute-start | bytes 393224 | tf_op jit(solution)/shard_map/ppermute | solution.py:264
  7.0 1.6 %collective-permute-start.3 = (bf16[2,2,128,128]{3,2,1,0:T(8,128)(2,1)}, bf16[2,2,128,128]{3,2,1,0:T(8,128)(2,1)S(1)}, u32[]{:S(2)}, u32[]{:S(2)}) collective-permute-start(bf16[2,2,128,128]{3,2,1,0:T(8,128)(2,1)} %get-tuple-element.28), channel_id=1, source_target_pairs={{0,8},{4,12},{8,0},{12,4},{16,24},{20,28},{24,16},{28,20},{1,9},{5... | collective-permute-start | bytes 393224 | tf_op jit(solution)/shard_map/ppermute | solution.py:264
  8.6 4.0 %collective-permute-start = (bf16[2,2,128,128]{3,2,1,0:T(8,128)(2,1)}, bf16[2,2,128,128]{3,2,1,0:T(8,128)(2,1)S(1)}, u32[]{:S(2)}, u32[]{:S(2)}) collective-permute-start(bf16[2,2,128,128]{3,2,1,0:T(8,128)(2,1)} %get-tuple-element.22), channel_id=1, source_target_pairs={{0,24},{4,28},{8,16},{12,20},{16,8},{20,12},{24,0},{28,4},{1,25},{... | collective-permute-start | bytes 393224 | tf_op jit(solution)/shard_map/ppermute | solution.py:264
  12.6 1.2 %collective-permute-start.1 = (bf16[2,2,128,128]{3,2,1,0:T(8,128)(2,1)}, bf16[2,2,128,128]{3,2,1,0:T(8,128)(2,1)S(1)}, u32[]{:S(2)}, u32[]{:S(2)}) collective-permute-start(bf16[2,2,128,128]{3,2,1,0:T(8,128)(2,1)} %get-tuple-element.23), channel_id=1, source_target_pairs={{0,28},{4,24},{8,20},{12,16},{16,12},{20,8},{24,4},{28,0},{1,29},{... | collective-permute-start | bytes 393224 | tf_op jit(solution)/shard_map/ppermute | solution.py:264
  13.8 1.9 %collective-permute-done.4.refs_4_ = bf16[2,2,128,128]{3,2,1,0:T(8,128)(2,1)S(1)} collective-permute-done((bf16[2,2,128,128]{3,2,1,0:T(8,128)(2,1)}, bf16[2,2,128,128]{3,2,1,0:T(8,128)(2,1)S(1)}, u32[]{:S(2)}, u32[]{:S(2)}) %collective-permute-start.4) | collective-permute-done | bytes 131104 | tf_op jit(solution)/shard_map/ppermute | solution.py:264
  15.7 0.7 copy-done.9
  16.3 1.9 %join.4.refs_0_ = bf16[4,2,2,128,128]{4,3,2,1,0:T(8,128)(2,1)} custom-call(s32[1]{0:T(128)} %constant.0.clone.1.refs_0_, bf16[2,2,128,128]{3,2,1,0:T(8,128)(2,1)} %get-tuple-element.26.refs_1_, bf16[2,2,128,128]{3,2,1,0:T(8,128)(2,1)} %copy-done.7, bf16[2,2,128,128]{3,2,1,0:T(8,128)(2,1)} %copy-done.8, bf16[2,2,128,128]{3,2,1,0:T(8,128)(2,1)} %copy-done.9), custom_call_target="tpu_custom_call" | custom-call | tf_op jit(solution)/shard_map/join/pallas_call | solution.py:282
  18.3 1.5 %collective-permute-start.10 = (bf16[4,2,2,128,128]{4,3,2,1,0:T(8,128)(2,1)}, bf16[4,2,2,128,128]{4,3,2,1,0:T(8,128)(2,1)S(1)}, u32[]{:S(2)}, u32[]{:S(2)}) collective-permute-start(bf16[4,2,2,128,128]{4,3,2,1,0:T(8,128)(2,1)} %join.4.refs_0_), channel_id=1, source_target_pairs={{0,2},{1,3},{2,0},{3,1},{4,6},{5,7},{6,4},{7,5},{8,10},{9,11},{10,... | collective-permute-start | bytes 1572872 | tf_op jit(solution)/shard_map/ppermute | solution.py:264
  19.8 1.6 %collective-permute-done.refs_1_ = bf16[2,2,128,128]{3,2,1,0:T(8,128)(2,1)S(1)} collective-permute-done((bf16[2,2,128,128]{3,2,1,0:T(8,128)(2,1)}, bf16[2,2,128,128]{3,2,1,0:T(8,128)(2,1)S(1)}, u32[]{:S(2)}, u32[]{:S(2)}) %collective-permute-start) | collective-permute-done | bytes 131104 | tf_op jit(solution)/shard_map/ppermute | solution.py:264
  21.3 1.4 %collective-permute-done.1.refs_2_ = bf16[2,2,128,128]{3,2,1,0:T(8,128)(2,1)S(1)} collective-permute-done((bf16[2,2,128,128]{3,2,1,0:T(8,128)(2,1)}, bf16[2,2,128,128]{3,2,1,0:T(8,128)(2,1)S(1)}, u32[]{:S(2)}, u32[]{:S(2)}) %collective-permute-start.1) | collective-permute-done | bytes 131104 | tf_op jit(solution)/shard_map/ppermute | solution.py:264
  22.7 0.7 copy-done.4
  23.4 1.7 %join.3.refs_2_ = bf16[2,2,2,128,128]{4,3,2,1,0:T(8,128)(2,1)} custom-call(s32[1]{0:T(128)} %constant.0.clone.1.refs_0_, bf16[2,2,128,128]{3,2,1,0:T(8,128)(2,1)} %copy-done.3, bf16[2,2,128,128]{3,2,1,0:T(8,128)(2,1)} %copy-done.4), custom_call_target="tpu_custom_call" | custom-call | tf_op jit(solution)/shard_map/join/pallas_call | solution.py:282
  25.1 8.6 %all-to-all-start = ((bf16[8,2,128,128]{3,2,1,0:T(8,128)(2,1)}), bf16[8,2,128,128]{3,2,1,0:T(8,128)(2,1)S(1)}, u32[]{:S(2)}, u32[]{:S(2)}) async-start(bf16[8,2,128,128]{3,2,1,0:T(8,128)(2,1)} %get-tuple-element.25), calls=%async_computation | async-start | bytes 1048576 | tf_op jit(solution)/shard_map/all_to_all | solution.py:292
  33.6 2.9 %collective-permute-start.5 = (bf16[2,2,128,128]{3,2,1,0:T(8,128)(2,1)S(1)}, bf16[2,2,128,128]{3,2,1,0:T(8,128)(2,1)S(1)}, u32[]{:S(2)}, u32[]{:S(2)}) collective-permute-start(bf16[2,2,128,128]{3,2,1,0:T(8,128)(2,1)S(1)} %copy-done.20), channel_id=1, source_target_pairs={{0,16},{4,20},{8,24},{12,28},{16,0},{20,4},{24,8},{28,12},{1,17},{... | collective-permute-start | bytes 393224 | tf_op jit(solution)/shard_map/ppermute | solution.py:264
  36.6 1.5 %collective-permute-start.6 = (bf16[2,2,128,128]{3,2,1,0:T(8,128)(2,1)S(1)}, bf16[2,2,128,128]{3,2,1,0:T(8,128)(2,1)S(1)}, u32[]{:S(2)}, u32[]{:S(2)}) collective-permute-start(bf16[2,2,128,128]{3,2,1,0:T(8,128)(2,1)S(1)} %copy-done.19), channel_id=1, source_target_pairs={{0,20},{4,16},{8,28},{12,24},{16,4},{20,0},{24,12},{28,8},{1,21},{... | collective-permute-start | bytes 393224 | tf_op jit(solution)/shard_map/ppermute | solution.py:264
  38.0 5.6 %plan.1 = (s32[4,544]{1,0:T(4,128)}, s32[1]{0:T(128)}) custom-call(s32[8,128]{1,0:T(8,128)} %get-tuple-element.19.table_ref, s32[32,32]{1,0:T(8,128)} %counts_ref.3, s32[32,32,32]{2,1,0:T(8,128)} %layout_ref.1), custom_call_target="tpu_custom_call" | custom-call | tf_op jit(solution)/shard_map/plan/pallas_call | solution.py:267
  43.6 9.1 %collective-permute-done.5.refs_1_ = bf16[2,2,128,128]{3,2,1,0:T(8,128)(2,1)S(1)} collective-permute-done((bf16[2,2,128,128]{3,2,1,0:T(8,128)(2,1)S(1)}, bf16[2,2,128,128]{3,2,1,0:T(8,128)(2,1)S(1)}, u32[]{:S(2)}, u32[]{:S(2)}) %collective-permute-start.5) | collective-permute-done | bytes 131104 | tf_op jit(solution)/shard_map/ppermute | solution.py:264
  52.7 1.9 %collective-permute-done.6.refs_2_ = bf16[2,2,128,128]{3,2,1,0:T(8,128)(2,1)S(1)} collective-permute-done((bf16[2,2,128,128]{3,2,1,0:T(8,128)(2,1)S(1)}, bf16[2,2,128,128]{3,2,1,0:T(8,128)(2,1)S(1)}, u32[]{:S(2)}, u32[]{:S(2)}) %collective-permute-start.6) | collective-permute-done | bytes 131104 | tf_op jit(solution)/shard_map/ppermute | solution.py:264
  54.6 0.7 copy-done.6
  55.2 2.4 %join.5.refs_1_ = bf16[2,2,2,128,128]{4,3,2,1,0:T(8,128)(2,1)} custom-call(s32[1]{0:T(128)} %get-tuple-element.21.refs_0_.total_ref, bf16[2,2,128,128]{3,2,1,0:T(8,128)(2,1)} %copy-done.5, bf16[2,2,128,128]{3,2,1,0:T(8,128)(2,1)} %copy-done.6), custom_call_target="tpu_custom_call" | custom-call | tf_op jit(solution)/shard_map/join/pallas_call | solution.py:282
  57.6 1.5 %collective-permute-start.11 = (bf16[2,2,2,128,128]{4,3,2,1,0:T(8,128)(2,1)}, bf16[2,2,2,128,128]{4,3,2,1,0:T(8,128)(2,1)S(1)}, u32[]{:S(2)}, u32[]{:S(2)}) collective-permute-start(bf16[2,2,2,128,128]{4,3,2,1,0:T(8,128)(2,1)} %join.5.refs_1_), channel_id=1, source_target_pairs={{0,2},{1,3},{2,0},{3,1},{4,6},{5,7},{6,4},{7,5},{8,10},{9,11},{10,... | collective-permute-start | bytes 786440 | tf_op jit(solution)/shard_map/ppermute | solution.py:264
  59.1 0.5 collective-permute-start.12
  60.2 6.0 %collective-permute-done.11.refs_7_ = bf16[2,2,2,128,128]{4,3,2,1,0:T(8,128)(2,1)S(1)} collective-permute-done((bf16[2,2,2,128,128]{4,3,2,1,0:T(8,128)(2,1)}, bf16[2,2,2,128,128]{4,3,2,1,0:T(8,128)(2,1)S(1)}, u32[]{:S(2)}, u32[]{:S(2)}) %collective-permute-start.11) | collective-permute-done | bytes 262176 | tf_op jit(solution)/shard_map/ppermute | solution.py:264
  66.2 0.5 collective-permute-start.14
  66.7 3.1 %collective-permute-done.12.refs_8_ = bf16[2,2,2,128,128]{4,3,2,1,0:T(8,128)(2,1)S(1)} collective-permute-done((bf16[2,2,2,128,128]{4,3,2,1,0:T(8,128)(2,1)S(1)}, bf16[2,2,2,128,128]{4,3,2,1,0:T(8,128)(2,1)S(1)}, u32[]{:S(2)}, u32[]{:S(2)}) %collective-permute-start.12) | collective-permute-done | bytes 262176 | tf_op jit(solution)/shard_map/ppermute | solution.py:264
  69.9 1.5 %collective-permute-done.15.refs_11_ = bf16[2,2,2,128,128]{4,3,2,1,0:T(8,128)(2,1)S(1)} collective-permute-done((bf16[2,2,2,128,128]{4,3,2,1,0:T(8,128)(2,1)S(1)}, bf16[2,2,2,128,128]{4,3,2,1,0:T(8,128)(2,1)S(1)}, u32[]{:S(2)}, u32[]{:S(2)}) %collective-permute-start.15) | collective-permute-done | bytes 262176 | tf_op jit(solution)/shard_map/ppermute | solution.py:264
  71.4 0.7 copy-done.18
  72.2 0.7 copy-done.11
  73.2 17.1 %attend.1 = bf16[8,2,128,128]{3,2,1,0:T(8,128)(2,1)} custom-call(s32[4,544]{1,0:T(4,128)} %get-tuple-element.20.unit_ref, s32[1]{0:T(128)} %get-tuple-element.21.refs_0_.total_ref, bf16[8,2,128,128]{3,2,1,0:T(8,128)(2,1)} %copy-done, bf16[4,2,2,128,128]{4,3,2,1,0:T(8,128)(2,1)} %join.4.refs_0_, bf16[2,2,2,128,128]{4,3,2,1,0:T(8,128)(2,1)} %join.5.refs_1_, ...), custom_call_target="tpu_custom_call" | custom-call | flops 8000000000 | bytes 6000000 | tf_op jit(solution)/shard_map/attend/pallas_call | solution.py:303
  90.3 19.8 %all_to_all.10.o_ref = bf16[8,2,128,128]{3,2,1,0:T(8,128)(2,1)} all-to-all(bf16[8,2,128,128]{3,2,1,0:T(8,128)(2,1)} %attend.1), channel_id=1, replica_groups=mesh['grp'=1,'uly'=8,'doc'=4] {'uly'}, dimensions={0} | all-to-all | bytes 1048576 | tf_op jit(solution)/shard_map/all_to_all | solution.py:328
  110.1 2.3 %unpack.1 = bf16[128,2048]{1,0:T(8,128)(2,1)} custom-call(s32[8,128]{1,0:T(8,128)} %get-tuple-element.19.table_ref, bf16[8,2,128,128]{3,2,1,0:T(8,128)(2,1)} %all_to_all.10.o_ref), custom_call_target="tpu_custom_call" | custom-call | tf_op jit(solution)/shard_map/unpack/pallas_call | solution.py:321
  (52 shorter events, 1.0 us)
Async XLA Ops:
  4.0 9.8 %collective-permute-start.2 = (bf16[2,2,128,128]{3,2,1,0:T(8,128)(2,1)}, bf16[2,2,128,128]{3,2,1,0:T(8,128)(2,1)S(1)}, u32[]{:S(2)}, u32[]{:S(2)}) collective-permute-start(bf16[2,2,128,128]{3,2,1,0:T(8,128)(2,1)} %get-tuple-element.27), channel_id=1, source_target_pairs={{0,4},{4,0},{8,12},{12,8},{16,20},{20,16},{24,28},{28,24},{1,5},{5... | collective-permute-start | bytes 393224 | tf_op jit(solution)/shard_map/ppermute | solution.py:264
  7.0 6.8 %collective-permute-start.3 = (bf16[2,2,128,128]{3,2,1,0:T(8,128)(2,1)}, bf16[2,2,128,128]{3,2,1,0:T(8,128)(2,1)S(1)}, u32[]{:S(2)}, u32[]{:S(2)}) collective-permute-start(bf16[2,2,128,128]{3,2,1,0:T(8,128)(2,1)} %get-tuple-element.28), channel_id=1, source_target_pairs={{0,8},{4,12},{8,0},{12,4},{16,24},{20,28},{24,16},{28,20},{1,9},{5... | collective-permute-start | bytes 393224 | tf_op jit(solution)/shard_map/ppermute | solution.py:264
  8.6 7.1 %collective-permute-start.4 = (bf16[2,2,128,128]{3,2,1,0:T(8,128)(2,1)}, bf16[2,2,128,128]{3,2,1,0:T(8,128)(2,1)S(1)}, u32[]{:S(2)}, u32[]{:S(2)}) collective-permute-start(bf16[2,2,128,128]{3,2,1,0:T(8,128)(2,1)} %get-tuple-element.29), channel_id=1, source_target_pairs={{0,12},{4,8},{8,4},{12,0},{16,28},{20,24},{24,20},{28,16},{1,13},{... | collective-permute-start | bytes 393224 | tf_op jit(solution)/shard_map/ppermute | solution.py:264
  8.6 12.7 %collective-permute-start = (bf16[2,2,128,128]{3,2,1,0:T(8,128)(2,1)}, bf16[2,2,128,128]{3,2,1,0:T(8,128)(2,1)S(1)}, u32[]{:S(2)}, u32[]{:S(2)}) collective-permute-start(bf16[2,2,128,128]{3,2,1,0:T(8,128)(2,1)} %get-tuple-element.22), channel_id=1, source_target_pairs={{0,24},{4,28},{8,16},{12,20},{16,8},{20,12},{24,0},{28,4},{1,25},{... | collective-permute-start | bytes 393224 | tf_op jit(solution)/shard_map/ppermute | solution.py:264
  12.6 10.1 %collective-permute-start.1 = (bf16[2,2,128,128]{3,2,1,0:T(8,128)(2,1)}, bf16[2,2,128,128]{3,2,1,0:T(8,128)(2,1)S(1)}, u32[]{:S(2)}, u32[]{:S(2)}) collective-permute-start(bf16[2,2,128,128]{3,2,1,0:T(8,128)(2,1)} %get-tuple-element.23), channel_id=1, source_target_pairs={{0,28},{4,24},{8,20},{12,16},{16,12},{20,8},{24,4},{28,0},{1,29},{... | collective-permute-start | bytes 393224 | tf_op jit(solution)/shard_map/ppermute | solution.py:264
  13.8 1.9 %copy-start.7 = (bf16[2,2,128,128]{3,2,1,0:T(8,128)(2,1)}, bf16[2,2,128,128]{3,2,1,0:T(8,128)(2,1)S(1)}, u32[]{:S(2)}) copy-start(bf16[2,2,128,128]{3,2,1,0:T(8,128)(2,1)S(1)} %collective-permute-done.2.refs_2_) | copy-start | bytes 393220
  13.8 1.9 %copy-start.8 = (bf16[2,2,128,128]{3,2,1,0:T(8,128)(2,1)}, bf16[2,2,128,128]{3,2,1,0:T(8,128)(2,1)S(1)}, u32[]{:S(2)}) copy-start(bf16[2,2,128,128]{3,2,1,0:T(8,128)(2,1)S(1)} %collective-permute-done.3.refs_3_) | copy-start | bytes 393220
  18.3 41.6 %collective-permute-start.10 = (bf16[4,2,2,128,128]{4,3,2,1,0:T(8,128)(2,1)}, bf16[4,2,2,128,128]{4,3,2,1,0:T(8,128)(2,1)S(1)}, u32[]{:S(2)}, u32[]{:S(2)}) collective-permute-start(bf16[4,2,2,128,128]{4,3,2,1,0:T(8,128)(2,1)} %join.4.refs_0_), channel_id=1, source_target_pairs={{0,2},{1,3},{2,0},{3,1},{4,6},{5,7},{6,4},{7,5},{8,10},{9,11},{10,... | collective-permute-start | bytes 1572872 | tf_op jit(solution)/shard_map/ppermute | solution.py:264
  21.3 1.4 %copy-start.3 = (bf16[2,2,128,128]{3,2,1,0:T(8,128)(2,1)}, bf16[2,2,128,128]{3,2,1,0:T(8,128)(2,1)S(1)}, u32[]{:S(2)}) copy-start(bf16[2,2,128,128]{3,2,1,0:T(8,128)(2,1)S(1)} %collective-permute-done.refs_1_) | copy-start | bytes 393220
  25.1 8.6 %copy-start.20 = (bf16[2,2,128,128]{3,2,1,0:T(8,128)(2,1)S(1)}, bf16[2,2,128,128]{3,2,1,0:T(8,128)(2,1)}, u32[]{:S(2)}) copy-start(bf16[2,2,128,128]{3,2,1,0:T(8,128)(2,1)} %get-tuple-element.30) | copy-start | bytes 393220
  25.1 11.5 %copy-start.19 = (bf16[2,2,128,128]{3,2,1,0:T(8,128)(2,1)S(1)}, bf16[2,2,128,128]{3,2,1,0:T(8,128)(2,1)}, u32[]{:S(2)}) copy-start(bf16[2,2,128,128]{3,2,1,0:T(8,128)(2,1)} %get-tuple-element.31) | copy-start | bytes 393220
  25.1 47.0 %all-to-all-start = ((bf16[8,2,128,128]{3,2,1,0:T(8,128)(2,1)}), bf16[8,2,128,128]{3,2,1,0:T(8,128)(2,1)S(1)}, u32[]{:S(2)}, u32[]{:S(2)}) async-start(bf16[8,2,128,128]{3,2,1,0:T(8,128)(2,1)} %get-tuple-element.25), calls=%async_computation | async-start | bytes 1048576 | tf_op jit(solution)/shard_map/all_to_all | solution.py:292
  33.6 19.0 %collective-permute-start.5 = (bf16[2,2,128,128]{3,2,1,0:T(8,128)(2,1)S(1)}, bf16[2,2,128,128]{3,2,1,0:T(8,128)(2,1)S(1)}, u32[]{:S(2)}, u32[]{:S(2)}) collective-permute-start(bf16[2,2,128,128]{3,2,1,0:T(8,128)(2,1)S(1)} %copy-done.20), channel_id=1, source_target_pairs={{0,16},{4,20},{8,24},{12,28},{16,0},{20,4},{24,8},{28,12},{1,17},{... | collective-permute-start | bytes 393224 | tf_op jit(solution)/shard_map/ppermute | solution.py:264
  36.6 18.0 %collective-permute-start.6 = (bf16[2,2,128,128]{3,2,1,0:T(8,128)(2,1)S(1)}, bf16[2,2,128,128]{3,2,1,0:T(8,128)(2,1)S(1)}, u32[]{:S(2)}, u32[]{:S(2)}) collective-permute-start(bf16[2,2,128,128]{3,2,1,0:T(8,128)(2,1)S(1)} %copy-done.19), channel_id=1, source_target_pairs={{0,20},{4,16},{8,28},{12,24},{16,4},{20,0},{24,12},{28,8},{1,21},{... | collective-permute-start | bytes 393224 | tf_op jit(solution)/shard_map/ppermute | solution.py:264
  38.0 21.6 %copy-start.1 = (bf16[4,2,2,128,128]{4,3,2,1,0:T(8,128)(2,1)S(1)}, bf16[4,2,2,128,128]{4,3,2,1,0:T(8,128)(2,1)}, u32[]{:S(2)}) copy-start(bf16[4,2,2,128,128]{4,3,2,1,0:T(8,128)(2,1)} %join.4.refs_0_) | copy-start | bytes 1572868
  52.6 1.9 %copy-start.5 = (bf16[2,2,128,128]{3,2,1,0:T(8,128)(2,1)}, bf16[2,2,128,128]{3,2,1,0:T(8,128)(2,1)S(1)}, u32[]{:S(2)}) copy-start(bf16[2,2,128,128]{3,2,1,0:T(8,128)(2,1)S(1)} %collective-permute-done.5.refs_1_) | copy-start | bytes 393220
  55.2 3.9 %copy-start.2 = (bf16[2,2,2,128,128]{4,3,2,1,0:T(8,128)(2,1)S(1)}, bf16[2,2,2,128,128]{4,3,2,1,0:T(8,128)(2,1)}, u32[]{:S(2)}) copy-start(bf16[2,2,2,128,128]{4,3,2,1,0:T(8,128)(2,1)} %join.3.refs_2_) | copy-start | bytes 786436
  57.6 8.6 %collective-permute-start.11 = (bf16[2,2,2,128,128]{4,3,2,1,0:T(8,128)(2,1)}, bf16[2,2,2,128,128]{4,3,2,1,0:T(8,128)(2,1)S(1)}, u32[]{:S(2)}, u32[]{:S(2)}) collective-permute-start(bf16[2,2,2,128,128]{4,3,2,1,0:T(8,128)(2,1)} %join.5.refs_1_), channel_id=1, source_target_pairs={{0,2},{1,3},{2,0},{3,1},{4,6},{5,7},{6,4},{7,5},{8,10},{9,11},{10,... | collective-permute-start | bytes 786440 | tf_op jit(solution)/shard_map/ppermute | solution.py:264
  59.1 7.1 %collective-permute-start.8 = (bf16[2,2,2,128,128]{4,3,2,1,0:T(8,128)(2,1)}, bf16[2,2,2,128,128]{4,3,2,1,0:T(8,128)(2,1)S(1)}, u32[]{:S(2)}, u32[]{:S(2)}) collective-permute-start(bf16[2,2,2,128,128]{4,3,2,1,0:T(8,128)(2,1)} %join.5.refs_1_), channel_id=1, source_target_pairs={{0,1},{1,0},{2,3},{3,2},{4,5},{5,4},{6,7},{7,6},{8,9},{9,8},{10,11... | collective-permute-start | bytes 786440 | tf_op jit(solution)/shard_map/ppermute | solution.py:264
  59.1 10.7 %collective-permute-start.12 = (bf16[2,2,2,128,128]{4,3,2,1,0:T(8,128)(2,1)S(1)}, bf16[2,2,2,128,128]{4,3,2,1,0:T(8,128)(2,1)S(1)}, u32[]{:S(2)}, u32[]{:S(2)}) collective-permute-start(bf16[2,2,2,128,128]{4,3,2,1,0:T(8,128)(2,1)S(1)} %copy-done.2), channel_id=1, source_target_pairs={{0,2},{1,3},{2,0},{3,1},{4,6},{5,7},{6,4},{7,5},{8,10},{9,11},{10,... | collective-permute-start | bytes 786440 | tf_op jit(solution)/shard_map/ppermute | solution.py:264
  59.7 12.4 %collective-permute-start.7 = (bf16[4,2,2,128,128]{4,3,2,1,0:T(8,128)(2,1)S(1)}, bf16[4,2,2,128,128]{4,3,2,1,0:T(8,128)(2,1)S(1)}, u32[]{:S(2)}, u32[]{:S(2)}) collective-permute-start(bf16[4,2,2,128,128]{4,3,2,1,0:T(8,128)(2,1)S(1)} %copy-done.1), channel_id=1, source_target_pairs={{0,1},{1,0},{2,3},{3,2},{4,5},{5,4},{6,7},{7,6},{8,9},{9,8},{10,11... | collective-permute-start | bytes 1572872 | tf_op jit(solution)/shard_map/ppermute | solution.py:264
  59.9 12.2 %copy-start.10 = (bf16[4,2,2,128,128]{4,3,2,1,0:T(8,128)(2,1)}, bf16[4,2,2,128,128]{4,3,2,1,0:T(8,128)(2,1)S(1)}, u32[]{:S(2)}) copy-start(bf16[4,2,2,128,128]{4,3,2,1,0:T(8,128)(2,1)S(1)} %collective-permute-done.10.refs_6_) | copy-start | bytes 1572868
  59.9 12.2 %collective-permute-start.13 = (bf16[4,2,2,128,128]{4,3,2,1,0:T(8,128)(2,1)S(1)}, bf16[4,2,2,128,128]{4,3,2,1,0:T(8,128)(2,1)S(1)}, u32[]{:S(2)}, u32[]{:S(2)}) collective-permute-start(bf16[4,2,2,128,128]{4,3,2,1,0:T(8,128)(2,1)S(1)} %collective-permute-done.10.refs_6_), channel_id=1, source_target_pairs={{0,1},{1,0},{2,3},{3,2},{4,5},{5,4},{6,7},{7,6},{8,9},{9,8},{10,11... | collective-permute-start | bytes 1572872 | tf_op jit(solution)/shard_map/ppermute | solution.py:264
  66.2 5.9 %copy-start.13 = (bf16[2,2,2,128,128]{4,3,2,1,0:T(8,128)(2,1)}, bf16[2,2,2,128,128]{4,3,2,1,0:T(8,128)(2,1)S(1)}, u32[]{:S(2)}) copy-start(bf16[2,2,2,128,128]{4,3,2,1,0:T(8,128)(2,1)S(1)} %collective-permute-done.11.refs_7_) | copy-start | bytes 786436
  66.2 3.6 %collective-permute-start.9 = (bf16[2,2,2,128,128]{4,3,2,1,0:T(8,128)(2,1)S(1)}, bf16[2,2,2,128,128]{4,3,2,1,0:T(8,128)(2,1)S(1)}, u32[]{:S(2)}, u32[]{:S(2)}) collective-permute-start(bf16[2,2,2,128,128]{4,3,2,1,0:T(8,128)(2,1)S(1)} %copy-done.2), channel_id=1, source_target_pairs={{0,1},{1,0},{2,3},{3,2},{4,5},{5,4},{6,7},{7,6},{8,9},{9,8},{10,11... | collective-permute-start | bytes 786440 | tf_op jit(solution)/shard_map/ppermute | solution.py:264
  66.2 5.9 %copy-start.14 = (bf16[2,2,2,128,128]{4,3,2,1,0:T(8,128)(2,1)}, bf16[2,2,2,128,128]{4,3,2,1,0:T(8,128)(2,1)S(1)}, u32[]{:S(2)}) copy-start(bf16[2,2,2,128,128]{4,3,2,1,0:T(8,128)(2,1)S(1)} %collective-permute-done.8.refs_4_) | copy-start | bytes 786436
  66.2 3.6 %collective-permute-start.14 = (bf16[2,2,2,128,128]{4,3,2,1,0:T(8,128)(2,1)S(1)}, bf16[2,2,2,128,128]{4,3,2,1,0:T(8,128)(2,1)S(1)}, u32[]{:S(2)}, u32[]{:S(2)}) collective-permute-start(bf16[2,2,2,128,128]{4,3,2,1,0:T(8,128)(2,1)S(1)} %collective-permute-done.11.refs_7_), channel_id=1, source_target_pairs={{0,1},{1,0},{2,3},{3,2},{4,5},{5,4},{6,7},{7,6},{8,9},{9,8},{10,11... | collective-permute-start | bytes 786440 | tf_op jit(solution)/shard_map/ppermute | solution.py:264
  69.8 2.3 %copy-start.15 = (bf16[2,2,2,128,128]{4,3,2,1,0:T(8,128)(2,1)}, bf16[2,2,2,128,128]{4,3,2,1,0:T(8,128)(2,1)S(1)}, u32[]{:S(2)}) copy-start(bf16[2,2,2,128,128]{4,3,2,1,0:T(8,128)(2,1)S(1)} %collective-permute-done.12.refs_8_) | copy-start | bytes 786436
  69.8 1.5 %collective-permute-start.15 = (bf16[2,2,2,128,128]{4,3,2,1,0:T(8,128)(2,1)S(1)}, bf16[2,2,2,128,128]{4,3,2,1,0:T(8,128)(2,1)S(1)}, u32[]{:S(2)}, u32[]{:S(2)}) collective-permute-start(bf16[2,2,2,128,128]{4,3,2,1,0:T(8,128)(2,1)S(1)} %collective-permute-done.12.refs_8_), channel_id=1, source_target_pairs={{0,1},{1,0},{2,3},{3,2},{4,5},{5,4},{6,7},{7,6},{8,9},{9,8},{10,11... | collective-permute-start | bytes 786440 | tf_op jit(solution)/shard_map/ppermute | solution.py:264
  69.8 2.3 %copy-start.16 = (bf16[2,2,2,128,128]{4,3,2,1,0:T(8,128)(2,1)}, bf16[2,2,2,128,128]{4,3,2,1,0:T(8,128)(2,1)S(1)}, u32[]{:S(2)}) copy-start(bf16[2,2,2,128,128]{4,3,2,1,0:T(8,128)(2,1)S(1)} %collective-permute-done.9.refs_5_) | copy-start | bytes 786436
  69.9 2.3 %copy-start.17 = (bf16[2,2,2,128,128]{4,3,2,1,0:T(8,128)(2,1)}, bf16[2,2,2,128,128]{4,3,2,1,0:T(8,128)(2,1)S(1)}, u32[]{:S(2)}) copy-start(bf16[2,2,2,128,128]{4,3,2,1,0:T(8,128)(2,1)S(1)} %collective-permute-done.14.refs_10_) | copy-start | bytes 786436
  72.1 1.1 copy-start.12
  (6 other events, 4.4 us)

commit v5 on v0

v5 whole, which is shorter than its diff:
```python
import functools

import jax
import jax.numpy as jnp
from jax import lax
from jax.experimental import pallas as pl
from jax.experimental.pallas import tpu as pltpu
from jax.sharding import PartitionSpec as P

H = 32
DH = 64
BLK = 128
KMAX = 32
UNROLL = 4
BIG = 1e30
F32 = jnp.float32
BF16 = jnp.bfloat16
VMEM = pl.BlockSpec(memory_space=pltpu.VMEM)
SMEM = pl.BlockSpec(memory_space=pltpu.SMEM)
ANY = pl.BlockSpec(memory_space=pl.ANY)
PARAMS = pltpu.CompilerParams(vmem_limit_bytes=58 << 20)


def rank_heads(counts_ref, table_ref, groups):
    counts = counts_ref[...].astype(BF16)
    blocks = counts.shape[1]
    over = (((1,), (1,)), ((), ()))
    mine = lax.dot_general(counts, jnp.ones((H, blocks), BF16), over, preferred_element_type=F32)
    theirs = lax.dot_general(jnp.ones((H, blocks), BF16), counts, over, preferred_element_type=F32)
    row = lax.broadcasted_iota(jnp.int32, (H, H), 0)
    lane = lax.broadcasted_iota(jnp.int32, (H, H), 1)
    bits = groups.bit_length() - 1

    def place_of(rank):
        slot, seat = rank >> bits, rank & (groups - 1)
        return slot * groups + jnp.where((slot & 1) == 0, seat, groups - 1 - seat)

    behind = (theirs > mine) | ((theirs == mine) & (lane < row))
    rank_down = jnp.sum(jnp.where(behind, 1.0, 0.0), axis=1, keepdims=True).astype(jnp.int32)
    ahead = (mine > theirs) | ((theirs == mine) & (row < lane))
    rank_along = jnp.sum(jnp.where(ahead, 1.0, 0.0), axis=0, keepdims=True).astype(jnp.int32)
    here = place_of(jnp.broadcast_to(rank_down, (H, H))) == lane
    head_at = jnp.sum(jnp.where(here, row.astype(F32), 0.0), axis=0, keepdims=True).astype(jnp.int32)
    table_ref[0:1, 0:H] = head_at
    table_ref[1:2, 0:H] = place_of(rank_along)


def turn_heads(source, turned):
    for pair in range(H // 2):
        tile = source[:, pair * 2 * DH : (pair + 1) * 2 * DH].T
        turned[2 * pair] = tile[:DH]
        turned[2 * pair + 1] = tile[DH:]


def put_heads(slot, table_ref, k_ref, turned_q, turned_v, out_ref):
    groups = out_ref.shape[0]
    low = lax.broadcasted_iota(jnp.int32, (DH, 2 * DH), 1) < DH
    for group in range(groups):
        head = table_ref[0, slot * groups + group]
        odd = head % 2
        lanes = pl.ds(pl.multiple_of((head // 2) * (2 * DH), 2 * DH), 2 * DH)
        plain = k_ref[pl.ds(pl.multiple_of(odd * DH, DH), DH), lanes]
        other = k_ref[pl.ds(pl.multiple_of((1 - odd) * DH, DH), DH), lanes]
        other = jnp.concatenate([other[:, DH:], other[:, :DH]], axis=1)
        out_ref[group, 0] = jnp.where(low == (odd == 0), plain, other)
        out_ref[group, 1] = turned_v[head]
        out_ref[group, 2] = turned_q[head]


def pack_first_kernel(groups, counts_ref, q_ref, k_ref, v_ref, table_ref, out_ref, turned_q, turned_v, table_vmem, sem):
    rank_heads(counts_ref, table_vmem, groups)
    copy = pltpu.make_async_copy(table_vmem, table_ref, sem)
    copy.start()
    turn_heads(q_ref, turned_q)
    turn_heads(v_ref, turned_v)
    copy.wait()
    put_heads(0, table_ref, k_ref, turned_q, turned_v, out_ref)


def pack_rest_kernel(slot, table_ref, q_ref, k_ref, v_ref, out_ref, turned_q, turned_v):
    turn_heads(q_ref, turned_q)
    turn_heads(v_ref, turned_v)
    put_heads(slot, table_ref, k_ref, turned_q, turned_v, out_ref)


def plan_kernel(uly, gather, table_ref, counts_ref, layout_ref, unit_ref, total_ref, lay_ref, sem):
    slots = total_ref.shape[0]
    groups = H // slots
    parts = groups // uly
    doc = lax.axis_index("doc")
    part, rest = doc // gather, doc % gather
    group = part * uly + lax.axis_index("uly")

    def rows_at(at):
        return (at * gather + rest) * uly

    copies = [
        pltpu.make_async_copy(
            layout_ref.at[table_ref[0, slot * groups + group], pl.ds(rows_at(at), uly)],
            lay_ref.at[slot, pl.ds(at * uly, uly)],
            sem.at[slot, at],
        )
        for slot in range(slots)
        for at in range(parts)
    ]
    for copy in copies:
        copy.start()

    def local(block):
        its = block // uly
        return ((its % gather) ^ rest) * groups + (its // gather) * uly + block % uly

    for copy in copies:
        copy.wait()
    for slot in range(slots):
        head = table_ref[0, slot * groups + group]

        def idle(base, many, slot=slot):
            for extra in range(many):
                unit_ref[slot, 0, base + extra] = groups
                unit_ref[slot, 1, base + extra] = 0
                unit_ref[slot, 2, base + extra] = 0
                unit_ref[slot, 3, base + extra] = 1

        def place_row(row, base, slot=slot, head=head):
            count = counts_ref[head, rows_at(row // uly) + row % uly]

            def place_unit(step, _):
                first = lay_ref[slot, row, 2 * step]
                whole = 2 * step + 1 < count
                second = jnp.where(whole, lay_ref[slot, row, jnp.minimum(2 * step + 1, KMAX - 1)], first)
                unit_ref[slot, 0, base + step] = row
                unit_ref[slot, 1, base + step] = local(first)
                unit_ref[slot, 2, base + step] = local(second)
                unit_ref[slot, 3, base + step] = whole.astype(jnp.int32)
                return 0

            units = (count + 1) // 2
            lax.fori_loop(0, units, place_unit, 0)
            return base + units

        idle(0, 2 * UNROLL)
        total = lax.fori_loop(0, groups, place_row, jnp.int32(2 * UNROLL))
        idle(total, 4 * UNROLL)
        total_ref[slot] = total


def attend_kernel(slot, gather, unit_ref, total_ref, *refs):
    arrived, refs = refs[:gather], refs[gather:]
    earlier, refs = refs[:slot], refs[slot:]
    out_ref, kv_ref, qt_ref, qz_ref, m_ref, l_ref, acc_ref, sem = refs[:8]
    score, top_of, out_of, sum_of = (refs[8 + 2 * at : 10 + 2 * at] for at in range(4))
    rows = qt_ref.shape[0]
    copies = [pltpu.make_async_copy(arrived[0].at[:, 2], qt_ref, sem.at[0])]
    copies += [
        pltpu.make_async_copy(array.at[:, 0:2], kv_ref.at[pl.ds(at * rows, rows)], sem.at[1 + at])
        for at, array in enumerate(arrived)
    ]
    copies += [
        pltpu.make_async_copy(result, out_ref.at[:, at], sem.at[1 + gather + at]) for at, result in enumerate(earlier)
    ]
    for copy in copies:
        copy.start()
    m_ref[...] = jnp.full(m_ref.shape, -BIG, F32)
    for ref in (l_ref, acc_ref):
        ref[...] = jnp.zeros(ref.shape, F32)
    zeros = jnp.zeros((DH, BLK), BF16)
    copies[0].wait()
    for row in range(rows):
        part = qt_ref[row]
        up = jnp.concatenate([part, zeros], axis=0)
        down = jnp.concatenate([zeros, part], axis=0)
        qz_ref[row] = jnp.concatenate([up, down], axis=1)
    qz_ref[rows] = jnp.zeros((2 * DH, 2 * BLK), BF16)
    for copy in copies[1:]:
        copy.wait()

    def make_scores(unit, lane, side):
        row, first, second = unit_ref[slot, 0, unit], unit_ref[slot, 1, unit], unit_ref[slot, 2, unit]
        keys = jnp.concatenate([kv_ref[first, 0], kv_ref[second, 0]], axis=0)
        scores = jnp.dot(keys, qz_ref[row], preferred_element_type=F32)
        score[side][lane] = scores
        top = jnp.max(scores.reshape(BLK // 8, 8, 2 * BLK), axis=0)
        top = jnp.maximum(top[:, :BLK], top[:, BLK:])
        top_of[side][lane] = jnp.broadcast_to(jnp.max(top, axis=0, keepdims=True), (8, BLK))

    def make_output(unit, lane, side):
        first, second = unit_ref[slot, 1, unit], unit_ref[slot, 2, unit]
        top = top_of[side][lane]
        limit = jnp.where(unit_ref[slot, 3, unit] == 1, top, top + BIG)
        scores = score[side][lane]
        tiles = (DH // 8, 8, BLK)
        weights = [
            jnp.exp(scores[at : at + DH, lanes : lanes + BLK].reshape(tiles) - bound[None])
            for at, bound in ((0, top), (DH, limit))
            for lanes in (0, BLK)
        ]
        sum_of[side][lane] = jnp.sum(sum(weights[1:], weights[0]), axis=0)
        weights = jnp.concatenate([part.reshape(DH, BLK) for part in weights], axis=0)
        values = jnp.concatenate([kv_ref[first, 1], kv_ref[second, 1]], axis=1)
        out_of[side][lane] = jnp.dot(values, weights.astype(BF16), preferred_element_type=F32)

    def merge(unit, lane, side):
        row = unit_ref[slot, 0, unit]
        top, old = top_of[side][lane], m_ref[row]
        new = jnp.maximum(old, top)
        a, b = jnp.exp(old - new), jnp.exp(top - new)
        m_ref[row] = new
        l_ref[row] = l_ref[row] * a + sum_of[side][lane] * b
        tiles = (DH // 8, 8, BLK)
        acc_ref[row] = (acc_ref[row].reshape(tiles) * a[None] + out_of[side][lane].reshape(tiles) * b[None]).reshape(
            DH, BLK
        )

    def step(index, _):
        for side in range(2):
            chunk = 2 * index + side
            for lane in range(UNROLL):
                merge(chunk * UNROLL + lane, lane, side)
            for lane in range(UNROLL):
                make_scores((chunk + 2) * UNROLL + lane, lane, side)
                make_output((chunk + 1) * UNROLL + lane, lane, 1 - side)
        return 0

    chunks = (total_ref[slot] + UNROLL - 1) // UNROLL
    lax.fori_loop(0, (chunks + 1) // 2, step, 0)
    for row in range(rows):
        total_w = jnp.sum(l_ref[row], axis=0, keepdims=True)
        result = (acc_ref[row] / total_w).astype(BF16)
        if len(out_ref.shape) == 4:
            out_ref[row, slot] = result
        else:
            out_ref[row] = result


def unpack_kernel(table_ref, o_ref, out_ref):
    groups = o_ref.shape[0]

    def fetch(head):
        place = table_ref[1, head]
        return o_ref[place % groups, place // groups]

    for pair in range(H // 2):
        both = jnp.concatenate([fetch(2 * pair), fetch(2 * pair + 1)], axis=0)
        out_ref[:, pair * 2 * DH : (pair + 1) * 2 * DH] = both.T


def shards(queries, key_vectors, value_vectors, layout, counts):
    uly, doc = lax.axis_size("uly"), lax.axis_size("doc")
    parts = max(min(doc // 2, H // (2 * uly)), 1)
    gather = doc // parts
    groups = uly * parts
    slots = H // groups
    shape = jax.ShapeDtypeStruct
    packed_shape = shape((groups, 3, DH, BLK), BF16)
    turned = [pltpu.VMEM((H, DH, BLK), BF16)] * 2
    table, first = pl.pallas_call(
        functools.partial(pack_first_kernel, groups),
        out_shape=(shape((8, 128), jnp.int32), packed_shape),
        in_specs=[VMEM] * 4,
        out_specs=(SMEM, VMEM),
        scratch_shapes=[*turned, pltpu.VMEM((8, 128), jnp.int32), pltpu.SemaphoreType.DMA],
        compiler_params=PARAMS,
        name="pack",
    )(counts, queries, key_vectors, value_vectors)
    packed = [first]
    for slot in range(1, slots):
        packed.append(
            pl.pallas_call(
                functools.partial(pack_rest_kernel, slot),
                out_shape=packed_shape,
                in_specs=[SMEM] + [VMEM] * 3,
                out_specs=VMEM,
                scratch_shapes=turned,
                compiler_params=PARAMS,
                name="pack",
            )(table, queries, key_vectors, value_vectors)
        )
    units, totals = pl.pallas_call(
        functools.partial(plan_kernel, uly, gather),
        out_shape=(shape((slots, 4, groups * KMAX // 2 + 8 * UNROLL), jnp.int32), shape((slots,), jnp.int32)),
        in_specs=[SMEM, SMEM, VMEM],
        out_specs=(SMEM, SMEM),
        scratch_shapes=[pltpu.SMEM((slots, groups, KMAX), jnp.int32), pltpu.SemaphoreType.DMA((slots, parts))],
        compiler_params=PARAMS,
        name="plan",
    )(table, counts, layout)

    members = [
        [(part * gather + rest) * uly + at for part in range(parts) for at in range(uly)] for rest in range(gather)
    ]
    swap = functools.partial(
        lax.all_to_all,
        axis_name=("doc", "uly"),
        split_axis=0,
        concat_axis=0,
        axis_index_groups=members,
        tiled=True,
    )

    def flip(array, bit):
        return lax.ppermute(array, "doc", [(at, at ^ bit) for at in range(doc)])

    arrived = swap(packed[0])
    arrived, units, totals, *packed = lax.optimization_barrier((arrived, units, totals, *packed))
    results = []
    for slot in range(slots):
        if slot:
            arrived, *results = lax.optimization_barrier((swap(packed[slot]), *results))
        arrays, bit = {0: arrived}, gather // 2
        while bit:
            arrays.update({at ^ bit: flip(array, bit) for at, array in list(arrays.items())})
            bit //= 2
        last = slot == slots - 1
        both = [pltpu.VMEM((UNROLL, BLK, 2 * BLK), F32)] * 2 + [pltpu.VMEM((UNROLL, 8, BLK), F32)] * 2
        both += [pltpu.VMEM((UNROLL, DH, BLK), F32)] * 2 + [pltpu.VMEM((UNROLL, 8, BLK), F32)] * 2
        earlier = results if last else []
        results.append(
            pl.pallas_call(
                functools.partial(attend_kernel, slot, gather),
                out_shape=shape((groups, slots, DH, BLK) if last else (groups, DH, BLK), BF16),
                in_specs=[SMEM, SMEM] + [ANY] * (gather + len(earlier)),
                out_specs=VMEM,
                scratch_shapes=[
                    pltpu.VMEM((gather * groups, 2, DH, BLK), BF16),
                    pltpu.VMEM((groups, DH, BLK), BF16),
                    pltpu.VMEM((groups + 1, 2 * DH, 2 * BLK), BF16),
                    pltpu.VMEM((groups + 1, 8, BLK), F32),
                    pltpu.VMEM((groups + 1, 8, BLK), F32),
                    pltpu.VMEM((groups + 1, DH, BLK), F32),
                    pltpu.SemaphoreType.DMA((1 + gather + slots,)),
                    *both,
                ],
                compiler_params=PARAMS,
                cost_estimate=pl.CostEstimate(flops=10**10, transcendentals=6 * 10**6, bytes_accessed=6 * 10**6),
                name="attend",
            )(units, totals, *[arrays[at] for at in range(gather)], *earlier)
        )
    return pl.pallas_call(
        unpack_kernel,
        out_shape=shape(queries.shape, BF16),
        in_specs=[SMEM, VMEM],
        out_specs=VMEM,
        compiler_params=PARAMS,
        name="unpack",
    )(table, swap(results[-1]))


def solution(mesh):
    placed = (
        P(("grp", "doc", "uly"), None),
        P(("grp", "doc", "uly"), None),
        P(("grp", "doc", "uly"), None),
        P("grp", None, None),
        P("grp", None),
    )
    return jax.shard_map(
        shards,
        mesh=mesh,
        in_specs=placed,
        out_specs=P(("grp", "doc", "uly"), None),
        check_vma=False,
    )
```

time: 331 us -> 88.9 us (0.27)
  local copies, waits for them, and re-layouts: 93.5 us -> 2.68 us
  matrix products: 69.1 us -> 0 us
  other arithmetic: 66 us -> 0 us
  blocking collectives: 69.2 us -> 19.9 us
  Pallas kernels: 0 us -> 43.6 us
  between operations: 23.4 us -> 0.07 us
  waiting for transfers between devices: 1.5 us -> 10.1 us
  starting transfers between devices: 3.68 us -> 12 us
    dot_general x40 -> x0, matrix products: 69.1 us -> none  [the longest x20 48.7 us: advance(): jnp.einsum('hyc,hcr->hyr', weights.astype(jnp.bfloat16), value_block_list...]
    gather x40 -> x0, local copies, waits for them, and re-layouts: 66.7 us -> none  [the longest x20 37 us: advance(): jnp.take(value_head, key_ids, axis=0).reshape(query_blocks, 4 * BLK, DH)]
    all_to_all x3 -> x1, blocking collectives: 69.2 us -> 19.9 us  [shards(): swap(results[-1])]
    pallas_call x0 -> x6, Pallas kernels: none -> 43.6 us  [the longest x2 22.6 us: shards(): pl.pallas_call(functools.partial(attend_kernel, slot, gather), out_shape=...]
    and x20 -> x0, other arithmetic: 25.2 us -> none  [advance(): jnp.take(key_head, key_ids, axis=0).reshape(query_blocks, 4 * BLK, DH)]
    select_n x20 -> x0, other arithmetic: 18.4 us -> none  [advance(): jnp.take(value_head, key_ids, axis=0).reshape(query_blocks, 4 * BLK, DH)]
    reduce_sum x20 -> x0, other arithmetic: 15 us -> none  [advance(): running_sum = running_sum * rescale + jnp.sum(weights, axis=-1)]
    slice x4 -> x0, local copies, waits for them, and re-layouts: 9.9 us -> none  [the longest x1 4.57 us: shards(): key_full[:, first_column:first_column + DH].reshape(all_blocks, BLK, DH)]
  transfers between devices with their start and end apart: 3 -> 4, of which waited for: 1 -> 3; matrix products, arithmetic and copies ran while one was open for 4% -> 0% of each run, Pallas kernels for 0% -> 36%
where the time goes in v5:
time: 88.9 us; the launch traced here: 88.2 us
  Pallas kernels  43.6 us (49%)
  blocking collectives  19.9 us (22%)
  starting transfers between devices  12 us (13%)
  waiting for transfers between devices  10.1 us (11%)
  local copies, waits for them, and re-layouts  2.68 us (3%)
    pallas_call x2, Pallas kernels, shards(): pl.pallas_call(functools.partial(attend_kernel, slot, gather), out_shape=...  22.6 us
    all_to_all x1, blocking collectives, shards(): swap(results[-1])  19.9 us
    pallas_call x1, Pallas kernels, shards(): pl.pallas_call(functools.partial(plan_kernel, uly, gather), out_shape=(sh...  12.8 us
    all_to_all x1, starting transfers between devices, shards(): arrived = swap(packed[0])  8.32 us
    all_to_all x1, waiting for transfers between devices, shards(): arrived = swap(packed[0])  4.93 us
    all_to_all x1, starting transfers between devices, shards(): arrived, *results = lax.optimization_barrier((swap(packed[slot]), *results))  3.65 us
    pallas_call x1, Pallas kernels, shards(): pl.pallas_call(functools.partial(pack_first_kernel, groups), out_shape=(s...  3.37 us
    all_to_all x1, waiting for transfers between devices, shards(): arrived, *results = lax.optimization_barrier((swap(packed[slot]), *results))  2.84 us
  transfers between devices with their start and end apart: 4, of which 3 were waited for; matrix products, arithmetic and copies ran while one was open for 0% of the time, Pallas kernels for 36%

profile of v5, /device:TPU:0, one launch (start us, length us, event | category | flops | bytes accessed | tf_op | source)
XLA Modules:
  0.0 88.2 jit_solution(8006818547712309130)
XLA Ops:
  0.0 3.4 %pack.2 = (s32[8,128]{1,0:T(8,128)}, bf16[16,3,64,128]{3,2,1,0:T(8,128)(2,1)}) custom-call(s32[32,32]{1,0:T(8,128)} %counts_ref.3, bf16[128,2048]{1,0:T(8,128)(2,1)} %q_ref.3, bf16[128,2048]{1,0:T(8,128)(2,1)} %k_ref.3, bf16[128,2048]{1,0:T(8,128)(2,1)} %v_ref.3), custom_call_target="tpu_custom_call" | custom-call | tf_op jit(solution)/shard_map/pack/pallas_call | solution.py:257
  3.4 8.3 %all-to-all-start = ((bf16[16,3,64,128]{3,2,1,0:T(8,128)(2,1)}), bf16[16,3,64,128]{3,2,1,0:T(8,128)(2,1)S(1)}, u32[]{:S(2)}, u32[]{:S(2)}) async-start(bf16[16,3,64,128]{3,2,1,0:T(8,128)(2,1)} %get-tuple-element.16), calls=%async_computation | async-start | bytes 1572864 | tf_op jit(solution)/shard_map/all_to_all | solution.py:304
  11.7 2.7 %pack.3 = bf16[16,3,64,128]{3,2,1,0:T(8,128)(2,1)} custom-call(s32[8,128]{1,0:T(8,128)} %get-tuple-element.15.table_ref, bf16[128,2048]{1,0:T(8,128)(2,1)} %q_ref.3, bf16[128,2048]{1,0:T(8,128)(2,1)} %k_ref.3, bf16[128,2048]{1,0:T(8,128)(2,1)} %v_ref.3), custom_call_target="tpu_custom_call" | custom-call | tf_op jit(solution)/shard_map/pack/pallas_call | solution.py:269
  14.4 12.8 %plan.1 = (s32[2,4,288]{2,1,0:T(4,128)}, s32[2]{0:T(128)}) custom-call(s32[8,128]{1,0:T(8,128)} %get-tuple-element.15.table_ref, s32[32,32]{1,0:T(8,128)} %counts_ref.3, s32[32,32,32]{2,1,0:T(8,128)} %layout_ref.1), custom_call_target="tpu_custom_call" | custom-call | tf_op jit(solution)/shard_map/plan/pallas_call | solution.py:279
  27.2 4.9 %all-to-all-done.refs_0_ = bf16[16,3,64,128]{3,2,1,0:T(8,128)(2,1)S(1)} async-done(((bf16[16,3,64,128]{3,2,1,0:T(8,128)(2,1)}), bf16[16,3,64,128]{3,2,1,0:T(8,128)(2,1)S(1)}, u32[]{:S(2)}, u32[]{:S(2)}) %all-to-all-start) | async-done | bytes 786464 | tf_op jit(solution)/shard_map/all_to_all | solution.py:304
  32.1 0.0 copy-start
  32.1 0.0 collective-permute-start
  32.1 0.9 %copy-done = bf16[16,3,64,128]{3,2,1,0:T(8,128)(2,1)} copy-done((bf16[16,3,64,128]{3,2,1,0:T(8,128)(2,1)}, bf16[16,3,64,128]{3,2,1,0:T(8,128)(2,1)S(1)}, u32[]{:S(2)}) %copy-start) | copy-done | bytes 786456
  33.0 3.6 %all-to-all-start.1 = ((bf16[16,3,64,128]{3,2,1,0:T(8,128)(2,1)}), bf16[16,3,64,128]{3,2,1,0:T(8,128)(2,1)S(1)}, u32[]{:S(2)}, u32[]{:S(2)}) async-start(bf16[16,3,64,128]{3,2,1,0:T(8,128)(2,1)} %pack.3), calls=%async_computation.1 | async-start | bytes 1572864 | tf_op jit(solution)/shard_map/all_to_all | solution.py:309
  36.7 0.0 collective-permute-done.refs_1_
  36.7 0.0 copy-start.2
  36.7 0.9 copy-done.2
  37.6 16.6 %attend.2.refs_2_ = bf16[16,64,128]{2,1,0:T(8,128)(2,1)} custom-call(s32[2,4,288]{2,1,0:T(4,128)} %get-tuple-element.19.unit_ref, s32[2]{0:T(128)} %get-tuple-element.20.total_ref, bf16[16,3,64,128]{3,2,1,0:T(8,128)(2,1)} %copy-done, bf16[16,3,64,128]{3,2,1,0:T(8,128)(2,1)} %copy-done.2), custom_call_target="tpu_custom_call" | custom-call | flops 10000000000 | bytes 6000000 | tf_op jit(solution)/shard_map/attend/pallas_call | solution.py:319
  54.2 2.8 %all-to-all-done.1.refs_0_ = bf16[16,3,64,128]{3,2,1,0:T(8,128)(2,1)S(1)} async-done(((bf16[16,3,64,128]{3,2,1,0:T(8,128)(2,1)}), bf16[16,3,64,128]{3,2,1,0:T(8,128)(2,1)S(1)}, u32[]{:S(2)}, u32[]{:S(2)}) %all-to-all-start.1) | async-done | bytes 786464 | tf_op jit(solution)/shard_map/all_to_all | solution.py:309
  57.1 0.0 copy-start.1
  57.1 0.0 collective-permute-start.1
  57.1 2.3 %collective-permute-done.1.refs_1_ = bf16[16,3,64,128]{3,2,1,0:T(8,128)(2,1)S(1)} collective-permute-done((bf16[16,3,64,128]{3,2,1,0:T(8,128)(2,1)S(1)}, bf16[16,3,64,128]{3,2,1,0:T(8,128)(2,1)S(1)}, u32[]{:S(2)}, u32[]{:S(2)}) %collective-permute-start.1) | collective-permute-done | bytes 786464 | tf_op jit(solution)/shard_map/ppermute | solution.py:302
  59.3 0.0 copy-done.1
  59.3 0.0 copy-start.3
  59.3 0.9 %copy-done.3 = bf16[16,3,64,128]{3,2,1,0:T(8,128)(2,1)} copy-done((bf16[16,3,64,128]{3,2,1,0:T(8,128)(2,1)}, bf16[16,3,64,128]{3,2,1,0:T(8,128)(2,1)S(1)}, u32[]{:S(2)}) %copy-start.3) | copy-done | bytes 786456
  60.3 6.0 %attend.3 = bf16[16,2,64,128]{3,2,1,0:T(8,128)(2,1)} custom-call(s32[2,4,288]{2,1,0:T(4,128)} %get-tuple-element.19.unit_ref, s32[2]{0:T(128)} %get-tuple-element.20.total_ref, bf16[16,3,64,128]{3,2,1,0:T(8,128)(2,1)} %copy-done.1, bf16[16,3,64,128]{3,2,1,0:T(8,128)(2,1)} %copy-done.3, bf16[16,64,128]{2,1,0:T(8,128)(2,1)} %attend.2.refs_2_), custom_call_target="tpu_custom_call" | custom-call | flops 10000000000 | bytes 6000000 | tf_op jit(solution)/shard_map/attend/pallas_call | solution.py:319
  66.2 19.9 %all_to_all.15.o_ref = bf16[16,2,64,128]{3,2,1,0:T(8,128)(2,1)} all-to-all(bf16[16,2,64,128]{3,2,1,0:T(8,128)(2,1)} %attend.3), channel_id=1, replica_groups={{0,4,8,12,16,20,24,28,2,6,10,14,18,22,26,30},{1,5,9,13,17,21,25,29,3,7,..., dimensions={0} | all-to-all | bytes 1048576 | tf_op jit(solution)/shard_map/all_to_all | solution.py:346
  86.1 2.1 %unpack.1 = bf16[128,2048]{1,0:T(8,128)(2,1)} custom-call(s32[8,128]{1,0:T(8,128)} %get-tuple-element.15.table_ref, bf16[16,2,64,128]{3,2,1,0:T(8,128)(2,1)} %all_to_all.15.o_ref), custom_call_target="tpu_custom_call" | custom-call | tf_op jit(solution)/shard_map/unpack/pallas_call | solution.py:339
Async XLA Ops:
  3.4 28.7 %all-to-all-start = ((bf16[16,3,64,128]{3,2,1,0:T(8,128)(2,1)}), bf16[16,3,64,128]{3,2,1,0:T(8,128)(2,1)S(1)}, u32[]{:S(2)}, u32[]{:S(2)}) async-start(bf16[16,3,64,128]{3,2,1,0:T(8,128)(2,1)} %get-tuple-element.16), calls=%async_computation | async-start | bytes 1572864 | tf_op jit(solution)/shard_map/all_to_all | solution.py:304
  32.1 0.9 %copy-start = (bf16[16,3,64,128]{3,2,1,0:T(8,128)(2,1)}, bf16[16,3,64,128]{3,2,1,0:T(8,128)(2,1)S(1)}, u32[]{:S(2)}) copy-start(bf16[16,3,64,128]{3,2,1,0:T(8,128)(2,1)S(1)} %all-to-all-done.refs_0_) | copy-start | bytes 2359300
  32.1 4.6 %collective-permute-start = (bf16[16,3,64,128]{3,2,1,0:T(8,128)(2,1)S(1)}, bf16[16,3,64,128]{3,2,1,0:T(8,128)(2,1)S(1)}, u32[]{:S(2)}, u32[]{:S(2)}) collective-permute-start(bf16[16,3,64,128]{3,2,1,0:T(8,128)(2,1)S(1)} %all-to-all-done.refs_0_), channel_id=1, source_target_pairs={{0,1},{1,0},{2,3},{3,2},{4,5},{5,4},{6,7},{7,6},{8,9},{9,8},{10,11... | collective-permute-start | bytes 2359304 | tf_op jit(solution)/shard_map/ppermute | solution.py:302
  33.0 24.0 %all-to-all-start.1 = ((bf16[16,3,64,128]{3,2,1,0:T(8,128)(2,1)}), bf16[16,3,64,128]{3,2,1,0:T(8,128)(2,1)S(1)}, u32[]{:S(2)}, u32[]{:S(2)}) async-start(bf16[16,3,64,128]{3,2,1,0:T(8,128)(2,1)} %pack.3), calls=%async_computation.1 | async-start | bytes 1572864 | tf_op jit(solution)/shard_map/all_to_all | solution.py:309
  36.7 0.9 copy-start.2
  57.1 2.3 %copy-start.1 = (bf16[16,3,64,128]{3,2,1,0:T(8,128)(2,1)}, bf16[16,3,64,128]{3,2,1,0:T(8,128)(2,1)S(1)}, u32[]{:S(2)}) copy-start(bf16[16,3,64,128]{3,2,1,0:T(8,128)(2,1)S(1)} %all-to-all-done.1.refs_0_) | copy-start | bytes 2359300
  57.1 2.3 %collective-permute-start.1 = (bf16[16,3,64,128]{3,2,1,0:T(8,128)(2,1)S(1)}, bf16[16,3,64,128]{3,2,1,0:T(8,128)(2,1)S(1)}, u32[]{:S(2)}, u32[]{:S(2)}) collective-permute-start(bf16[16,3,64,128]{3,2,1,0:T(8,128)(2,1)S(1)} %all-to-all-done.1.refs_0_), channel_id=1, source_target_pairs={{0,1},{1,0},{2,3},{3,2},{4,5},{5,4},{6,7},{7,6},{8,9},{9,8},{10,11... | collective-permute-start | bytes 2359304 | tf_op jit(solution)/shard_map/ppermute | solution.py:302
  59.3 0.9 %copy-start.3 = (bf16[16,3,64,128]{3,2,1,0:T(8,128)(2,1)}, bf16[16,3,64,128]{3,2,1,0:T(8,128)(2,1)S(1)}, u32[]{:S(2)}) copy-start(bf16[16,3,64,128]{3,2,1,0:T(8,128)(2,1)S(1)} %collective-permute-done.1.refs_1_) | copy-start | bytes 2359300

commit v6 on v5

--- a/solution.py
+++ b/solution.py
@@ -17,8 +17,7 @@
 BF16 = jnp.bfloat16
 VMEM = pl.BlockSpec(memory_space=pltpu.VMEM)
 SMEM = pl.BlockSpec(memory_space=pltpu.SMEM)
-ANY = pl.BlockSpec(memory_space=pl.ANY)
-PARAMS = pltpu.CompilerParams(vmem_limit_bytes=58 << 20)
+PARAMS = pltpu.CompilerParams(vmem_limit_bytes=28 << 20)
 
 
 def rank_heads(counts_ref, table_ref, groups):
@@ -52,35 +51,46 @@
         turned[2 * pair + 1] = tile[DH:]
 
 
-def put_heads(slot, table_ref, k_ref, turned_q, turned_v, out_ref):
-    groups = out_ref.shape[0]
+def fold_head(source, head):
+    odd = head % 2
     low = lax.broadcasted_iota(jnp.int32, (DH, 2 * DH), 1) < DH
-    for group in range(groups):
-        head = table_ref[0, slot * groups + group]
-        odd = head % 2
-        lanes = pl.ds(pl.multiple_of((head // 2) * (2 * DH), 2 * DH), 2 * DH)
-        plain = k_ref[pl.ds(pl.multiple_of(odd * DH, DH), DH), lanes]
-        other = k_ref[pl.ds(pl.multiple_of((1 - odd) * DH, DH), DH), lanes]
-        other = jnp.concatenate([other[:, DH:], other[:, :DH]], axis=1)
-        out_ref[group, 0] = jnp.where(low == (odd == 0), plain, other)
-        out_ref[group, 1] = turned_v[head]
-        out_ref[group, 2] = turned_q[head]
-
-
-def pack_first_kernel(groups, counts_ref, q_ref, k_ref, v_ref, table_ref, out_ref, turned_q, turned_v, table_vmem, sem):
+    lanes = pl.ds(pl.multiple_of((head // 2) * (2 * DH), 2 * DH), 2 * DH)
+    plain = source[pl.ds(pl.multiple_of(odd * DH, DH), DH), lanes]
+    other = source[pl.ds(pl.multiple_of((1 - odd) * DH, DH), DH), lanes]
+    return jnp.where(low == (odd == 0), plain, swap_halves(other))
+
+
+def swap_halves(tile):
+    return jnp.concatenate([tile[:, DH:], tile[:, :DH]], axis=1)
+
+
+def turn_folded(first, second):
+    low = lax.broadcasted_iota(jnp.int32, (DH, 2 * DH), 1) < DH
+    turned = jnp.concatenate([first, second], axis=0).T
+    early, late = turned[:DH], turned[DH:]
+    return jnp.where(low, early, swap_halves(late)), jnp.where(low, swap_halves(early), late)
+
+
+def pack_first_kernel(groups, counts_ref, q_ref, k_ref, v_ref, table_ref, out_ref, table_vmem, sem):
     rank_heads(counts_ref, table_vmem, groups)
     copy = pltpu.make_async_copy(table_vmem, table_ref, sem)
     copy.start()
-    turn_heads(q_ref, turned_q)
-    turn_heads(v_ref, turned_v)
     copy.wait()
-    put_heads(0, table_ref, k_ref, turned_q, turned_v, out_ref)
+    for group in range(groups):
+        head = table_ref[0, group]
+        for at, source in enumerate((k_ref, v_ref, q_ref)):
+            out_ref[group, at] = fold_head(source, head)
 
 
 def pack_rest_kernel(slot, table_ref, q_ref, k_ref, v_ref, out_ref, turned_q, turned_v):
     turn_heads(q_ref, turned_q)
     turn_heads(v_ref, turned_v)
-    put_heads(slot, table_ref, k_ref, turned_q, turned_v, out_ref)
+    groups = out_ref.shape[0]
+    for group in range(groups):
+        head = table_ref[0, slot * groups + group]
+        out_ref[group, 0] = fold_head(k_ref, head)
+        out_ref[group, 1] = turned_v[head]
+        out_ref[group, 2] = turned_q[head]
 
 
 def plan_kernel(uly, gather, table_ref, counts_ref, layout_ref, unit_ref, total_ref, lay_ref, sem):
@@ -148,32 +158,33 @@
 def attend_kernel(slot, gather, unit_ref, total_ref, *refs):
     arrived, refs = refs[:gather], refs[gather:]
     earlier, refs = refs[:slot], refs[slot:]
-    out_ref, kv_ref, qt_ref, qz_ref, m_ref, l_ref, acc_ref, sem = refs[:8]
-    score, top_of, out_of, sum_of = (refs[8 + 2 * at : 10 + 2 * at] for at in range(4))
-    rows = qt_ref.shape[0]
-    copies = [pltpu.make_async_copy(arrived[0].at[:, 2], qt_ref, sem.at[0])]
-    copies += [
-        pltpu.make_async_copy(array.at[:, 0:2], kv_ref.at[pl.ds(at * rows, rows)], sem.at[1 + at])
-        for at, array in enumerate(arrived)
-    ]
-    copies += [
-        pltpu.make_async_copy(result, out_ref.at[:, at], sem.at[1 + gather + at]) for at, result in enumerate(earlier)
-    ]
-    for copy in copies:
-        copy.start()
+    out_ref, kv_ref, qz_ref, m_ref, l_ref, acc_ref = refs[:6]
+    score, top_of, out_of, sum_of = (refs[6 + 2 * at : 8 + 2 * at] for at in range(4))
+    rows = arrived[0].shape[0]
     m_ref[...] = jnp.full(m_ref.shape, -BIG, F32)
     for ref in (l_ref, acc_ref):
         ref[...] = jnp.zeros(ref.shape, F32)
     zeros = jnp.zeros((DH, BLK), BF16)
-    copies[0].wait()
-    for row in range(rows):
-        part = qt_ref[row]
+
+    def put_query(row, part):
         up = jnp.concatenate([part, zeros], axis=0)
         down = jnp.concatenate([zeros, part], axis=0)
         qz_ref[row] = jnp.concatenate([up, down], axis=1)
+
+    for row in range(0, rows, 2):
+        pair = [arrived[0][row, 2], arrived[0][row + 1, 2]]
+        for at, part in enumerate(turn_folded(*pair) if slot == 0 else pair):
+            put_query(row + at, part)
     qz_ref[rows] = jnp.zeros((2 * DH, 2 * BLK), BF16)
-    for copy in copies[1:]:
-        copy.wait()
+    for at, array in enumerate(arrived):
+        for row in range(0, rows, 2):
+            place = at * rows + row
+            kv_ref[place, 0], kv_ref[place + 1, 0] = array[row, 0], array[row + 1, 0]
+            pair = [array[row, 1], array[row + 1, 1]]
+            kv_ref[place, 1], kv_ref[place + 1, 1] = turn_folded(*pair) if slot == 0 else pair
+    for at, result in enumerate(earlier):
+        for row in range(rows):
+            out_ref[row, at] = result[row]
 
     def make_scores(unit, lane, side):
         row, first, second = unit_ref[slot, 0, unit], unit_ref[slot, 1, unit], unit_ref[slot, 2, unit]
@@ -252,14 +263,14 @@
     groups = uly * parts
     slots = H // groups
     shape = jax.ShapeDtypeStruct
-    packed_shape = shape((groups, 3, DH, BLK), BF16)
+    packed_shape = pltpu.VMEM((groups, 3, DH, BLK), BF16)
     turned = [pltpu.VMEM((H, DH, BLK), BF16)] * 2
     table, first = pl.pallas_call(
         functools.partial(pack_first_kernel, groups),
         out_shape=(shape((8, 128), jnp.int32), packed_shape),
         in_specs=[VMEM] * 4,
         out_specs=(SMEM, VMEM),
-        scratch_shapes=[*turned, pltpu.VMEM((8, 128), jnp.int32), pltpu.SemaphoreType.DMA],
+        scratch_shapes=[pltpu.VMEM((8, 128), jnp.int32), pltpu.SemaphoreType.DMA],
         compiler_params=PARAMS,
         name="pack",
     )(counts, queries, key_vectors, value_vectors)
@@ -298,6 +309,9 @@
         tiled=True,
     )
 
+    def hold(array):
+        return pltpu.with_memory_space_constraint(array, pltpu.VMEM)
+
     def flip(array, bit):
         return lax.ppermute(array, "doc", [(at, at ^ bit) for at in range(doc)])
 
@@ -318,23 +332,21 @@
         results.append(
             pl.pallas_call(
                 functools.partial(attend_kernel, slot, gather),
-                out_shape=shape((groups, slots, DH, BLK) if last else (groups, DH, BLK), BF16),
-                in_specs=[SMEM, SMEM] + [ANY] * (gather + len(earlier)),
+                out_shape=pltpu.VMEM((groups, slots, DH, BLK) if last else (groups, DH, BLK), BF16),
+                in_specs=[SMEM, SMEM] + [VMEM] * (gather + len(earlier)),
                 out_specs=VMEM,
                 scratch_shapes=[
                     pltpu.VMEM((gather * groups, 2, DH, BLK), BF16),
-                    pltpu.VMEM((groups, DH, BLK), BF16),
                     pltpu.VMEM((groups + 1, 2 * DH, 2 * BLK), BF16),
                     pltpu.VMEM((groups + 1, 8, BLK), F32),
                     pltpu.VMEM((groups + 1, 8, BLK), F32),
                     pltpu.VMEM((groups + 1, DH, BLK), F32),
-                    pltpu.SemaphoreType.DMA((1 + gather + slots,)),
                     *both,
                 ],
                 compiler_params=PARAMS,
                 cost_estimate=pl.CostEstimate(flops=10**10, transcendentals=6 * 10**6, bytes_accessed=6 * 10**6),
                 name="attend",
-            )(units, totals, *[arrays[at] for at in range(gather)], *earlier)
+            )(units, totals, *[hold(arrays[at]) for at in range(gather)], *[hold(result) for result in earlier])
         )
     return pl.pallas_call(
         unpack_kernel,
@@ -343,7 +355,7 @@
         out_specs=VMEM,
         compiler_params=PARAMS,
         name="unpack",
-    )(table, swap(results[-1]))
+    )(table, hold(swap(results[-1])))
 
 
 def solution(mesh):

time: 88.9 us -> 87.3 us (0.982)
  Pallas kernels: 43.6 us -> 36.3 us
  waiting for transfers between devices: 10.1 us -> 15.2 us
  local copies, waits for them, and re-layouts: 2.68 us -> 3.87 us
    pallas_call x2, Pallas kernels: 22.6 us -> 18.4 us  [shards(): pl.pallas_call(functools.partial(attend_kernel, slot, gather), out_shape=...]
    all_to_all x1, waiting for transfers between devices: 2.84 us -> 6.57 us  [shards(): arrived, *results = lax.optimization_barrier((swap(packed[slot]), *results))]
    all_to_all x1, waiting for transfers between devices: 4.93 us -> 6.33 us  [shards(): arrived = swap(packed[0])]
    pallas_call x1, Pallas kernels: 3.37 us -> 2.17 us  [shards(): pl.pallas_call(functools.partial(pack_first_kernel, groups), out_shape=(s...]
    unnamed x8 -> x18, local copies, waits for them, and re-layouts: 2.68 us -> 3.87 us
  transfers between devices with their start and end apart: 4 -> 4, of which waited for: 3 -> 3; matrix products, arithmetic and copies ran while one was open for 0% -> 0% of each run, Pallas kernels for 36% -> 33%
where the time goes in v6:
time: 87.3 us; the launch traced here: 86.8 us
  Pallas kernels  36.3 us (42%)
  blocking collectives  19.2 us (22%)
  waiting for transfers between devices  15.2 us (17%)
  starting transfers between devices  12.1 us (14%)
  local copies, waits for them, and re-layouts  3.87 us (4%)
    all_to_all x1, blocking collectives, shards(): swap(results[-1])  19.2 us
    pallas_call x2, Pallas kernels, shards(): pl.pallas_call(functools.partial(attend_kernel, slot, gather), out_shape=...  18.4 us
    pallas_call x1, Pallas kernels, shards(): pl.pallas_call(functools.partial(plan_kernel, uly, gather), out_shape=(sh...  12.1 us
    all_to_all x1, starting transfers between devices, shards(): arrived = swap(packed[0])  8.46 us
    all_to_all x1, waiting for transfers between devices, shards(): arrived, *results = lax.optimization_barrier((swap(packed[slot]), *results))  6.57 us
    all_to_all x1, waiting for transfers between devices, shards(): arrived = swap(packed[0])  6.33 us
    unnamed x18, local copies, waits for them, and re-layouts  3.87 us
    all_to_all x1, starting transfers between devices, shards(): arrived, *results = lax.optimization_barrier((swap(packed[slot]), *results))  3.65 us
  transfers between devices with their start and end apart: 4, of which 3 were waited for; matrix products, arithmetic and copies ran while one was open for 0% of the time, Pallas kernels for 33%

profile of v6, /device:TPU:0, one launch (start us, length us, event | category | flops | bytes accessed | tf_op | source)
XLA Modules:
  0.0 86.8 jit_solution(11036123463678467506)
XLA Ops:
  0.0 0.0 copy-start
  0.0 1.0 %copy-done = bf16[128,2048]{1,0:T(8,128)(2,1)S(1)} copy-done((bf16[128,2048]{1,0:T(8,128)(2,1)S(1)}, bf16[128,2048]{1,0:T(8,128)(2,1)}, u32[]{:S(2)}) %copy-start) | copy-done | bytes 524312
  1.0 0.0 copy-start.2
  1.0 1.0 %copy-done.2 = bf16[128,2048]{1,0:T(8,128)(2,1)S(1)} copy-done((bf16[128,2048]{1,0:T(8,128)(2,1)S(1)}, bf16[128,2048]{1,0:T(8,128)(2,1)}, u32[]{:S(2)}) %copy-start.2) | copy-done | bytes 524312
  2.1 1.0 %copy-done.4 = bf16[128,2048]{1,0:T(8,128)(2,1)S(1)} copy-done((bf16[128,2048]{1,0:T(8,128)(2,1)S(1)}, bf16[128,2048]{1,0:T(8,128)(2,1)}, u32[]{:S(2)}) %copy-start.4) | copy-done | bytes 524312
  3.1 0.0 copy-start.7
  3.1 0.7 copy-done.7
  3.8 2.2 %pack.2 = (s32[8,128]{1,0:T(8,128)S(1)}, bf16[16,3,64,128]{3,2,1,0:T(8,128)(2,1)}) custom-call(s32[32,32]{1,0:T(8,128)S(1)} %copy-done.7, bf16[128,2048]{1,0:T(8,128)(2,1)S(1)} %copy-done, bf16[128,2048]{1,0:T(8,128)(2,1)S(1)} %copy-done.2, bf16[128,2048]{1,0:T(8,128)(2,1)S(1)} %copy-done.4), custom_call_target="tpu_custom_call" | custom-call | tf_op jit(solution)/shard_map/pack/pallas_call | solution.py:268
  6.0 0.0 copy-start.1
  6.0 0.0 copy-start.3
  6.0 0.0 copy-start.5
  6.1 8.5 %all-to-all-start = ((bf16[16,3,64,128]{3,2,1,0:T(8,128)(2,1)}), bf16[16,3,64,128]{3,2,1,0:T(8,128)(2,1)S(1)}, u32[]{:S(2)}, u32[]{:S(2)}) async-start(bf16[16,3,64,128]{3,2,1,0:T(8,128)(2,1)} %get-tuple-element.16), calls=%async_computation | async-start | bytes 1572864 | tf_op jit(solution)/shard_map/all_to_all | solution.py:318
  14.5 0.0 copy-done.1
  14.5 0.0 copy-done.3
  14.5 0.0 copy-done.5
  14.6 0.0 copy-start.6
  14.6 0.0 copy-start.8
  14.6 2.0 %pack.3 = bf16[16,3,64,128]{3,2,1,0:T(8,128)(2,1)} custom-call(s32[8,128]{1,0:T(8,128)S(1)} %get-tuple-element.15.table_ref, bf16[128,2048]{1,0:T(8,128)(2,1)S(1)} %copy-done.1, bf16[128,2048]{1,0:T(8,128)(2,1)S(1)} %copy-done.3, bf16[128,2048]{1,0:T(8,128)(2,1)S(1)} %copy-done.5), custom_call_target="tpu_custom_call" | custom-call | tf_op jit(solution)/shard_map/pack/pallas_call | solution.py:280
  16.5 0.0 copy-done.6
  16.5 0.0 copy-done.8
  16.5 12.1 %plan.1 = (s32[2,4,288]{2,1,0:T(4,128)S(1)}, s32[2]{0:T(128)S(1)}) custom-call(s32[8,128]{1,0:T(8,128)S(1)} %get-tuple-element.15.table_ref, s32[32,32]{1,0:T(8,128)S(1)} %copy-done.8, s32[32,32,32]{2,1,0:T(8,128)S(1)} %copy-done.6), custom_call_target="tpu_custom_call" | custom-call | tf_op jit(solution)/shard_map/plan/pallas_call | solution.py:290
  28.6 6.3 %all-to-all-done.refs_0_ = bf16[16,3,64,128]{3,2,1,0:T(8,128)(2,1)S(1)} async-done(((bf16[16,3,64,128]{3,2,1,0:T(8,128)(2,1)}), bf16[16,3,64,128]{3,2,1,0:T(8,128)(2,1)S(1)}, u32[]{:S(2)}, u32[]{:S(2)}) %all-to-all-start) | async-done | bytes 786464 | tf_op jit(solution)/shard_map/all_to_all | solution.py:318
  34.9 0.0 collective-permute-start
  34.9 3.6 %all-to-all-start.1 = ((bf16[16,3,64,128]{3,2,1,0:T(8,128)(2,1)}), bf16[16,3,64,128]{3,2,1,0:T(8,128)(2,1)S(1)}, u32[]{:S(2)}, u32[]{:S(2)}) async-start(bf16[16,3,64,128]{3,2,1,0:T(8,128)(2,1)} %pack.3), calls=%async_computation.1 | async-start | bytes 1572864 | tf_op jit(solution)/shard_map/all_to_all | solution.py:323
  38.6 0.0 collective-permute-done.refs_1_
  38.6 14.6 %attend.2.refs_2_ = bf16[16,64,128]{2,1,0:T(8,128)(2,1)S(1)} custom-call(s32[2,4,288]{2,1,0:T(4,128)S(1)} %get-tuple-element.19.unit_ref, s32[2]{0:T(128)S(1)} %get-tuple-element.20.total_ref, bf16[16,3,64,128]{3,2,1,0:T(8,128)(2,1)S(1)} %all-to-all-done.refs_0_, bf16[16,3,64,128]{3,2,1,0:T(8,128)(2,1)S(1)} %collective-permute-done.refs_1_), custom_call_target="tpu_custom_call" | custom-call | flops 10000000000 | bytes 6000000 | tf_op jit(solution)/shard_map/attend/pallas_call | solution.py:333
  53.2 6.6 %all-to-all-done.1.refs_0_ = bf16[16,3,64,128]{3,2,1,0:T(8,128)(2,1)S(1)} async-done(((bf16[16,3,64,128]{3,2,1,0:T(8,128)(2,1)}), bf16[16,3,64,128]{3,2,1,0:T(8,128)(2,1)S(1)}, u32[]{:S(2)}, u32[]{:S(2)}) %all-to-all-start.1) | async-done | bytes 786464 | tf_op jit(solution)/shard_map/all_to_all | solution.py:323
  59.8 0.0 collective-permute-start.1
  59.8 2.3 %collective-permute-done.1.refs_1_ = bf16[16,3,64,128]{3,2,1,0:T(8,128)(2,1)S(1)} collective-permute-done((bf16[16,3,64,128]{3,2,1,0:T(8,128)(2,1)S(1)}, bf16[16,3,64,128]{3,2,1,0:T(8,128)(2,1)S(1)}, u32[]{:S(2)}, u32[]{:S(2)}) %collective-permute-start.1) | collective-permute-done | bytes 786464 | tf_op jit(solution)/shard_map/ppermute | solution.py:316
  62.1 3.8 %attend.3 = bf16[16,2,64,128]{3,2,1,0:T(8,128)(2,1)S(1)} custom-call(s32[2,4,288]{2,1,0:T(4,128)S(1)} %get-tuple-element.19.unit_ref, s32[2]{0:T(128)S(1)} %get-tuple-element.20.total_ref, bf16[16,3,64,128]{3,2,1,0:T(8,128)(2,1)S(1)} %all-to-all-done.1.refs_0_, bf16[16,3,64,128]{3,2,1,0:T(8,128)(2,1)S(1)} %collective-permute-done.1.refs_1_, ...), custom_call_target="tpu_custom_call" | custom-call | flops 10000000000 | bytes 6000000 | tf_op jit(solution)/shard_map/attend/pallas_call | solution.py:333
  65.9 19.2 %all_to_all.15.o_ref = bf16[16,2,64,128]{3,2,1,0:T(8,128)(2,1)S(1)} all-to-all(bf16[16,2,64,128]{3,2,1,0:T(8,128)(2,1)S(1)} %attend.3), channel_id=1, replica_groups={{0,4,8,12,16,20,24,28,2,6,10,14,18,22,26,30},{1,5,9,13,17,21,25,29,3,7,..., dimensions={0} | all-to-all | bytes 1048576 | tf_op jit(solution)/shard_map/all_to_all | solution.py:358
  85.1 1.7 %unpack.1 = bf16[128,2048]{1,0:T(8,128)(2,1)} custom-call(s32[8,128]{1,0:T(8,128)S(1)} %get-tuple-element.15.table_ref, bf16[16,2,64,128]{3,2,1,0:T(8,128)(2,1)S(1)} %all_to_all.15.o_ref), custom_call_target="tpu_custom_call" | custom-call | tf_op jit(solution)/shard_map/unpack/pallas_call | solution.py:351
  (1 shorter events, 0.0 us)
Async XLA Ops:
  0.0 1.0 %copy-start = (bf16[128,2048]{1,0:T(8,128)(2,1)S(1)}, bf16[128,2048]{1,0:T(8,128)(2,1)}, u32[]{:S(2)}) copy-start(bf16[128,2048]{1,0:T(8,128)(2,1)} %q_ref.3) | copy-start | bytes 1572868
  1.0 1.0 %copy-start.2 = (bf16[128,2048]{1,0:T(8,128)(2,1)S(1)}, bf16[128,2048]{1,0:T(8,128)(2,1)}, u32[]{:S(2)}) copy-start(bf16[128,2048]{1,0:T(8,128)(2,1)} %k_ref.3) | copy-start | bytes 1572868
  2.1 1.0 %copy-start.4 = (bf16[128,2048]{1,0:T(8,128)(2,1)S(1)}, bf16[128,2048]{1,0:T(8,128)(2,1)}, u32[]{:S(2)}) copy-start(bf16[128,2048]{1,0:T(8,128)(2,1)} %v_ref.3) | copy-start | bytes 1572868
  3.1 0.7 copy-start.7
  6.0 8.5 %copy-start.1 = (bf16[128,2048]{1,0:T(8,128)(2,1)S(1)}, bf16[128,2048]{1,0:T(8,128)(2,1)}, u32[]{:S(2)}) copy-start(bf16[128,2048]{1,0:T(8,128)(2,1)} %q_ref.3) | copy-start | bytes 1572868
  6.0 8.5 %copy-start.3 = (bf16[128,2048]{1,0:T(8,128)(2,1)S(1)}, bf16[128,2048]{1,0:T(8,128)(2,1)}, u32[]{:S(2)}) copy-start(bf16[128,2048]{1,0:T(8,128)(2,1)} %k_ref.3) | copy-start | bytes 1572868
  6.0 8.5 %copy-start.5 = (bf16[128,2048]{1,0:T(8,128)(2,1)S(1)}, bf16[128,2048]{1,0:T(8,128)(2,1)}, u32[]{:S(2)}) copy-start(bf16[128,2048]{1,0:T(8,128)(2,1)} %v_ref.3) | copy-start | bytes 1572868
  6.1 28.9 %all-to-all-start = ((bf16[16,3,64,128]{3,2,1,0:T(8,128)(2,1)}), bf16[16,3,64,128]{3,2,1,0:T(8,128)(2,1)S(1)}, u32[]{:S(2)}, u32[]{:S(2)}) async-start(bf16[16,3,64,128]{3,2,1,0:T(8,128)(2,1)} %get-tuple-element.16), calls=%async_computation | async-start | bytes 1572864 | tf_op jit(solution)/shard_map/all_to_all | solution.py:318
  14.6 2.0 %copy-start.6 = (s32[32,32,32]{2,1,0:T(8,128)S(1)}, s32[32,32,32]{2,1,0:T(8,128)}, u32[]{:S(2)}) copy-start(s32[32,32,32]{2,1,0:T(8,128)} %layout_ref.1) | copy-start | bytes 393220
  14.6 2.0 %copy-start.8 = (s32[32,32]{1,0:T(8,128)S(1)}, s32[32,32]{1,0:T(8,128)}, u32[]{:S(2)}) copy-start(s32[32,32]{1,0:T(8,128)} %counts_ref.3) | copy-start | bytes 12292
  34.9 3.7 %collective-permute-start = (bf16[16,3,64,128]{3,2,1,0:T(8,128)(2,1)S(1)}, bf16[16,3,64,128]{3,2,1,0:T(8,128)(2,1)S(1)}, u32[]{:S(2)}, u32[]{:S(2)}) collective-permute-start(bf16[16,3,64,128]{3,2,1,0:T(8,128)(2,1)S(1)} %all-to-all-done.refs_0_), channel_id=1, source_target_pairs={{0,1},{1,0},{2,3},{3,2},{4,5},{5,4},{6,7},{7,6},{8,9},{9,8},{10,11... | collective-permute-start | bytes 2359304 | tf_op jit(solution)/shard_map/ppermute | solution.py:316
  34.9 24.9 %all-to-all-start.1 = ((bf16[16,3,64,128]{3,2,1,0:T(8,128)(2,1)}), bf16[16,3,64,128]{3,2,1,0:T(8,128)(2,1)S(1)}, u32[]{:S(2)}, u32[]{:S(2)}) async-start(bf16[16,3,64,128]{3,2,1,0:T(8,128)(2,1)} %pack.3), calls=%async_computation.1 | async-start | bytes 1572864 | tf_op jit(solution)/shard_map/all_to_all | solution.py:323
  59.8 2.3 %collective-permute-start.1 = (bf16[16,3,64,128]{3,2,1,0:T(8,128)(2,1)S(1)}, bf16[16,3,64,128]{3,2,1,0:T(8,128)(2,1)S(1)}, u32[]{:S(2)}, u32[]{:S(2)}) collective-permute-start(bf16[16,3,64,128]{3,2,1,0:T(8,128)(2,1)S(1)} %all-to-all-done.1.refs_0_), channel_id=1, source_target_pairs={{0,1},{1,0},{2,3},{3,2},{4,5},{5,4},{6,7},{7,6},{8,9},{9,8},{10,11... | collective-permute-start | bytes 2359304 | tf_op jit(solution)/shard_map/ppermute | solution.py:316

commit v7 on v6

--- a/solution.py
+++ b/solution.py
@@ -17,6 +17,7 @@
 BF16 = jnp.bfloat16
 VMEM = pl.BlockSpec(memory_space=pltpu.VMEM)
 SMEM = pl.BlockSpec(memory_space=pltpu.SMEM)
+HBM = pl.BlockSpec(memory_space=pltpu.HBM)
 PARAMS = pltpu.CompilerParams(vmem_limit_bytes=28 << 20)
 
 
@@ -71,26 +72,60 @@
     return jnp.where(low, early, swap_halves(late)), jnp.where(low, swap_halves(early), late)
 
 
-def pack_first_kernel(groups, counts_ref, q_ref, k_ref, v_ref, table_ref, out_ref, table_vmem, sem):
+def load(arrays, buffers, sems):
+    rows = arrays[0].shape[0] // 4
+    copies = [
+        [
+            pltpu.make_async_copy(array.at[pl.ds(at * rows, rows)], buffer.at[pl.ds(at * rows, rows)], sems.at[which, at])
+            for at in range(4)
+        ]
+        for which, (array, buffer) in enumerate(zip(arrays, buffers))
+    ]
+    for group in copies:
+        for copy in group:
+            copy.start()
+    return copies
+
+
+def pack_first_kernel(groups, counts_ref, q_hbm, k_hbm, v_hbm, table_ref, out_hbm, q_ref, k_ref, v_ref, sems, table_vmem, sem, out_ref, out_sem):
+    copies = load((k_hbm, v_hbm, q_hbm), (k_ref, v_ref, q_ref), sems)
     rank_heads(counts_ref, table_vmem, groups)
     copy = pltpu.make_async_copy(table_vmem, table_ref, sem)
     copy.start()
     copy.wait()
-    for group in range(groups):
-        head = table_ref[0, group]
-        for at, source in enumerate((k_ref, v_ref, q_ref)):
-            out_ref[group, at] = fold_head(source, head)
-
-
-def pack_rest_kernel(slot, table_ref, q_ref, k_ref, v_ref, out_ref, turned_q, turned_v):
+    leave = []
+    for which, source, places in ((0, k_ref, ((2, 0), (3, 1))), (1, v_ref, ((0, 0),)), (2, q_ref, ((1, 0),))):
+        for copy in copies[which]:
+            copy.wait()
+        for at, slot in places:
+            if at < out_ref.shape[0]:
+                for group in range(groups):
+                    out_ref[at, group] = fold_head(source, table_ref[0, slot * groups + group])
+                leave.append(pltpu.make_async_copy(out_ref.at[at], out_hbm.at[:, at], out_sem.at[at]))
+                leave[-1].start()
+    for copy in leave:
+        copy.wait()
+
+
+def pack_rest_kernel(slot, table_ref, q_hbm, k_hbm, v_hbm, out_ref, q_ref, k_ref, v_ref, sems, turned_q, turned_v):
+    copies = load((k_hbm, v_hbm, q_hbm), (k_ref, v_ref, q_ref), sems)
+    for group in copies:
+        for copy in group:
+            copy.wait()
     turn_heads(q_ref, turned_q)
     turn_heads(v_ref, turned_v)
-    groups = out_ref.shape[0]
+    groups, tiles = out_ref.shape[:2]
     for group in range(groups):
         head = table_ref[0, slot * groups + group]
-        out_ref[group, 0] = fold_head(k_ref, head)
-        out_ref[group, 1] = turned_v[head]
-        out_ref[group, 2] = turned_q[head]
+        out_ref[group, 0] = turned_v[head]
+        out_ref[group, 1] = turned_q[head]
+        if tiles > 2:
+            out_ref[group, 2] = fold_head(k_ref, table_ref[0, (slot + 1) * groups + group])
+
+
+def mirror(value, size):
+    bits = size.bit_length() - 1
+    return sum(((value >> at) & 1) << (bits - 1 - at) for at in range(bits)) if bits else value
 
 
 def plan_kernel(uly, gather, table_ref, counts_ref, layout_ref, unit_ref, total_ref, lay_ref, sem):
@@ -99,7 +134,7 @@
     parts = groups // uly
     doc = lax.axis_index("doc")
     part, rest = doc // gather, doc % gather
-    group = part * uly + lax.axis_index("uly")
+    group = part * uly + mirror(lax.axis_index("uly"), uly)
 
     def rows_at(at):
         return (at * gather + rest) * uly
@@ -118,7 +153,7 @@
 
     def local(block):
         its = block // uly
-        return ((its % gather) ^ rest) * groups + (its // gather) * uly + block % uly
+        return ((its % gather) ^ rest) * groups + (its // gather) * uly + mirror(block % uly, uly)
 
     for copy in copies:
         copy.wait()
@@ -133,12 +168,13 @@
                 unit_ref[slot, 3, base + extra] = 1
 
         def place_row(row, base, slot=slot, head=head):
-            count = counts_ref[head, rows_at(row // uly) + row % uly]
+            token = (row // uly) * uly + mirror(row % uly, uly)
+            count = counts_ref[head, rows_at(row // uly) + mirror(row % uly, uly)]
 
             def place_unit(step, _):
-                first = lay_ref[slot, row, 2 * step]
+                first = lay_ref[slot, token, 2 * step]
                 whole = 2 * step + 1 < count
-                second = jnp.where(whole, lay_ref[slot, row, jnp.minimum(2 * step + 1, KMAX - 1)], first)
+                second = jnp.where(whole, lay_ref[slot, token, jnp.minimum(2 * step + 1, KMAX - 1)], first)
                 unit_ref[slot, 0, base + step] = row
                 unit_ref[slot, 1, base + step] = local(first)
                 unit_ref[slot, 2, base + step] = local(second)
@@ -157,6 +193,8 @@
 
 def attend_kernel(slot, gather, unit_ref, total_ref, *refs):
     arrived, refs = refs[:gather], refs[gather:]
+    before, refs = (refs[:gather], refs[gather:]) if slot else (arrived, refs)
+    key_at = 3 if slot == 1 else 2
     earlier, refs = refs[:slot], refs[slot:]
     out_ref, kv_ref, qz_ref, m_ref, l_ref, acc_ref = refs[:6]
     score, top_of, out_of, sum_of = (refs[6 + 2 * at : 8 + 2 * at] for at in range(4))
@@ -172,15 +210,15 @@
         qz_ref[row] = jnp.concatenate([up, down], axis=1)
 
     for row in range(0, rows, 2):
-        pair = [arrived[0][row, 2], arrived[0][row + 1, 2]]
+        pair = [arrived[0][row, 1], arrived[0][row + 1, 1]]
         for at, part in enumerate(turn_folded(*pair) if slot == 0 else pair):
             put_query(row + at, part)
     qz_ref[rows] = jnp.zeros((2 * DH, 2 * BLK), BF16)
-    for at, array in enumerate(arrived):
+    for at, (array, keys) in enumerate(zip(arrived, before)):
         for row in range(0, rows, 2):
             place = at * rows + row
-            kv_ref[place, 0], kv_ref[place + 1, 0] = array[row, 0], array[row + 1, 0]
-            pair = [array[row, 1], array[row + 1, 1]]
+            kv_ref[place, 0], kv_ref[place + 1, 0] = keys[row, key_at], keys[row + 1, key_at]
+            pair = [array[row, 0], array[row + 1, 0]]
             kv_ref[place, 1], kv_ref[place + 1, 1] = turn_folded(*pair) if slot == 0 else pair
     for at, result in enumerate(earlier):
         for row in range(rows):
@@ -263,14 +301,20 @@
     groups = uly * parts
     slots = H // groups
     shape = jax.ShapeDtypeStruct
-    packed_shape = pltpu.VMEM((groups, 3, DH, BLK), BF16)
-    turned = [pltpu.VMEM((H, DH, BLK), BF16)] * 2
+    slot_tiles = [2 + (slot == 0) + (slot + 1 < slots) for slot in range(slots)]
+    held = [pltpu.VMEM(queries.shape, BF16)] * 3 + [pltpu.SemaphoreType.DMA((3, 4))]
     table, first = pl.pallas_call(
         functools.partial(pack_first_kernel, groups),
-        out_shape=(shape((8, 128), jnp.int32), packed_shape),
-        in_specs=[VMEM] * 4,
-        out_specs=(SMEM, VMEM),
-        scratch_shapes=[pltpu.VMEM((8, 128), jnp.int32), pltpu.SemaphoreType.DMA],
+        out_shape=(shape((8, 128), jnp.int32), shape((groups, slot_tiles[0], DH, BLK), BF16)),
+        in_specs=[VMEM] + [HBM] * 3,
+        out_specs=(SMEM, HBM),
+        scratch_shapes=[
+            *held,
+            pltpu.VMEM((8, 128), jnp.int32),
+            pltpu.SemaphoreType.DMA,
+            pltpu.VMEM((slot_tiles[0], groups, DH, BLK), BF16),
+            pltpu.SemaphoreType.DMA((slot_tiles[0],)),
+        ],
         compiler_params=PARAMS,
         name="pack",
     )(counts, queries, key_vectors, value_vectors)
@@ -279,10 +323,10 @@
         packed.append(
             pl.pallas_call(
                 functools.partial(pack_rest_kernel, slot),
-                out_shape=packed_shape,
-                in_specs=[SMEM] + [VMEM] * 3,
+                out_shape=pltpu.VMEM((groups, slot_tiles[slot], DH, BLK), BF16),
+                in_specs=[SMEM] + [HBM] * 3,
                 out_specs=VMEM,
-                scratch_shapes=turned,
+                scratch_shapes=[*held] + [pltpu.VMEM((H, DH, BLK), BF16)] * 2,
                 compiler_params=PARAMS,
                 name="pack",
             )(table, queries, key_vectors, value_vectors)
@@ -298,7 +342,8 @@
     )(table, counts, layout)
 
     members = [
-        [(part * gather + rest) * uly + at for part in range(parts) for at in range(uly)] for rest in range(gather)
+        [(part * gather + rest) * uly + mirror(at, uly) for part in range(parts) for at in range(uly)]
+        for rest in range(gather)
     ]
     swap = functools.partial(
         lax.all_to_all,
@@ -317,8 +362,9 @@
 
     arrived = swap(packed[0])
     arrived, units, totals, *packed = lax.optimization_barrier((arrived, units, totals, *packed))
-    results = []
+    results, arrays = [], {}
     for slot in range(slots):
+        before = arrays if slot else {}
         if slot:
             arrived, *results = lax.optimization_barrier((swap(packed[slot]), *results))
         arrays, bit = {0: arrived}, gather // 2
@@ -333,7 +379,7 @@
             pl.pallas_call(
                 functools.partial(attend_kernel, slot, gather),
                 out_shape=pltpu.VMEM((groups, slots, DH, BLK) if last else (groups, DH, BLK), BF16),
-                in_specs=[SMEM, SMEM] + [VMEM] * (gather + len(earlier)),
+                in_specs=[SMEM, SMEM] + [VMEM] * (gather + len(before) + len(earlier)),
                 out_specs=VMEM,
                 scratch_shapes=[
                     pltpu.VMEM((gather * groups, 2, DH, BLK), BF16),
@@ -346,7 +392,7 @@
                 compiler_params=PARAMS,
                 cost_estimate=pl.CostEstimate(flops=10**10, transcendentals=6 * 10**6, bytes_accessed=6 * 10**6),
                 name="attend",
-            )(units, totals, *[hold(arrays[at]) for at in range(gather)], *[hold(result) for result in earlier])
+            )(units, totals, *[hold(part[at]) for part in (arrays, before) for at in range(len(part))], *[hold(result) for result in earlier])
         )
     return pl.pallas_call(
         unpack_kernel,

time: 87.3 us -> 90.2 us (1.033)
  Pallas kernels: 36.3 us -> 42.5 us
  waiting for transfers between devices: 15.2 us -> 9.88 us
  local copies, waits for them, and re-layouts: 3.87 us -> 4.84 us
    all_to_all x1, waiting for transfers between devices: 6.57 us -> 0.19 us  [shards(): arrived, *results = lax.optimization_barrier((swap(packed[slot]), *results))]
    pallas_call x1, Pallas kernels: 2.17 us -> 4.61 us  [shards(): pl.pallas_call(functools.partial(pack_first_kernel, groups), out_shape=(s...]
    pallas_call x1, Pallas kernels: 1.96 us -> 3.88 us  [shards(): pl.pallas_call(functools.partial(pack_rest_kernel, slot), out_shape=pltpu...]
    pallas_call x1, Pallas kernels: 12.1 us -> 13.9 us  [shards(): pl.pallas_call(functools.partial(plan_kernel, uly, gather), out_shape=(sh...]
    all_to_all x1, waiting for transfers between devices: 6.33 us -> 7.78 us  [shards(): arrived = swap(packed[0])]
    unnamed x18 -> x20, local copies, waits for them, and re-layouts: 3.87 us -> 4.84 us
    all_to_all x1, blocking collectives: 19.2 us -> 20.1 us  [shards(): swap(results[-1])]
  transfers between devices with their start and end apart: 4 -> 4, of which waited for: 3 -> 3; matrix products, arithmetic and copies ran while one was open for 0% -> 0% of each run, Pallas kernels for 33% -> 37%
where the time goes in v7:
time: 90.2 us; the launch traced here: 89.9 us
  Pallas kernels  42.5 us (47%)
  blocking collectives  20.1 us (22%)
  starting transfers between devices  12.4 us (14%)
  waiting for transfers between devices  9.88 us (11%)
  local copies, waits for them, and re-layouts  4.84 us (5%)
    all_to_all x1, blocking collectives, shards(): swap(results[-1])  20.1 us
    pallas_call x2, Pallas kernels, shards(): pl.pallas_call(functools.partial(attend_kernel, slot, gather), out_shape=...  18.4 us
    pallas_call x1, Pallas kernels, shards(): pl.pallas_call(functools.partial(plan_kernel, uly, gather), out_shape=(sh...  13.9 us
    all_to_all x1, starting transfers between devices, shards(): arrived = swap(packed[0])  8.44 us
    all_to_all x1, waiting for transfers between devices, shards(): arrived = swap(packed[0])  7.78 us
    unnamed x20, local copies, waits for them, and re-layouts  4.84 us
    pallas_call x1, Pallas kernels, shards(): pl.pallas_call(functools.partial(pack_first_kernel, groups), out_shape=(s...  4.61 us
    all_to_all x1, starting transfers between devices, shards(): arrived, *results = lax.optimization_barrier((swap(packed[slot]), *results))  3.98 us
  transfers between devices with their start and end apart: 4, of which 3 were waited for; matrix products, arithmetic and copies ran while one was open for 0% of the time, Pallas kernels for 37%

profile of v7, /device:TPU:0, one launch (start us, length us, event | category | flops | bytes accessed | tf_op | source)
XLA Modules:
  0.0 89.9 jit_solution(8555415509555580224)
XLA Ops:
  0.0 0.0 copy-start
  0.0 1.0 %copy-done = bf16[128,2048]{1,0:T(8,128)(2,1)S(1)} copy-done((bf16[128,2048]{1,0:T(8,128)(2,1)S(1)}, bf16[128,2048]{1,0:T(8,128)(2,1)}, u32[]{:S(2)}) %copy-start) | copy-done | bytes 524312
  1.0 0.0 copy-start.2
  1.0 1.0 %copy-done.2 = bf16[128,2048]{1,0:T(8,128)(2,1)S(1)} copy-done((bf16[128,2048]{1,0:T(8,128)(2,1)S(1)}, bf16[128,2048]{1,0:T(8,128)(2,1)}, u32[]{:S(2)}) %copy-start.2) | copy-done | bytes 524312
  2.1 0.0 copy-start.4
  2.1 1.0 %copy-done.4 = bf16[128,2048]{1,0:T(8,128)(2,1)S(1)} copy-done((bf16[128,2048]{1,0:T(8,128)(2,1)S(1)}, bf16[128,2048]{1,0:T(8,128)(2,1)}, u32[]{:S(2)}) %copy-start.4) | copy-done | bytes 524312
  3.1 0.0 copy-start.8
  3.1 0.7 copy-done.8
  3.8 4.6 %pack.2 = (s32[8,128]{1,0:T(8,128)S(1)}, bf16[16,4,64,128]{3,2,1,0:T(8,128)(2,1)S(1)}) custom-call(s32[32,32]{1,0:T(8,128)S(1)} %copy-done.8, bf16[128,2048]{1,0:T(8,128)(2,1)S(1)} %copy-done, bf16[128,2048]{1,0:T(8,128)(2,1)S(1)} %copy-done.2, bf16[128,2048]{1,0:T(8,128)(2,1)S(1)} %copy-done.4), custom_call_target="tpu_custom_call" | custom-call | tf_op jit(solution)/shard_map/pack/pallas_call | solution.py:306
  8.5 0.0 copy-start.6
  8.5 1.0 %copy-done.6 = bf16[16,4,64,128]{3,2,1,0:T(8,128)(2,1)} copy-done((bf16[16,4,64,128]{3,2,1,0:T(8,128)(2,1)}, bf16[16,4,64,128]{3,2,1,0:T(8,128)(2,1)S(1)}, u32[]{:S(2)}) %copy-start.6) | copy-done | bytes 1048600
  9.5 8.4 %all-to-all-start = ((bf16[16,4,64,128]{3,2,1,0:T(8,128)(2,1)}), bf16[16,4,64,128]{3,2,1,0:T(8,128)(2,1)S(1)}, u32[]{:S(2)}, u32[]{:S(2)}) async-start(bf16[16,4,64,128]{3,2,1,0:T(8,128)(2,1)} %copy-done.6), calls=%async_computation | async-start | bytes 2097152 | tf_op jit(solution)/shard_map/all_to_all | solution.py:363
  17.9 0.0 copy-done.1
  17.9 0.0 copy-done.3
  17.9 0.0 copy-done.5
  17.9 0.0 copy-start.7
  17.9 0.0 copy-start.9
  18.0 3.9 %pack.3 = bf16[16,2,64,128]{3,2,1,0:T(8,128)(2,1)} custom-call(s32[8,128]{1,0:T(8,128)S(1)} %get-tuple-element.15.table_ref, bf16[128,2048]{1,0:T(8,128)(2,1)S(1)} %copy-done.1, bf16[128,2048]{1,0:T(8,128)(2,1)S(1)} %copy-done.3, bf16[128,2048]{1,0:T(8,128)(2,1)S(1)} %copy-done.5), custom_call_target="tpu_custom_call" | custom-call | tf_op jit(solution)/shard_map/pack/pallas_call | solution.py:324
  21.9 0.0 copy-done.7
  21.9 0.0 copy-done.9
  21.9 13.9 %plan.1 = (s32[2,4,288]{2,1,0:T(4,128)S(1)}, s32[2]{0:T(128)S(1)}) custom-call(s32[8,128]{1,0:T(8,128)S(1)} %get-tuple-element.15.table_ref, s32[32,32]{1,0:T(8,128)S(1)} %copy-done.9, s32[32,32,32]{2,1,0:T(8,128)S(1)} %copy-done.7), custom_call_target="tpu_custom_call" | custom-call | tf_op jit(solution)/shard_map/plan/pallas_call | solution.py:334
  35.8 7.8 %all-to-all-done.refs_0_.refs_2_ = bf16[16,4,64,128]{3,2,1,0:T(8,128)(2,1)S(1)} async-done(((bf16[16,4,64,128]{3,2,1,0:T(8,128)(2,1)}), bf16[16,4,64,128]{3,2,1,0:T(8,128)(2,1)S(1)}, u32[]{:S(2)}, u32[]{:S(2)}) %all-to-all-start) | async-done | bytes 1048608 | tf_op jit(solution)/shard_map/all_to_all | solution.py:363
  43.6 0.0 collective-permute-start
  43.6 4.0 %all-to-all-start.1 = ((bf16[16,2,64,128]{3,2,1,0:T(8,128)(2,1)}), bf16[16,2,64,128]{3,2,1,0:T(8,128)(2,1)S(1)}, u32[]{:S(2)}, u32[]{:S(2)}) async-start(bf16[16,2,64,128]{3,2,1,0:T(8,128)(2,1)} %pack.3), calls=%async_computation.1 | async-start | bytes 1048576 | tf_op jit(solution)/shard_map/all_to_all | solution.py:369
  47.6 0.0 collective-permute-done.refs_1_.refs_3_
  47.6 15.1 %attend.2.refs_4_ = bf16[16,64,128]{2,1,0:T(8,128)(2,1)S(1)} custom-call(s32[2,4,288]{2,1,0:T(4,128)S(1)} %get-tuple-element.19.unit_ref, s32[2]{0:T(128)S(1)} %get-tuple-element.20.total_ref, bf16[16,4,64,128]{3,2,1,0:T(8,128)(2,1)S(1)} %all-to-all-done.refs_0_.refs_2_, bf16[16,4,64,128]{3,2,1,0:T(8,128)(2,1)S(1)} %collective-permute-done.refs_1_.refs_3_), custom_call_target="tpu_custom_call" | custom-call | flops 10000000000 | bytes 6000000 | tf_op jit(solution)/shard_map/attend/pallas_call | solution.py:379
  62.6 0.2 all-to-all-done.1.refs_0_
  62.8 0.0 collective-permute-start.1
  62.8 1.9 %collective-permute-done.1.refs_1_ = bf16[16,2,64,128]{3,2,1,0:T(8,128)(2,1)S(1)} collective-permute-done((bf16[16,2,64,128]{3,2,1,0:T(8,128)(2,1)S(1)}, bf16[16,2,64,128]{3,2,1,0:T(8,128)(2,1)S(1)}, u32[]{:S(2)}, u32[]{:S(2)}) %collective-permute-start.1) | collective-permute-done | bytes 524320 | tf_op jit(solution)/shard_map/ppermute | solution.py:361
  64.7 3.4 %attend.3 = bf16[16,2,64,128]{3,2,1,0:T(8,128)(2,1)S(1)} custom-call(s32[2,4,288]{2,1,0:T(4,128)S(1)} %get-tuple-element.19.unit_ref, s32[2]{0:T(128)S(1)} %get-tuple-element.20.total_ref, bf16[16,2,64,128]{3,2,1,0:T(8,128)(2,1)S(1)} %all-to-all-done.1.refs_0_, bf16[16,2,64,128]{3,2,1,0:T(8,128)(2,1)S(1)} %collective-permute-done.1.refs_1_, ...), custom_call_target="tpu_custom_call" | custom-call | flops 10000000000 | bytes 6000000 | tf_op jit(solution)/shard_map/attend/pallas_call | solution.py:379
  68.1 20.1 %all_to_all.15.o_ref = bf16[16,2,64,128]{3,2,1,0:T(8,128)(2,1)S(1)} all-to-all(bf16[16,2,64,128]{3,2,1,0:T(8,128)(2,1)S(1)} %attend.3), channel_id=1, replica_groups={{0,16,8,24,4,20,12,28,2,18,10,26,6,22,14,30},{1,17,9,25,5,21,13,29,3,19..., dimensions={0} | all-to-all | bytes 1048576 | tf_op jit(solution)/shard_map/all_to_all | solution.py:404
  88.2 1.7 %unpack.1 = bf16[128,2048]{1,0:T(8,128)(2,1)} custom-call(s32[8,128]{1,0:T(8,128)S(1)} %get-tuple-element.15.table_ref, bf16[16,2,64,128]{3,2,1,0:T(8,128)(2,1)S(1)} %all_to_all.15.o_ref), custom_call_target="tpu_custom_call" | custom-call | tf_op jit(solution)/shard_map/unpack/pallas_call | solution.py:397
  (3 shorter events, 0.0 us)
Async XLA Ops:
  0.0 1.0 %copy-start = (bf16[128,2048]{1,0:T(8,128)(2,1)S(1)}, bf16[128,2048]{1,0:T(8,128)(2,1)}, u32[]{:S(2)}) copy-start(bf16[128,2048]{1,0:T(8,128)(2,1)} %q_hbm.3) | copy-start | bytes 1572868
  1.0 1.0 %copy-start.2 = (bf16[128,2048]{1,0:T(8,128)(2,1)S(1)}, bf16[128,2048]{1,0:T(8,128)(2,1)}, u32[]{:S(2)}) copy-start(bf16[128,2048]{1,0:T(8,128)(2,1)} %k_hbm.3) | copy-start | bytes 1572868
  2.1 1.0 %copy-start.4 = (bf16[128,2048]{1,0:T(8,128)(2,1)S(1)}, bf16[128,2048]{1,0:T(8,128)(2,1)}, u32[]{:S(2)}) copy-start(bf16[128,2048]{1,0:T(8,128)(2,1)} %v_hbm.3) | copy-start | bytes 1572868
  3.1 0.7 copy-start.8
  8.5 1.0 %copy-start.6 = (bf16[16,4,64,128]{3,2,1,0:T(8,128)(2,1)}, bf16[16,4,64,128]{3,2,1,0:T(8,128)(2,1)S(1)}, u32[]{:S(2)}) copy-start(bf16[16,4,64,128]{3,2,1,0:T(8,128)(2,1)S(1)} %get-tuple-element.16) | copy-start | bytes 3145732
  9.4 8.5 %copy-start.1 = (bf16[128,2048]{1,0:T(8,128)(2,1)S(1)}, bf16[128,2048]{1,0:T(8,128)(2,1)}, u32[]{:S(2)}) copy-start(bf16[128,2048]{1,0:T(8,128)(2,1)} %q_hbm.3) | copy-start | bytes 1572868
  9.5 8.5 %copy-start.3 = (bf16[128,2048]{1,0:T(8,128)(2,1)S(1)}, bf16[128,2048]{1,0:T(8,128)(2,1)}, u32[]{:S(2)}) copy-start(bf16[128,2048]{1,0:T(8,128)(2,1)} %k_hbm.3) | copy-start | bytes 1572868
  9.5 8.5 %copy-start.5 = (bf16[128,2048]{1,0:T(8,128)(2,1)S(1)}, bf16[128,2048]{1,0:T(8,128)(2,1)}, u32[]{:S(2)}) copy-start(bf16[128,2048]{1,0:T(8,128)(2,1)} %v_hbm.3) | copy-start | bytes 1572868
  9.5 34.1 %all-to-all-start = ((bf16[16,4,64,128]{3,2,1,0:T(8,128)(2,1)}), bf16[16,4,64,128]{3,2,1,0:T(8,128)(2,1)S(1)}, u32[]{:S(2)}, u32[]{:S(2)}) async-start(bf16[16,4,64,128]{3,2,1,0:T(8,128)(2,1)} %copy-done.6), calls=%async_computation | async-start | bytes 2097152 | tf_op jit(solution)/shard_map/all_to_all | solution.py:363
  17.9 3.9 %copy-start.7 = (s32[32,32,32]{2,1,0:T(8,128)S(1)}, s32[32,32,32]{2,1,0:T(8,128)}, u32[]{:S(2)}) copy-start(s32[32,32,32]{2,1,0:T(8,128)} %layout_ref.1) | copy-start | bytes 393220
  17.9 3.9 %copy-start.9 = (s32[32,32]{1,0:T(8,128)S(1)}, s32[32,32]{1,0:T(8,128)}, u32[]{:S(2)}) copy-start(s32[32,32]{1,0:T(8,128)} %counts_ref.3) | copy-start | bytes 12292
  43.6 4.0 %collective-permute-start = (bf16[16,4,64,128]{3,2,1,0:T(8,128)(2,1)S(1)}, bf16[16,4,64,128]{3,2,1,0:T(8,128)(2,1)S(1)}, u32[]{:S(2)}, u32[]{:S(2)}) collective-permute-start(bf16[16,4,64,128]{3,2,1,0:T(8,128)(2,1)S(1)} %all-to-all-done.refs_0_.refs_2_), channel_id=1, source_target_pairs={{0,1},{1,0},{2,3},{3,2},{4,5},{5,4},{6,7},{7,6},{8,9},{9,8},{10,11... | collective-permute-start | bytes 3145736 | tf_op jit(solution)/shard_map/ppermute | solution.py:361
  43.6 19.2 %all-to-all-start.1 = ((bf16[16,2,64,128]{3,2,1,0:T(8,128)(2,1)}), bf16[16,2,64,128]{3,2,1,0:T(8,128)(2,1)S(1)}, u32[]{:S(2)}, u32[]{:S(2)}) async-start(bf16[16,2,64,128]{3,2,1,0:T(8,128)(2,1)} %pack.3), calls=%async_computation.1 | async-start | bytes 1048576 | tf_op jit(solution)/shard_map/all_to_all | solution.py:369
  62.8 1.9 %collective-permute-start.1 = (bf16[16,2,64,128]{3,2,1,0:T(8,128)(2,1)S(1)}, bf16[16,2,64,128]{3,2,1,0:T(8,128)(2,1)S(1)}, u32[]{:S(2)}, u32[]{:S(2)}) collective-permute-start(bf16[16,2,64,128]{3,2,1,0:T(8,128)(2,1)S(1)} %all-to-all-done.1.refs_0_), channel_id=1, source_target_pairs={{0,1},{1,0},{2,3},{3,2},{4,5},{5,4},{6,7},{7,6},{8,9},{9,8},{10,11... | collective-permute-start | bytes 1572872 | tf_op jit(solution)/shard_map/ppermute | solution.py:361

commit v8 on v7

--- a/solution.py
+++ b/solution.py
@@ -87,8 +87,13 @@
     return copies
 
 
-def pack_first_kernel(groups, counts_ref, q_hbm, k_hbm, v_hbm, table_ref, out_hbm, q_ref, k_ref, v_ref, sems, table_vmem, sem, out_ref, out_sem):
+def pack_first_kernel(
+    groups, counts_hbm, q_hbm, k_hbm, v_hbm, table_ref, out_hbm, q_ref, k_ref, v_ref, sems, counts_ref, table_vmem, sem, out_ref, out_sem
+):
+    fetch = pltpu.make_async_copy(counts_hbm, counts_ref, sem)
+    fetch.start()
     copies = load((k_hbm, v_hbm, q_hbm), (k_ref, v_ref, q_ref), sems)
+    fetch.wait()
     rank_heads(counts_ref, table_vmem, groups)
     copy = pltpu.make_async_copy(table_vmem, table_ref, sem)
     copy.start()
@@ -301,15 +306,19 @@
     groups = uly * parts
     slots = H // groups
     shape = jax.ShapeDtypeStruct
+    queries, key_vectors, value_vectors = (
+        pltpu.with_memory_space_constraint(array, pltpu.HBM) for array in (queries, key_vectors, value_vectors)
+    )
     slot_tiles = [2 + (slot == 0) + (slot + 1 < slots) for slot in range(slots)]
     held = [pltpu.VMEM(queries.shape, BF16)] * 3 + [pltpu.SemaphoreType.DMA((3, 4))]
     table, first = pl.pallas_call(
         functools.partial(pack_first_kernel, groups),
-        out_shape=(shape((8, 128), jnp.int32), shape((groups, slot_tiles[0], DH, BLK), BF16)),
-        in_specs=[VMEM] + [HBM] * 3,
+        out_shape=(shape((8, 128), jnp.int32), pltpu.HBM((groups, slot_tiles[0], DH, BLK), BF16)),
+        in_specs=[HBM] * 4,
         out_specs=(SMEM, HBM),
         scratch_shapes=[
             *held,
+            pltpu.VMEM(counts.shape, jnp.int32),
             pltpu.VMEM((8, 128), jnp.int32),
             pltpu.SemaphoreType.DMA,
             pltpu.VMEM((slot_tiles[0], groups, DH, BLK), BF16),
@@ -317,7 +326,7 @@
         ],
         compiler_params=PARAMS,
         name="pack",
-    )(counts, queries, key_vectors, value_vectors)
+    )(pltpu.with_memory_space_constraint(counts, pltpu.HBM), queries, key_vectors, value_vectors)
     packed = [first]
     for slot in range(1, slots):
         packed.append(

time: 90.2 us -> 85.8 us (0.951)
  local copies, waits for them, and re-layouts: 4.84 us -> 0.01 us
    unnamed x20 -> x4, local copies, waits for them, and re-layouts: 4.84 us -> 0.01 us
  transfers between devices with their start and end apart: 4 -> 4, of which waited for: 3 -> 2; matrix products, arithmetic and copies ran while one was open for 0% -> 0% of each run, Pallas kernels for 37% -> 38%
where the time goes in v8:
time: 85.8 us; the launch traced here: 85.5 us
  Pallas kernels  42.6 us (50%)
  blocking collectives  20.2 us (24%)
  starting transfers between devices  12.4 us (14%)
  waiting for transfers between devices  10.2 us (12%)
    all_to_all x1, blocking collectives, shards(): swap(results[-1])  20.2 us
    pallas_call x2, Pallas kernels, shards(): pl.pallas_call(functools.partial(attend_kernel, slot, gather), out_shape=...  19.2 us
    pallas_call x1, Pallas kernels, shards(): pl.pallas_call(functools.partial(plan_kernel, uly, gather), out_shape=(sh...  14 us
    all_to_all x1, starting transfers between devices, shards(): arrived = swap(packed[0])  8.32 us
    all_to_all x1, waiting for transfers between devices, shards(): arrived = swap(packed[0])  8.32 us
    pallas_call x1, Pallas kernels, shards(): pl.pallas_call(functools.partial(pack_first_kernel, groups), out_shape=(s...  4.44 us
    all_to_all x1, starting transfers between devices, shards(): arrived, *results = lax.optimization_barrier((swap(packed[slot]), *results))  3.98 us
    pallas_call x1, Pallas kernels, shards(): pl.pallas_call(functools.partial(pack_rest_kernel, slot), out_shape=pltpu...  3.29 us
  transfers between devices with their start and end apart: 4, of which 2 were waited for; matrix products, arithmetic and copies ran while one was open for 0% of the time, Pallas kernels for 38%

profile of v8, /device:TPU:0, one launch (start us, length us, event | category | flops | bytes accessed | tf_op | source)
XLA Modules:
  0.0 85.5 jit_solution(99210994940866111)
XLA Ops:
  0.0 4.4 %pack.2 = (s32[8,128]{1,0:T(8,128)S(1)}, bf16[16,4,64,128]{3,2,1,0:T(8,128)(2,1)}) custom-call(s32[32,32]{1,0:T(8,128)} %counts_ref.1, bf16[128,2048]{1,0:T(8,128)(2,1)} %q_hbm.3, bf16[128,2048]{1,0:T(8,128)(2,1)} %k_hbm.3, bf16[128,2048]{1,0:T(8,128)(2,1)} %v_hbm.3), custom_call_target="tpu_custom_call" | custom-call | tf_op jit(solution)/shard_map/pack/pallas_call | solution.py:314
  4.4 8.3 %all-to-all-start = ((bf16[16,4,64,128]{3,2,1,0:T(8,128)(2,1)}), bf16[16,4,64,128]{3,2,1,0:T(8,128)(2,1)S(1)}, u32[]{:S(2)}, u32[]{:S(2)}) async-start(bf16[16,4,64,128]{3,2,1,0:T(8,128)(2,1)} %get-tuple-element.16), calls=%async_computation | async-start | bytes 2097152 | tf_op jit(solution)/shard_map/all_to_all | solution.py:372
  12.8 0.0 copy-start
  12.8 0.0 copy-start.1
  12.8 3.3 %pack.3 = bf16[16,2,64,128]{3,2,1,0:T(8,128)(2,1)} custom-call(s32[8,128]{1,0:T(8,128)S(1)} %get-tuple-element.15.table_ref, bf16[128,2048]{1,0:T(8,128)(2,1)} %q_hbm.3, bf16[128,2048]{1,0:T(8,128)(2,1)} %k_hbm.3, bf16[128,2048]{1,0:T(8,128)(2,1)} %v_hbm.3), custom_call_target="tpu_custom_call" | custom-call | tf_op jit(solution)/shard_map/pack/pallas_call | solution.py:333
  16.1 0.0 copy-done
  16.1 0.0 copy-done.1
  16.1 14.0 %plan.1 = (s32[2,4,288]{2,1,0:T(4,128)S(1)}, s32[2]{0:T(128)S(1)}) custom-call(s32[8,128]{1,0:T(8,128)S(1)} %get-tuple-element.15.table_ref, s32[32,32]{1,0:T(8,128)S(1)} %copy-done.1, s32[32,32,32]{2,1,0:T(8,128)S(1)} %copy-done), custom_call_target="tpu_custom_call" | custom-call | tf_op jit(solution)/shard_map/plan/pallas_call | solution.py:343
  30.1 8.3 %all-to-all-done.refs_0_.refs_2_ = bf16[16,4,64,128]{3,2,1,0:T(8,128)(2,1)S(1)} async-done(((bf16[16,4,64,128]{3,2,1,0:T(8,128)(2,1)}), bf16[16,4,64,128]{3,2,1,0:T(8,128)(2,1)S(1)}, u32[]{:S(2)}, u32[]{:S(2)}) %all-to-all-start) | async-done | bytes 1048608 | tf_op jit(solution)/shard_map/all_to_all | solution.py:372
  38.4 0.0 collective-permute-start
  38.5 4.0 %all-to-all-start.1 = ((bf16[16,2,64,128]{3,2,1,0:T(8,128)(2,1)}), bf16[16,2,64,128]{3,2,1,0:T(8,128)(2,1)S(1)}, u32[]{:S(2)}, u32[]{:S(2)}) async-start(bf16[16,2,64,128]{3,2,1,0:T(8,128)(2,1)} %pack.3), calls=%async_computation.1 | async-start | bytes 1048576 | tf_op jit(solution)/shard_map/all_to_all | solution.py:378
  42.4 0.0 collective-permute-done.refs_1_.refs_3_
  42.5 15.3 %attend.2.refs_4_ = bf16[16,64,128]{2,1,0:T(8,128)(2,1)S(1)} custom-call(s32[2,4,288]{2,1,0:T(4,128)S(1)} %get-tuple-element.19.unit_ref, s32[2]{0:T(128)S(1)} %get-tuple-element.20.total_ref, bf16[16,4,64,128]{3,2,1,0:T(8,128)(2,1)S(1)} %all-to-all-done.refs_0_.refs_2_, bf16[16,4,64,128]{3,2,1,0:T(8,128)(2,1)S(1)} %collective-permute-done.refs_1_.refs_3_), custom_call_target="tpu_custom_call" | custom-call | flops 10000000000 | bytes 6000000 | tf_op jit(solution)/shard_map/attend/pallas_call | solution.py:388
  57.7 0.0 all-to-all-done.1.refs_0_
  57.7 0.1 collective-permute-start.1
  57.8 1.9 %collective-permute-done.1.refs_1_ = bf16[16,2,64,128]{3,2,1,0:T(8,128)(2,1)S(1)} collective-permute-done((bf16[16,2,64,128]{3,2,1,0:T(8,128)(2,1)S(1)}, bf16[16,2,64,128]{3,2,1,0:T(8,128)(2,1)S(1)}, u32[]{:S(2)}, u32[]{:S(2)}) %collective-permute-start.1) | collective-permute-done | bytes 524320 | tf_op jit(solution)/shard_map/ppermute | solution.py:370
  59.7 4.0 %attend.3 = bf16[16,2,64,128]{3,2,1,0:T(8,128)(2,1)S(1)} custom-call(s32[2,4,288]{2,1,0:T(4,128)S(1)} %get-tuple-element.19.unit_ref, s32[2]{0:T(128)S(1)} %get-tuple-element.20.total_ref, bf16[16,2,64,128]{3,2,1,0:T(8,128)(2,1)S(1)} %all-to-all-done.1.refs_0_, bf16[16,2,64,128]{3,2,1,0:T(8,128)(2,1)S(1)} %collective-permute-done.1.refs_1_, ...), custom_call_target="tpu_custom_call" | custom-call | flops 10000000000 | bytes 6000000 | tf_op jit(solution)/shard_map/attend/pallas_call | solution.py:388
  63.7 20.2 %all_to_all.15.o_ref = bf16[16,2,64,128]{3,2,1,0:T(8,128)(2,1)S(1)} all-to-all(bf16[16,2,64,128]{3,2,1,0:T(8,128)(2,1)S(1)} %attend.3), channel_id=1, replica_groups={{0,16,8,24,4,20,12,28,2,18,10,26,6,22,14,30},{1,17,9,25,5,21,13,29,3,19..., dimensions={0} | all-to-all | bytes 1048576 | tf_op jit(solution)/shard_map/all_to_all | solution.py:413
  83.8 1.7 %unpack.1 = bf16[128,2048]{1,0:T(8,128)(2,1)} custom-call(s32[8,128]{1,0:T(8,128)S(1)} %get-tuple-element.15.table_ref, bf16[16,2,64,128]{3,2,1,0:T(8,128)(2,1)S(1)} %all_to_all.15.o_ref), custom_call_target="tpu_custom_call" | custom-call | tf_op jit(solution)/shard_map/unpack/pallas_call | solution.py:406
Async XLA Ops:
  4.4 34.0 %all-to-all-start = ((bf16[16,4,64,128]{3,2,1,0:T(8,128)(2,1)}), bf16[16,4,64,128]{3,2,1,0:T(8,128)(2,1)S(1)}, u32[]{:S(2)}, u32[]{:S(2)}) async-start(bf16[16,4,64,128]{3,2,1,0:T(8,128)(2,1)} %get-tuple-element.16), calls=%async_computation | async-start | bytes 2097152 | tf_op jit(solution)/shard_map/all_to_all | solution.py:372
  12.8 3.3 %copy-start = (s32[32,32,32]{2,1,0:T(8,128)S(1)}, s32[32,32,32]{2,1,0:T(8,128)}, u32[]{:S(2)}) copy-start(s32[32,32,32]{2,1,0:T(8,128)} %layout_ref.1) | copy-start | bytes 393220
  12.8 3.3 %copy-start.1 = (s32[32,32]{1,0:T(8,128)S(1)}, s32[32,32]{1,0:T(8,128)}, u32[]{:S(2)}) copy-start(s32[32,32]{1,0:T(8,128)} %counts_ref.1) | copy-start | bytes 12292
  38.4 4.0 %collective-permute-start = (bf16[16,4,64,128]{3,2,1,0:T(8,128)(2,1)S(1)}, bf16[16,4,64,128]{3,2,1,0:T(8,128)(2,1)S(1)}, u32[]{:S(2)}, u32[]{:S(2)}) collective-permute-start(bf16[16,4,64,128]{3,2,1,0:T(8,128)(2,1)S(1)} %all-to-all-done.refs_0_.refs_2_), channel_id=1, source_target_pairs={{0,1},{1,0},{2,3},{3,2},{4,5},{5,4},{6,7},{7,6},{8,9},{9,8},{10,11... | collective-permute-start | bytes 3145736 | tf_op jit(solution)/shard_map/ppermute | solution.py:370
  38.5 19.3 %all-to-all-start.1 = ((bf16[16,2,64,128]{3,2,1,0:T(8,128)(2,1)}), bf16[16,2,64,128]{3,2,1,0:T(8,128)(2,1)S(1)}, u32[]{:S(2)}, u32[]{:S(2)}) async-start(bf16[16,2,64,128]{3,2,1,0:T(8,128)(2,1)} %pack.3), calls=%async_computation.1 | async-start | bytes 1048576 | tf_op jit(solution)/shard_map/all_to_all | solution.py:378
  57.7 2.0 %collective-permute-start.1 = (bf16[16,2,64,128]{3,2,1,0:T(8,128)(2,1)S(1)}, bf16[16,2,64,128]{3,2,1,0:T(8,128)(2,1)S(1)}, u32[]{:S(2)}, u32[]{:S(2)}) collective-permute-start(bf16[16,2,64,128]{3,2,1,0:T(8,128)(2,1)S(1)} %all-to-all-done.1.refs_0_), channel_id=1, source_target_pairs={{0,1},{1,0},{2,3},{3,2},{4,5},{5,4},{6,7},{7,6},{8,9},{9,8},{10,11... | collective-permute-start | bytes 1572872 | tf_op jit(solution)/shard_map/ppermute | solution.py:370

commit v9 on v8

--- a/solution.py
+++ b/solution.py
@@ -11,7 +11,7 @@
 DH = 64
 BLK = 128
 KMAX = 32
-UNROLL = 4
+UNROLL = 6
 BIG = 1e30
 F32 = jnp.float32
 BF16 = jnp.bfloat16
@@ -271,7 +271,6 @@
             chunk = 2 * index + side
             for lane in range(UNROLL):
                 merge(chunk * UNROLL + lane, lane, side)
-            for lane in range(UNROLL):
                 make_scores((chunk + 2) * UNROLL + lane, lane, side)
                 make_output((chunk + 1) * UNROLL + lane, lane, 1 - side)
         return 0

time: 85.8 us -> 84.5 us (0.985)
  Pallas kernels: 42.6 us -> 39.5 us
  waiting for transfers between devices: 10.2 us -> 12.8 us
    pallas_call x2, Pallas kernels: 19.2 us -> 16.5 us  [shards(): pl.pallas_call(functools.partial(attend_kernel, slot, gather), out_shape=...]
    all_to_all x1, waiting for transfers between devices: 0.01 us -> 2.14 us  [shards(): arrived, *results = lax.optimization_barrier((swap(packed[slot]), *results))]
  transfers between devices with their start and end apart: 4 -> 4, of which waited for: 2 -> 3; matrix products, arithmetic and copies ran while one was open for 0% -> 0% of each run, Pallas kernels for 38% -> 36%
where the time goes in v9:
time: 84.5 us; the launch traced here: 84.1 us
  Pallas kernels  39.5 us (47%)
  blocking collectives  19.4 us (23%)
  waiting for transfers between devices  12.8 us (15%)
  starting transfers between devices  12.3 us (15%)
    all_to_all x1, blocking collectives, shards(): swap(results[-1])  19.4 us
    pallas_call x2, Pallas kernels, shards(): pl.pallas_call(functools.partial(attend_kernel, slot, gather), out_shape=...  16.5 us
    pallas_call x1, Pallas kernels, shards(): pl.pallas_call(functools.partial(plan_kernel, uly, gather), out_shape=(sh...  13.6 us
    all_to_all x1, waiting for transfers between devices, shards(): arrived = swap(packed[0])  8.75 us
    all_to_all x1, starting transfers between devices, shards(): arrived = swap(packed[0])  8.32 us
    pallas_call x1, Pallas kernels, shards(): pl.pallas_call(functools.partial(pack_first_kernel, groups), out_shape=(s...  4.44 us
    all_to_all x1, starting transfers between devices, shards(): arrived, *results = lax.optimization_barrier((swap(packed[slot]), *results))  3.98 us
    pallas_call x1, Pallas kernels, shards(): pl.pallas_call(functools.partial(pack_rest_kernel, slot), out_shape=pltpu...  3.29 us
  transfers between devices with their start and end apart: 4, of which 3 were waited for; matrix products, arithmetic and copies ran while one was open for 0% of the time, Pallas kernels for 36%

profile of v9, /device:TPU:0, one launch (start us, length us, event | category | flops | bytes accessed | tf_op | source)
XLA Modules:
  0.0 84.1 jit_solution(17614058860905895824)
XLA Ops:
  0.0 4.4 %pack.2 = (s32[8,128]{1,0:T(8,128)S(1)}, bf16[16,4,64,128]{3,2,1,0:T(8,128)(2,1)}) custom-call(s32[32,32]{1,0:T(8,128)} %counts_ref.1, bf16[128,2048]{1,0:T(8,128)(2,1)} %q_hbm.3, bf16[128,2048]{1,0:T(8,128)(2,1)} %k_hbm.3, bf16[128,2048]{1,0:T(8,128)(2,1)} %v_hbm.3), custom_call_target="tpu_custom_call" | custom-call | tf_op jit(solution)/shard_map/pack/pallas_call | solution.py:313
  4.4 8.3 %all-to-all-start = ((bf16[16,4,64,128]{3,2,1,0:T(8,128)(2,1)}), bf16[16,4,64,128]{3,2,1,0:T(8,128)(2,1)S(1)}, u32[]{:S(2)}, u32[]{:S(2)}) async-start(bf16[16,4,64,128]{3,2,1,0:T(8,128)(2,1)} %get-tuple-element.16), calls=%async_computation | async-start | bytes 2097152 | tf_op jit(solution)/shard_map/all_to_all | solution.py:371
  12.8 0.0 copy-start
  12.8 0.0 copy-start.1
  12.8 3.3 %pack.3 = bf16[16,2,64,128]{3,2,1,0:T(8,128)(2,1)} custom-call(s32[8,128]{1,0:T(8,128)S(1)} %get-tuple-element.15.table_ref, bf16[128,2048]{1,0:T(8,128)(2,1)} %q_hbm.3, bf16[128,2048]{1,0:T(8,128)(2,1)} %k_hbm.3, bf16[128,2048]{1,0:T(8,128)(2,1)} %v_hbm.3), custom_call_target="tpu_custom_call" | custom-call | tf_op jit(solution)/shard_map/pack/pallas_call | solution.py:332
  16.1 0.0 copy-done
  16.1 0.0 copy-done.1
  16.1 13.6 %plan.1 = (s32[2,4,304]{2,1,0:T(4,128)S(1)}, s32[2]{0:T(128)S(1)}) custom-call(s32[8,128]{1,0:T(8,128)S(1)} %get-tuple-element.15.table_ref, s32[32,32]{1,0:T(8,128)S(1)} %copy-done.1, s32[32,32,32]{2,1,0:T(8,128)S(1)} %copy-done), custom_call_target="tpu_custom_call" | custom-call | tf_op jit(solution)/shard_map/plan/pallas_call | solution.py:342
  29.7 8.8 %all-to-all-done.refs_0_.refs_2_ = bf16[16,4,64,128]{3,2,1,0:T(8,128)(2,1)S(1)} async-done(((bf16[16,4,64,128]{3,2,1,0:T(8,128)(2,1)}), bf16[16,4,64,128]{3,2,1,0:T(8,128)(2,1)S(1)}, u32[]{:S(2)}, u32[]{:S(2)}) %all-to-all-start) | async-done | bytes 1048608 | tf_op jit(solution)/shard_map/all_to_all | solution.py:371
  38.4 0.0 collective-permute-start
  38.5 4.0 %all-to-all-start.1 = ((bf16[16,2,64,128]{3,2,1,0:T(8,128)(2,1)}), bf16[16,2,64,128]{3,2,1,0:T(8,128)(2,1)S(1)}, u32[]{:S(2)}, u32[]{:S(2)}) async-start(bf16[16,2,64,128]{3,2,1,0:T(8,128)(2,1)} %pack.3), calls=%async_computation.1 | async-start | bytes 1048576 | tf_op jit(solution)/shard_map/all_to_all | solution.py:377
  42.4 0.0 collective-permute-done.refs_1_.refs_3_
  42.5 13.1 %attend.2.refs_4_ = bf16[16,64,128]{2,1,0:T(8,128)(2,1)S(1)} custom-call(s32[2,4,304]{2,1,0:T(4,128)S(1)} %get-tuple-element.19.unit_ref, s32[2]{0:T(128)S(1)} %get-tuple-element.20.total_ref, bf16[16,4,64,128]{3,2,1,0:T(8,128)(2,1)S(1)} %all-to-all-done.refs_0_.refs_2_, bf16[16,4,64,128]{3,2,1,0:T(8,128)(2,1)S(1)} %collective-permute-done.refs_1_.refs_3_), custom_call_target="tpu_custom_call" | custom-call | flops 10000000000 | bytes 6000000 | tf_op jit(solution)/shard_map/attend/pallas_call | solution.py:387
  55.6 2.1 %all-to-all-done.1.refs_0_ = bf16[16,2,64,128]{3,2,1,0:T(8,128)(2,1)S(1)} async-done(((bf16[16,2,64,128]{3,2,1,0:T(8,128)(2,1)}), bf16[16,2,64,128]{3,2,1,0:T(8,128)(2,1)S(1)}, u32[]{:S(2)}, u32[]{:S(2)}) %all-to-all-start.1) | async-done | bytes 524320 | tf_op jit(solution)/shard_map/all_to_all | solution.py:377
  57.7 0.0 collective-permute-start.1
  57.7 1.9 %collective-permute-done.1.refs_1_ = bf16[16,2,64,128]{3,2,1,0:T(8,128)(2,1)S(1)} collective-permute-done((bf16[16,2,64,128]{3,2,1,0:T(8,128)(2,1)S(1)}, bf16[16,2,64,128]{3,2,1,0:T(8,128)(2,1)S(1)}, u32[]{:S(2)}, u32[]{:S(2)}) %collective-permute-start.1) | collective-permute-done | bytes 524320 | tf_op jit(solution)/shard_map/ppermute | solution.py:369
  59.6 3.4 %attend.3 = bf16[16,2,64,128]{3,2,1,0:T(8,128)(2,1)S(1)} custom-call(s32[2,4,304]{2,1,0:T(4,128)S(1)} %get-tuple-element.19.unit_ref, s32[2]{0:T(128)S(1)} %get-tuple-element.20.total_ref, bf16[16,2,64,128]{3,2,1,0:T(8,128)(2,1)S(1)} %all-to-all-done.1.refs_0_, bf16[16,2,64,128]{3,2,1,0:T(8,128)(2,1)S(1)} %collective-permute-done.1.refs_1_, ...), custom_call_target="tpu_custom_call" | custom-call | flops 10000000000 | bytes 6000000 | tf_op jit(solution)/shard_map/attend/pallas_call | solution.py:387
  63.0 19.4 %all_to_all.15.o_ref = bf16[16,2,64,128]{3,2,1,0:T(8,128)(2,1)S(1)} all-to-all(bf16[16,2,64,128]{3,2,1,0:T(8,128)(2,1)S(1)} %attend.3), channel_id=1, replica_groups={{0,16,8,24,4,20,12,28,2,18,10,26,6,22,14,30},{1,17,9,25,5,21,13,29,3,19..., dimensions={0} | all-to-all | bytes 1048576 | tf_op jit(solution)/shard_map/all_to_all | solution.py:412
  82.5 1.7 %unpack.1 = bf16[128,2048]{1,0:T(8,128)(2,1)} custom-call(s32[8,128]{1,0:T(8,128)S(1)} %get-tuple-element.15.table_ref, bf16[16,2,64,128]{3,2,1,0:T(8,128)(2,1)S(1)} %all_to_all.15.o_ref), custom_call_target="tpu_custom_call" | custom-call | tf_op jit(solution)/shard_map/unpack/pallas_call | solution.py:405
Async XLA Ops:
  4.4 34.0 %all-to-all-start = ((bf16[16,4,64,128]{3,2,1,0:T(8,128)(2,1)}), bf16[16,4,64,128]{3,2,1,0:T(8,128)(2,1)S(1)}, u32[]{:S(2)}, u32[]{:S(2)}) async-start(bf16[16,4,64,128]{3,2,1,0:T(8,128)(2,1)} %get-tuple-element.16), calls=%async_computation | async-start | bytes 2097152 | tf_op jit(solution)/shard_map/all_to_all | solution.py:371
  12.8 3.3 %copy-start = (s32[32,32,32]{2,1,0:T(8,128)S(1)}, s32[32,32,32]{2,1,0:T(8,128)}, u32[]{:S(2)}) copy-start(s32[32,32,32]{2,1,0:T(8,128)} %layout_ref.1) | copy-start | bytes 393220
  12.8 3.3 %copy-start.1 = (s32[32,32]{1,0:T(8,128)S(1)}, s32[32,32]{1,0:T(8,128)}, u32[]{:S(2)}) copy-start(s32[32,32]{1,0:T(8,128)} %counts_ref.1) | copy-start | bytes 12292
  38.4 4.0 %collective-permute-start = (bf16[16,4,64,128]{3,2,1,0:T(8,128)(2,1)S(1)}, bf16[16,4,64,128]{3,2,1,0:T(8,128)(2,1)S(1)}, u32[]{:S(2)}, u32[]{:S(2)}) collective-permute-start(bf16[16,4,64,128]{3,2,1,0:T(8,128)(2,1)S(1)} %all-to-all-done.refs_0_.refs_2_), channel_id=1, source_target_pairs={{0,1},{1,0},{2,3},{3,2},{4,5},{5,4},{6,7},{7,6},{8,9},{9,8},{10,11... | collective-permute-start | bytes 3145736 | tf_op jit(solution)/shard_map/ppermute | solution.py:369
  38.5 19.2 %all-to-all-start.1 = ((bf16[16,2,64,128]{3,2,1,0:T(8,128)(2,1)}), bf16[16,2,64,128]{3,2,1,0:T(8,128)(2,1)S(1)}, u32[]{:S(2)}, u32[]{:S(2)}) async-start(bf16[16,2,64,128]{3,2,1,0:T(8,128)(2,1)} %pack.3), calls=%async_computation.1 | async-start | bytes 1048576 | tf_op jit(solution)/shard_map/all_to_all | solution.py:377
  57.7 1.9 %collective-permute-start.1 = (bf16[16,2,64,128]{3,2,1,0:T(8,128)(2,1)S(1)}, bf16[16,2,64,128]{3,2,1,0:T(8,128)(2,1)S(1)}, u32[]{:S(2)}, u32[]{:S(2)}) collective-permute-start(bf16[16,2,64,128]{3,2,1,0:T(8,128)(2,1)S(1)} %all-to-all-done.1.refs_0_), channel_id=1, source_target_pairs={{0,1},{1,0},{2,3},{3,2},{4,5},{5,4},{6,7},{7,6},{8,9},{9,8},{10,11... | collective-permute-start | bytes 1572872 | tf_op jit(solution)/shard_map/ppermute | solution.py:369

commit v10 on v9

--- a/solution.py
+++ b/solution.py
@@ -87,29 +87,15 @@
     return copies
 
 
-def pack_first_kernel(
-    groups, counts_hbm, q_hbm, k_hbm, v_hbm, table_ref, out_hbm, q_ref, k_ref, v_ref, sems, counts_ref, table_vmem, sem, out_ref, out_sem
-):
-    fetch = pltpu.make_async_copy(counts_hbm, counts_ref, sem)
-    fetch.start()
-    copies = load((k_hbm, v_hbm, q_hbm), (k_ref, v_ref, q_ref), sems)
-    fetch.wait()
+def pack_first_kernel(groups, counts_ref, q_ref, k_ref, v_ref, table_ref, out_ref, table_vmem, sem):
     rank_heads(counts_ref, table_vmem, groups)
     copy = pltpu.make_async_copy(table_vmem, table_ref, sem)
     copy.start()
     copy.wait()
-    leave = []
-    for which, source, places in ((0, k_ref, ((2, 0), (3, 1))), (1, v_ref, ((0, 0),)), (2, q_ref, ((1, 0),))):
-        for copy in copies[which]:
-            copy.wait()
-        for at, slot in places:
-            if at < out_ref.shape[0]:
-                for group in range(groups):
-                    out_ref[at, group] = fold_head(source, table_ref[0, slot * groups + group])
-                leave.append(pltpu.make_async_copy(out_ref.at[at], out_hbm.at[:, at], out_sem.at[at]))
-                leave[-1].start()
-    for copy in leave:
-        copy.wait()
+    for group in range(groups):
+        head = table_ref[0, group]
+        for at, source in enumerate((v_ref, q_ref, k_ref)):
+            out_ref[group, at] = fold_head(source, head)
 
 
 def pack_rest_kernel(slot, table_ref, q_hbm, k_hbm, v_hbm, out_ref, q_ref, k_ref, v_ref, sems, turned_q, turned_v):
@@ -119,13 +105,12 @@
             copy.wait()
     turn_heads(q_ref, turned_q)
     turn_heads(v_ref, turned_v)
-    groups, tiles = out_ref.shape[:2]
+    groups = out_ref.shape[0]
     for group in range(groups):
         head = table_ref[0, slot * groups + group]
         out_ref[group, 0] = turned_v[head]
         out_ref[group, 1] = turned_q[head]
-        if tiles > 2:
-            out_ref[group, 2] = fold_head(k_ref, table_ref[0, (slot + 1) * groups + group])
+        out_ref[group, 2] = fold_head(k_ref, head)
 
 
 def mirror(value, size):
@@ -198,8 +183,6 @@
 
 def attend_kernel(slot, gather, unit_ref, total_ref, *refs):
     arrived, refs = refs[:gather], refs[gather:]
-    before, refs = (refs[:gather], refs[gather:]) if slot else (arrived, refs)
-    key_at = 3 if slot == 1 else 2
     earlier, refs = refs[:slot], refs[slot:]
     out_ref, kv_ref, qz_ref, m_ref, l_ref, acc_ref = refs[:6]
     score, top_of, out_of, sum_of = (refs[6 + 2 * at : 8 + 2 * at] for at in range(4))
@@ -219,10 +202,10 @@
         for at, part in enumerate(turn_folded(*pair) if slot == 0 else pair):
             put_query(row + at, part)
     qz_ref[rows] = jnp.zeros((2 * DH, 2 * BLK), BF16)
-    for at, (array, keys) in enumerate(zip(arrived, before)):
+    for at, array in enumerate(arrived):
         for row in range(0, rows, 2):
             place = at * rows + row
-            kv_ref[place, 0], kv_ref[place + 1, 0] = keys[row, key_at], keys[row + 1, key_at]
+            kv_ref[place, 0], kv_ref[place + 1, 0] = array[row, 2], array[row + 1, 2]
             pair = [array[row, 0], array[row + 1, 0]]
             kv_ref[place, 1], kv_ref[place + 1, 1] = turn_folded(*pair) if slot == 0 else pair
     for at, result in enumerate(earlier):
@@ -279,7 +262,7 @@
     lax.fori_loop(0, (chunks + 1) // 2, step, 0)
     for row in range(rows):
         total_w = jnp.sum(l_ref[row], axis=0, keepdims=True)
-        result = (acc_ref[row] / total_w).astype(BF16)
+        result = (acc_ref[row] * (1.0 / total_w)).astype(BF16)
         if len(out_ref.shape) == 4:
             out_ref[row, slot] = result
         else:
@@ -308,21 +291,14 @@
     queries, key_vectors, value_vectors = (
         pltpu.with_memory_space_constraint(array, pltpu.HBM) for array in (queries, key_vectors, value_vectors)
     )
-    slot_tiles = [2 + (slot == 0) + (slot + 1 < slots) for slot in range(slots)]
+    packed_shape = pltpu.HBM((groups, 3, DH, BLK), BF16)
     held = [pltpu.VMEM(queries.shape, BF16)] * 3 + [pltpu.SemaphoreType.DMA((3, 4))]
     table, first = pl.pallas_call(
         functools.partial(pack_first_kernel, groups),
-        out_shape=(shape((8, 128), jnp.int32), pltpu.HBM((groups, slot_tiles[0], DH, BLK), BF16)),
-        in_specs=[HBM] * 4,
-        out_specs=(SMEM, HBM),
-        scratch_shapes=[
-            *held,
-            pltpu.VMEM(counts.shape, jnp.int32),
-            pltpu.VMEM((8, 128), jnp.int32),
-            pltpu.SemaphoreType.DMA,
-            pltpu.VMEM((slot_tiles[0], groups, DH, BLK), BF16),
-            pltpu.SemaphoreType.DMA((slot_tiles[0],)),
-        ],
+        out_shape=(shape((8, 128), jnp.int32), packed_shape),
+        in_specs=[VMEM] * 4,
+        out_specs=(SMEM, VMEM),
+        scratch_shapes=[pltpu.VMEM((8, 128), jnp.int32), pltpu.SemaphoreType.DMA],
         compiler_params=PARAMS,
         name="pack",
     )(pltpu.with_memory_space_constraint(counts, pltpu.HBM), queries, key_vectors, value_vectors)
@@ -331,7 +307,7 @@
         packed.append(
             pl.pallas_call(
                 functools.partial(pack_rest_kernel, slot),
-                out_shape=pltpu.VMEM((groups, slot_tiles[slot], DH, BLK), BF16),
+                out_shape=packed_shape,
                 in_specs=[SMEM] + [HBM] * 3,
                 out_specs=VMEM,
                 scratch_shapes=[*held] + [pltpu.VMEM((H, DH, BLK), BF16)] * 2,
@@ -370,9 +346,8 @@
 
     arrived = swap(packed[0])
     arrived, units, totals, *packed = lax.optimization_barrier((arrived, units, totals, *packed))
-    results, arrays = [], {}
+    results = []
     for slot in range(slots):
-        before = arrays if slot else {}
         if slot:
             arrived, *results = lax.optimization_barrier((swap(packed[slot]), *results))
         arrays, bit = {0: arrived}, gather // 2
@@ -387,7 +362,7 @@
             pl.pallas_call(
                 functools.partial(attend_kernel, slot, gather),
                 out_shape=pltpu.VMEM((groups, slots, DH, BLK) if last else (groups, DH, BLK), BF16),
-                in_specs=[SMEM, SMEM] + [VMEM] * (gather + len(before) + len(earlier)),
+                in_specs=[SMEM, SMEM] + [VMEM] * (gather + len(earlier)),
                 out_specs=VMEM,
                 scratch_shapes=[
                     pltpu.VMEM((gather * groups, 2, DH, BLK), BF16),
@@ -400,7 +375,7 @@
                 compiler_params=PARAMS,
                 cost_estimate=pl.CostEstimate(flops=10**10, transcendentals=6 * 10**6, bytes_accessed=6 * 10**6),
                 name="attend",
-            )(units, totals, *[hold(part[at]) for part in (arrays, before) for at in range(len(part))], *[hold(result) for result in earlier])
+            )(units, totals, *[hold(arrays[at]) for at in range(gather)], *[hold(result) for result in earlier])
         )
     return pl.pallas_call(
         unpack_kernel,

time: 84.5 us -> 83.9 us (level)
  Pallas kernels: 39.5 us -> 37.6 us
  waiting for transfers between devices: 12.8 us -> 13.9 us
    all_to_all x1, waiting for transfers between devices: 2.14 us -> 8.18 us  [shards(): arrived, *results = lax.optimization_barrier((swap(packed[slot]), *results))]
    all_to_all x1, waiting for transfers between devices: 8.75 us -> 3.42 us  [shards(): arrived = swap(packed[0])]
    pallas_call x1, Pallas kernels: 4.44 us -> 3.53 us  [shards(): pl.pallas_call(functools.partial(pack_first_kernel, groups), out_shape=(s...]
  transfers between devices with their start and end apart: 4 -> 4, of which waited for: 3 -> 3; matrix products, arithmetic and copies ran while one was open for 0% -> 0% of each run, Pallas kernels for 36% -> 35%
where the time goes in v10:
time: 83.9 us; the launch traced here: 83.5 us
  Pallas kernels  37.6 us (45%)
  blocking collectives  19.4 us (23%)
  waiting for transfers between devices  13.9 us (17%)
  starting transfers between devices  12.5 us (15%)
    all_to_all x1, blocking collectives, shards(): swap(results[-1])  19.4 us
    pallas_call x2, Pallas kernels, shards(): pl.pallas_call(functools.partial(attend_kernel, slot, gather), out_shape=...  15.9 us
    pallas_call x1, Pallas kernels, shards(): pl.pallas_call(functools.partial(plan_kernel, uly, gather), out_shape=(sh...  13 us
    all_to_all x1, starting transfers between devices, shards(): arrived = swap(packed[0])  8.32 us
    all_to_all x1, waiting for transfers between devices, shards(): arrived, *results = lax.optimization_barrier((swap(packed[slot]), *results))  8.18 us
    all_to_all x1, starting transfers between devices, shards(): arrived, *results = lax.optimization_barrier((swap(packed[slot]), *results))  4.12 us
    pallas_call x1, Pallas kernels, shards(): pl.pallas_call(functools.partial(pack_first_kernel, groups), out_shape=(s...  3.53 us
    pallas_call x1, Pallas kernels, shards(): pl.pallas_call(functools.partial(pack_rest_kernel, slot), out_shape=packe...  3.49 us
  transfers between devices with their start and end apart: 4, of which 3 were waited for; matrix products, arithmetic and copies ran while one was open for 0% of the time, Pallas kernels for 35%

profile of v10, /device:TPU:0, one launch (start us, length us, event | category | flops | bytes accessed | tf_op | source)
XLA Modules:
  0.0 83.5 jit_solution(14921594969376538282)
XLA Ops:
  0.0 3.5 %pack.2 = (s32[8,128]{1,0:T(8,128)S(1)}, bf16[16,3,64,128]{3,2,1,0:T(8,128)(2,1)}) custom-call(s32[32,32]{1,0:T(8,128)} %counts_ref.3, bf16[128,2048]{1,0:T(8,128)(2,1)} %q_hbm.1, bf16[128,2048]{1,0:T(8,128)(2,1)} %k_hbm.1, bf16[128,2048]{1,0:T(8,128)(2,1)} %v_hbm.1), custom_call_target="tpu_custom_call" | custom-call | tf_op jit(solution)/shard_map/pack/pallas_call | solution.py:296
  3.5 8.3 %all-to-all-start = ((bf16[16,3,64,128]{3,2,1,0:T(8,128)(2,1)}), bf16[16,3,64,128]{3,2,1,0:T(8,128)(2,1)S(1)}, u32[]{:S(2)}, u32[]{:S(2)}) async-start(bf16[16,3,64,128]{3,2,1,0:T(8,128)(2,1)} %get-tuple-element.16), calls=%async_computation | async-start | bytes 1572864 | tf_op jit(solution)/shard_map/all_to_all | solution.py:347
  11.9 0.0 copy-start
  11.9 0.0 copy-start.1
  11.9 3.5 %pack.3 = bf16[16,3,64,128]{3,2,1,0:T(8,128)(2,1)} custom-call(s32[8,128]{1,0:T(8,128)S(1)} %get-tuple-element.15.table_ref, bf16[128,2048]{1,0:T(8,128)(2,1)} %q_hbm.1, bf16[128,2048]{1,0:T(8,128)(2,1)} %k_hbm.1, bf16[128,2048]{1,0:T(8,128)(2,1)} %v_hbm.1), custom_call_target="tpu_custom_call" | custom-call | tf_op jit(solution)/shard_map/pack/pallas_call | solution.py:308
  15.4 0.0 copy-done
  15.4 0.0 copy-done.1
  15.4 13.0 %plan.1 = (s32[2,4,304]{2,1,0:T(4,128)S(1)}, s32[2]{0:T(128)S(1)}) custom-call(s32[8,128]{1,0:T(8,128)S(1)} %get-tuple-element.15.table_ref, s32[32,32]{1,0:T(8,128)S(1)} %copy-done.1, s32[32,32,32]{2,1,0:T(8,128)S(1)} %copy-done), custom_call_target="tpu_custom_call" | custom-call | tf_op jit(solution)/shard_map/plan/pallas_call | solution.py:318
  28.5 3.4 %all-to-all-done.refs_0_ = bf16[16,3,64,128]{3,2,1,0:T(8,128)(2,1)S(1)} async-done(((bf16[16,3,64,128]{3,2,1,0:T(8,128)(2,1)}), bf16[16,3,64,128]{3,2,1,0:T(8,128)(2,1)S(1)}, u32[]{:S(2)}, u32[]{:S(2)}) %all-to-all-start) | async-done | bytes 786464 | tf_op jit(solution)/shard_map/all_to_all | solution.py:347
  31.9 0.0 collective-permute-start
  31.9 4.1 %all-to-all-start.1 = ((bf16[16,3,64,128]{3,2,1,0:T(8,128)(2,1)}), bf16[16,3,64,128]{3,2,1,0:T(8,128)(2,1)S(1)}, u32[]{:S(2)}, u32[]{:S(2)}) async-start(bf16[16,3,64,128]{3,2,1,0:T(8,128)(2,1)} %pack.3), calls=%async_computation.1 | async-start | bytes 1572864 | tf_op jit(solution)/shard_map/all_to_all | solution.py:352
  36.0 0.0 collective-permute-done.refs_1_
  36.0 12.5 %attend.2.refs_2_ = bf16[16,64,128]{2,1,0:T(8,128)(2,1)S(1)} custom-call(s32[2,4,304]{2,1,0:T(4,128)S(1)} %get-tuple-element.19.unit_ref, s32[2]{0:T(128)S(1)} %get-tuple-element.20.total_ref, bf16[16,3,64,128]{3,2,1,0:T(8,128)(2,1)S(1)} %all-to-all-done.refs_0_, bf16[16,3,64,128]{3,2,1,0:T(8,128)(2,1)S(1)} %collective-permute-done.refs_1_), custom_call_target="tpu_custom_call" | custom-call | flops 10000000000 | bytes 6000000 | tf_op jit(solution)/shard_map/attend/pallas_call | solution.py:362
  48.5 8.2 %all-to-all-done.1.refs_0_ = bf16[16,3,64,128]{3,2,1,0:T(8,128)(2,1)S(1)} async-done(((bf16[16,3,64,128]{3,2,1,0:T(8,128)(2,1)}), bf16[16,3,64,128]{3,2,1,0:T(8,128)(2,1)S(1)}, u32[]{:S(2)}, u32[]{:S(2)}) %all-to-all-start.1) | async-done | bytes 786464 | tf_op jit(solution)/shard_map/all_to_all | solution.py:352
  56.7 0.0 collective-permute-start.1
  56.7 2.3 %collective-permute-done.1.refs_1_ = bf16[16,3,64,128]{3,2,1,0:T(8,128)(2,1)S(1)} collective-permute-done((bf16[16,3,64,128]{3,2,1,0:T(8,128)(2,1)S(1)}, bf16[16,3,64,128]{3,2,1,0:T(8,128)(2,1)S(1)}, u32[]{:S(2)}, u32[]{:S(2)}) %collective-permute-start.1) | collective-permute-done | bytes 786464 | tf_op jit(solution)/shard_map/ppermute | solution.py:345
  59.0 3.4 %attend.3 = bf16[16,2,64,128]{3,2,1,0:T(8,128)(2,1)S(1)} custom-call(s32[2,4,304]{2,1,0:T(4,128)S(1)} %get-tuple-element.19.unit_ref, s32[2]{0:T(128)S(1)} %get-tuple-element.20.total_ref, bf16[16,3,64,128]{3,2,1,0:T(8,128)(2,1)S(1)} %all-to-all-done.1.refs_0_, bf16[16,3,64,128]{3,2,1,0:T(8,128)(2,1)S(1)} %collective-permute-done.1.refs_1_, ...), custom_call_target="tpu_custom_call" | custom-call | flops 10000000000 | bytes 6000000 | tf_op jit(solution)/shard_map/attend/pallas_call | solution.py:362
  62.4 19.4 %all_to_all.15.o_ref = bf16[16,2,64,128]{3,2,1,0:T(8,128)(2,1)S(1)} all-to-all(bf16[16,2,64,128]{3,2,1,0:T(8,128)(2,1)S(1)} %attend.3), channel_id=1, replica_groups={{0,16,8,24,4,20,12,28,2,18,10,26,6,22,14,30},{1,17,9,25,5,21,13,29,3,19..., dimensions={0} | all-to-all | bytes 1048576 | tf_op jit(solution)/shard_map/all_to_all | solution.py:387
  81.8 1.7 %unpack.1 = bf16[128,2048]{1,0:T(8,128)(2,1)} custom-call(s32[8,128]{1,0:T(8,128)S(1)} %get-tuple-element.15.table_ref, bf16[16,2,64,128]{3,2,1,0:T(8,128)(2,1)S(1)} %all_to_all.15.o_ref), custom_call_target="tpu_custom_call" | custom-call | tf_op jit(solution)/shard_map/unpack/pallas_call | solution.py:380
Async XLA Ops:
  3.5 28.3 %all-to-all-start = ((bf16[16,3,64,128]{3,2,1,0:T(8,128)(2,1)}), bf16[16,3,64,128]{3,2,1,0:T(8,128)(2,1)S(1)}, u32[]{:S(2)}, u32[]{:S(2)}) async-start(bf16[16,3,64,128]{3,2,1,0:T(8,128)(2,1)} %get-tuple-element.16), calls=%async_computation | async-start | bytes 1572864 | tf_op jit(solution)/shard_map/all_to_all | solution.py:347
  11.9 3.5 %copy-start = (s32[32,32,32]{2,1,0:T(8,128)S(1)}, s32[32,32,32]{2,1,0:T(8,128)}, u32[]{:S(2)}) copy-start(s32[32,32,32]{2,1,0:T(8,128)} %layout_ref.1) | copy-start | bytes 393220
  11.9 3.5 %copy-start.1 = (s32[32,32]{1,0:T(8,128)S(1)}, s32[32,32]{1,0:T(8,128)}, u32[]{:S(2)}) copy-start(s32[32,32]{1,0:T(8,128)} %counts_ref.3) | copy-start | bytes 12292
  31.9 4.1 %collective-permute-start = (bf16[16,3,64,128]{3,2,1,0:T(8,128)(2,1)S(1)}, bf16[16,3,64,128]{3,2,1,0:T(8,128)(2,1)S(1)}, u32[]{:S(2)}, u32[]{:S(2)}) collective-permute-start(bf16[16,3,64,128]{3,2,1,0:T(8,128)(2,1)S(1)} %all-to-all-done.refs_0_), channel_id=1, source_target_pairs={{0,1},{1,0},{2,3},{3,2},{4,5},{5,4},{6,7},{7,6},{8,9},{9,8},{10,11... | collective-permute-start | bytes 2359304 | tf_op jit(solution)/shard_map/ppermute | solution.py:345
  31.9 24.8 %all-to-all-start.1 = ((bf16[16,3,64,128]{3,2,1,0:T(8,128)(2,1)}), bf16[16,3,64,128]{3,2,1,0:T(8,128)(2,1)S(1)}, u32[]{:S(2)}, u32[]{:S(2)}) async-start(bf16[16,3,64,128]{3,2,1,0:T(8,128)(2,1)} %pack.3), calls=%async_computation.1 | async-start | bytes 1572864 | tf_op jit(solution)/shard_map/all_to_all | solution.py:352
  56.7 2.3 %collective-permute-start.1 = (bf16[16,3,64,128]{3,2,1,0:T(8,128)(2,1)S(1)}, bf16[16,3,64,128]{3,2,1,0:T(8,128)(2,1)S(1)}, u32[]{:S(2)}, u32[]{:S(2)}) collective-permute-start(bf16[16,3,64,128]{3,2,1,0:T(8,128)(2,1)S(1)} %all-to-all-done.1.refs_0_), channel_id=1, source_target_pairs={{0,1},{1,0},{2,3},{3,2},{4,5},{5,4},{6,7},{7,6},{8,9},{9,8},{10,11... | collective-permute-start | bytes 2359304 | tf_op jit(solution)/shard_map/ppermute | solution.py:345

commit v11 on v10

--- a/solution.py
+++ b/solution.py
@@ -249,17 +249,24 @@
             DH, BLK
         )
 
+    def advance(chunk, side):
+        for lane in range(UNROLL):
+            merge(chunk * UNROLL + lane, lane, side)
+            make_scores((chunk + 2) * UNROLL + lane, lane, side)
+            make_output((chunk + 1) * UNROLL + lane, lane, 1 - side)
+
     def step(index, _):
-        for side in range(2):
-            chunk = 2 * index + side
-            for lane in range(UNROLL):
-                merge(chunk * UNROLL + lane, lane, side)
-                make_scores((chunk + 2) * UNROLL + lane, lane, side)
-                make_output((chunk + 1) * UNROLL + lane, lane, 1 - side)
+        advance(2 * index, 0)
+        advance(2 * index + 1, 1)
         return 0
 
     chunks = (total_ref[slot] + UNROLL - 1) // UNROLL
-    lax.fori_loop(0, (chunks + 1) // 2, step, 0)
+    lax.fori_loop(0, chunks // 2, step, 0)
+
+    @pl.when(chunks % 2 == 1)
+    def _():
+        advance(chunks - 1, 0)
+
     for row in range(rows):
         total_w = jnp.sum(l_ref[row], axis=0, keepdims=True)
         result = (acc_ref[row] * (1.0 / total_w)).astype(BF16)
@@ -269,16 +276,25 @@
             out_ref[row] = result
 
 
-def unpack_kernel(table_ref, o_ref, out_ref):
+def unpack_kernel(table_ref, o_ref, out_hbm, out_ref, sem):
     groups = o_ref.shape[0]
+    pairs = H // 2 // out_ref.shape[0]
 
     def fetch(head):
         place = table_ref[1, head]
         return o_ref[place % groups, place // groups]
 
-    for pair in range(H // 2):
-        both = jnp.concatenate([fetch(2 * pair), fetch(2 * pair + 1)], axis=0)
-        out_ref[:, pair * 2 * DH : (pair + 1) * 2 * DH] = both.T
+    copies = []
+    for part in range(out_ref.shape[0]):
+        for at in range(pairs):
+            head = 2 * (part * pairs + at)
+            both = jnp.concatenate([fetch(head), fetch(head + 1)], axis=0)
+            out_ref[part, :, at * 2 * DH : (at + 1) * 2 * DH] = both.T
+        lanes = pl.ds(part * pairs * 2 * DH, pairs * 2 * DH)
+        copies.append(pltpu.make_async_copy(out_ref.at[part], out_hbm.at[:, lanes], sem.at[part]))
+        copies[-1].start()
+    for copy in copies:
+        copy.wait()
 
 
 def shards(queries, key_vectors, value_vectors, layout, counts):
@@ -379,9 +395,10 @@
         )
     return pl.pallas_call(
         unpack_kernel,
-        out_shape=shape(queries.shape, BF16),
+        out_shape=pltpu.HBM(queries.shape, BF16),
         in_specs=[SMEM, VMEM],
-        out_specs=VMEM,
+        out_specs=HBM,
+        scratch_shapes=[pltpu.VMEM((4, BLK, H * DH // 4), BF16), pltpu.SemaphoreType.DMA((4,))],
         compiler_params=PARAMS,
         name="unpack",
     )(table, hold(swap(results[-1])))

time: 83.9 us -> 83.4 us (level)
  Pallas kernels: 37.6 us -> 35.8 us
  waiting for transfers between devices: 13.9 us -> 15.3 us
    pallas_call x2, Pallas kernels: 15.9 us -> 14.1 us  [shards(): pl.pallas_call(functools.partial(attend_kernel, slot, gather), out_shape=...]
    all_to_all x1, waiting for transfers between devices: 8.18 us -> 9.73 us  [shards(): arrived, *results = lax.optimization_barrier((swap(packed[slot]), *results))]
  transfers between devices with their start and end apart: 4 -> 4, of which waited for: 3 -> 3; matrix products, arithmetic and copies ran while one was open for 0% -> 0% of each run, Pallas kernels for 35% -> 33%
where the time goes in v11:
time: 83.4 us; the launch traced here: 83.1 us
  Pallas kernels  35.8 us (43%)
  blocking collectives  19.4 us (23%)
  waiting for transfers between devices  15.3 us (18%)
  starting transfers between devices  12.5 us (15%)
    all_to_all x1, blocking collectives, shards(): swap(results[-1])  19.4 us
    pallas_call x2, Pallas kernels, shards(): pl.pallas_call(functools.partial(attend_kernel, slot, gather), out_shape=...  14.1 us
    pallas_call x1, Pallas kernels, shards(): pl.pallas_call(functools.partial(plan_kernel, uly, gather), out_shape=(sh...  13.2 us
    all_to_all x1, waiting for transfers between devices, shards(): arrived, *results = lax.optimization_barrier((swap(packed[slot]), *results))  9.73 us
    all_to_all x1, starting transfers between devices, shards(): arrived = swap(packed[0])  8.32 us
    all_to_all x1, starting transfers between devices, shards(): arrived, *results = lax.optimization_barrier((swap(packed[slot]), *results))  4.12 us
    pallas_call x1, Pallas kernels, shards(): pl.pallas_call(functools.partial(pack_first_kernel, groups), out_shape=(s...  3.53 us
    pallas_call x1, Pallas kernels, shards(): pl.pallas_call(functools.partial(pack_rest_kernel, slot), out_shape=packe...  3.49 us
  transfers between devices with their start and end apart: 4, of which 3 were waited for; matrix products, arithmetic and copies ran while one was open for 0% of the time, Pallas kernels for 33%

profile of v11, /device:TPU:0, one launch (start us, length us, event | category | flops | bytes accessed | tf_op | source)
XLA Modules:
  0.0 83.1 jit_solution(8756485832368506569)
XLA Ops:
  0.0 3.5 %pack.2 = (s32[8,128]{1,0:T(8,128)S(1)}, bf16[16,3,64,128]{3,2,1,0:T(8,128)(2,1)}) custom-call(s32[32,32]{1,0:T(8,128)} %counts_ref.3, bf16[128,2048]{1,0:T(8,128)(2,1)} %q_hbm.1, bf16[128,2048]{1,0:T(8,128)(2,1)} %k_hbm.1, bf16[128,2048]{1,0:T(8,128)(2,1)} %v_hbm.1), custom_call_target="tpu_custom_call" | custom-call | tf_op jit(solution)/shard_map/pack/pallas_call | solution.py:312
  3.5 8.3 %all-to-all-start = ((bf16[16,3,64,128]{3,2,1,0:T(8,128)(2,1)}), bf16[16,3,64,128]{3,2,1,0:T(8,128)(2,1)S(1)}, u32[]{:S(2)}, u32[]{:S(2)}) async-start(bf16[16,3,64,128]{3,2,1,0:T(8,128)(2,1)} %get-tuple-element.16), calls=%async_computation | async-start | bytes 1572864 | tf_op jit(solution)/shard_map/all_to_all | solution.py:363
  11.9 0.0 copy-start
  11.9 0.0 copy-start.1
  11.9 3.5 %pack.3 = bf16[16,3,64,128]{3,2,1,0:T(8,128)(2,1)} custom-call(s32[8,128]{1,0:T(8,128)S(1)} %get-tuple-element.15.table_ref, bf16[128,2048]{1,0:T(8,128)(2,1)} %q_hbm.1, bf16[128,2048]{1,0:T(8,128)(2,1)} %k_hbm.1, bf16[128,2048]{1,0:T(8,128)(2,1)} %v_hbm.1), custom_call_target="tpu_custom_call" | custom-call | tf_op jit(solution)/shard_map/pack/pallas_call | solution.py:324
  15.4 0.0 copy-done
  15.4 0.0 copy-done.1
  15.4 13.2 %plan.1 = (s32[2,4,304]{2,1,0:T(4,128)S(1)}, s32[2]{0:T(128)S(1)}) custom-call(s32[8,128]{1,0:T(8,128)S(1)} %get-tuple-element.15.table_ref, s32[32,32]{1,0:T(8,128)S(1)} %copy-done.1, s32[32,32,32]{2,1,0:T(8,128)S(1)} %copy-done), custom_call_target="tpu_custom_call" | custom-call | tf_op jit(solution)/shard_map/plan/pallas_call | solution.py:334
  28.6 3.3 %all-to-all-done.refs_0_ = bf16[16,3,64,128]{3,2,1,0:T(8,128)(2,1)S(1)} async-done(((bf16[16,3,64,128]{3,2,1,0:T(8,128)(2,1)}), bf16[16,3,64,128]{3,2,1,0:T(8,128)(2,1)S(1)}, u32[]{:S(2)}, u32[]{:S(2)}) %all-to-all-start) | async-done | bytes 786464 | tf_op jit(solution)/shard_map/all_to_all | solution.py:363
  31.9 0.0 collective-permute-start
  31.9 4.1 %all-to-all-start.1 = ((bf16[16,3,64,128]{3,2,1,0:T(8,128)(2,1)}), bf16[16,3,64,128]{3,2,1,0:T(8,128)(2,1)S(1)}, u32[]{:S(2)}, u32[]{:S(2)}) async-start(bf16[16,3,64,128]{3,2,1,0:T(8,128)(2,1)} %pack.3), calls=%async_computation.1 | async-start | bytes 1572864 | tf_op jit(solution)/shard_map/all_to_all | solution.py:368
  36.0 0.0 collective-permute-done.refs_1_
  36.0 10.9 %attend.2.refs_2_ = bf16[16,64,128]{2,1,0:T(8,128)(2,1)S(1)} custom-call(s32[2,4,304]{2,1,0:T(4,128)S(1)} %get-tuple-element.19.unit_ref, s32[2]{0:T(128)S(1)} %get-tuple-element.20.total_ref, bf16[16,3,64,128]{3,2,1,0:T(8,128)(2,1)S(1)} %all-to-all-done.refs_0_, bf16[16,3,64,128]{3,2,1,0:T(8,128)(2,1)S(1)} %collective-permute-done.refs_1_), custom_call_target="tpu_custom_call" | custom-call | flops 10000000000 | bytes 6000000 | tf_op jit(solution)/shard_map/attend/pallas_call | solution.py:378
  47.0 9.7 %all-to-all-done.1.refs_0_ = bf16[16,3,64,128]{3,2,1,0:T(8,128)(2,1)S(1)} async-done(((bf16[16,3,64,128]{3,2,1,0:T(8,128)(2,1)}), bf16[16,3,64,128]{3,2,1,0:T(8,128)(2,1)S(1)}, u32[]{:S(2)}, u32[]{:S(2)}) %all-to-all-start.1) | async-done | bytes 786464 | tf_op jit(solution)/shard_map/all_to_all | solution.py:368
  56.7 0.0 collective-permute-start.1
  56.7 2.3 %collective-permute-done.1.refs_1_ = bf16[16,3,64,128]{3,2,1,0:T(8,128)(2,1)S(1)} collective-permute-done((bf16[16,3,64,128]{3,2,1,0:T(8,128)(2,1)S(1)}, bf16[16,3,64,128]{3,2,1,0:T(8,128)(2,1)S(1)}, u32[]{:S(2)}, u32[]{:S(2)}) %collective-permute-start.1) | collective-permute-done | bytes 786464 | tf_op jit(solution)/shard_map/ppermute | solution.py:361
  59.0 3.2 %attend.3 = bf16[16,2,64,128]{3,2,1,0:T(8,128)(2,1)S(1)} custom-call(s32[2,4,304]{2,1,0:T(4,128)S(1)} %get-tuple-element.19.unit_ref, s32[2]{0:T(128)S(1)} %get-tuple-element.20.total_ref, bf16[16,3,64,128]{3,2,1,0:T(8,128)(2,1)S(1)} %all-to-all-done.1.refs_0_, bf16[16,3,64,128]{3,2,1,0:T(8,128)(2,1)S(1)} %collective-permute-done.1.refs_1_, ...), custom_call_target="tpu_custom_call" | custom-call | flops 10000000000 | bytes 6000000 | tf_op jit(solution)/shard_map/attend/pallas_call | solution.py:378
  62.1 19.4 %all_to_all.15.o_ref = bf16[16,2,64,128]{3,2,1,0:T(8,128)(2,1)S(1)} all-to-all(bf16[16,2,64,128]{3,2,1,0:T(8,128)(2,1)S(1)} %attend.3), channel_id=1, replica_groups={{0,16,8,24,4,20,12,28,2,18,10,26,6,22,14,30},{1,17,9,25,5,21,13,29,3,19..., dimensions={0} | all-to-all | bytes 1048576 | tf_op jit(solution)/shard_map/all_to_all | solution.py:404
  81.5 1.6 %unpack.1 = bf16[128,2048]{1,0:T(8,128)(2,1)} custom-call(s32[8,128]{1,0:T(8,128)S(1)} %get-tuple-element.15.table_ref, bf16[16,2,64,128]{3,2,1,0:T(8,128)(2,1)S(1)} %all_to_all.15.o_ref), custom_call_target="tpu_custom_call" | custom-call | tf_op jit(solution)/shard_map/unpack/pallas_call | solution.py:396
Async XLA Ops:
  3.5 28.3 %all-to-all-start = ((bf16[16,3,64,128]{3,2,1,0:T(8,128)(2,1)}), bf16[16,3,64,128]{3,2,1,0:T(8,128)(2,1)S(1)}, u32[]{:S(2)}, u32[]{:S(2)}) async-start(bf16[16,3,64,128]{3,2,1,0:T(8,128)(2,1)} %get-tuple-element.16), calls=%async_computation | async-start | bytes 1572864 | tf_op jit(solution)/shard_map/all_to_all | solution.py:363
  11.9 3.5 %copy-start = (s32[32,32,32]{2,1,0:T(8,128)S(1)}, s32[32,32,32]{2,1,0:T(8,128)}, u32[]{:S(2)}) copy-start(s32[32,32,32]{2,1,0:T(8,128)} %layout_ref.1) | copy-start | bytes 393220
  11.9 3.5 %copy-start.1 = (s32[32,32]{1,0:T(8,128)S(1)}, s32[32,32]{1,0:T(8,128)}, u32[]{:S(2)}) copy-start(s32[32,32]{1,0:T(8,128)} %counts_ref.3) | copy-start | bytes 12292
  31.9 4.1 %collective-permute-start = (bf16[16,3,64,128]{3,2,1,0:T(8,128)(2,1)S(1)}, bf16[16,3,64,128]{3,2,1,0:T(8,128)(2,1)S(1)}, u32[]{:S(2)}, u32[]{:S(2)}) collective-permute-start(bf16[16,3,64,128]{3,2,1,0:T(8,128)(2,1)S(1)} %all-to-all-done.refs_0_), channel_id=1, source_target_pairs={{0,1},{1,0},{2,3},{3,2},{4,5},{5,4},{6,7},{7,6},{8,9},{9,8},{10,11... | collective-permute-start | bytes 2359304 | tf_op jit(solution)/shard_map/ppermute | solution.py:361
  31.9 24.8 %all-to-all-start.1 = ((bf16[16,3,64,128]{3,2,1,0:T(8,128)(2,1)}), bf16[16,3,64,128]{3,2,1,0:T(8,128)(2,1)S(1)}, u32[]{:S(2)}, u32[]{:S(2)}) async-start(bf16[16,3,64,128]{3,2,1,0:T(8,128)(2,1)} %pack.3), calls=%async_computation.1 | async-start | bytes 1572864 | tf_op jit(solution)/shard_map/all_to_all | solution.py:368
  56.7 2.3 %collective-permute-start.1 = (bf16[16,3,64,128]{3,2,1,0:T(8,128)(2,1)S(1)}, bf16[16,3,64,128]{3,2,1,0:T(8,128)(2,1)S(1)}, u32[]{:S(2)}, u32[]{:S(2)}) collective-permute-start(bf16[16,3,64,128]{3,2,1,0:T(8,128)(2,1)S(1)} %all-to-all-done.1.refs_0_), channel_id=1, source_target_pairs={{0,1},{1,0},{2,3},{3,2},{4,5},{5,4},{6,7},{7,6},{8,9},{9,8},{10,11... | collective-permute-start | bytes 2359304 | tf_op jit(solution)/shard_map/ppermute | solution.py:361

commit v12 on v11

--- a/solution.py
+++ b/solution.py
@@ -87,18 +87,27 @@
     return copies
 
 
-def pack_first_kernel(groups, counts_ref, q_ref, k_ref, v_ref, table_ref, out_ref, table_vmem, sem):
+def reversal(groups, gather, rest):
+    return (rest & 1) * (groups - 1) if gather > 1 else 0
+
+
+def own_reversal(groups, gather):
+    return reversal(groups, gather, lax.axis_index("doc") % gather)
+
+
+def pack_first_kernel(groups, gather, counts_ref, q_ref, k_ref, v_ref, table_ref, out_ref, table_vmem, sem):
     rank_heads(counts_ref, table_vmem, groups)
     copy = pltpu.make_async_copy(table_vmem, table_ref, sem)
     copy.start()
     copy.wait()
+    turn = own_reversal(groups, gather)
     for group in range(groups):
-        head = table_ref[0, group]
+        head = table_ref[0, group ^ turn]
         for at, source in enumerate((v_ref, q_ref, k_ref)):
             out_ref[group, at] = fold_head(source, head)
 
 
-def pack_rest_kernel(slot, table_ref, q_hbm, k_hbm, v_hbm, out_ref, q_ref, k_ref, v_ref, sems, turned_q, turned_v):
+def pack_rest_kernel(slot, gather, table_ref, q_hbm, k_hbm, v_hbm, out_ref, q_ref, k_ref, v_ref, sems, turned_q, turned_v):
     copies = load((k_hbm, v_hbm, q_hbm), (k_ref, v_ref, q_ref), sems)
     for group in copies:
         for copy in group:
@@ -106,8 +115,9 @@
     turn_heads(q_ref, turned_q)
     turn_heads(v_ref, turned_v)
     groups = out_ref.shape[0]
+    turn = own_reversal(groups, gather)
     for group in range(groups):
-        head = table_ref[0, slot * groups + group]
+        head = table_ref[0, slot * groups + (group ^ turn)]
         out_ref[group, 0] = turned_v[head]
         out_ref[group, 1] = turned_q[head]
         out_ref[group, 2] = fold_head(k_ref, head)
@@ -143,7 +153,8 @@
 
     def local(block):
         its = block // uly
-        return ((its % gather) ^ rest) * groups + (its // gather) * uly + mirror(block % uly, uly)
+        place = (its // gather) * uly + mirror(block % uly, uly)
+        return ((its % gather) ^ rest) * groups + (place ^ reversal(groups, gather, its % gather))
 
     for copy in copies:
         copy.wait()
@@ -158,8 +169,9 @@
                 unit_ref[slot, 3, base + extra] = 1
 
         def place_row(row, base, slot=slot, head=head):
-            token = (row // uly) * uly + mirror(row % uly, uly)
-            count = counts_ref[head, rows_at(row // uly) + mirror(row % uly, uly)]
+            place = row ^ reversal(groups, gather, rest)
+            token = (place // uly) * uly + mirror(place % uly, uly)
+            count = counts_ref[head, rows_at(place // uly) + mirror(place % uly, uly)]
 
             def place_unit(step, _):
                 first = lay_ref[slot, token, 2 * step]
@@ -175,8 +187,8 @@
             lax.fori_loop(0, units, place_unit, 0)
             return base + units
 
-        idle(0, 2 * UNROLL)
-        total = lax.fori_loop(0, groups, place_row, jnp.int32(2 * UNROLL))
+        idle(0, UNROLL)
+        total = lax.fori_loop(0, groups, place_row, jnp.int32(UNROLL))
         idle(total, 4 * UNROLL)
         total_ref[slot] = total
 
@@ -260,12 +272,21 @@
         advance(2 * index + 1, 1)
         return 0
 
-    chunks = (total_ref[slot] + UNROLL - 1) // UNROLL
+    chunks = (total_ref[slot] + UNROLL - 1) // UNROLL - 1
+    for lane in range(UNROLL):
+        make_scores(UNROLL + lane, lane, 1)
     lax.fori_loop(0, chunks // 2, step, 0)
 
     @pl.when(chunks % 2 == 1)
     def _():
         advance(chunks - 1, 0)
+        for lane in range(UNROLL):
+            merge(chunks * UNROLL + lane, lane, 1)
+
+    @pl.when(chunks % 2 == 0)
+    def _():
+        for lane in range(UNROLL):
+            merge(chunks * UNROLL + lane, lane, 0)
 
     for row in range(rows):
         total_w = jnp.sum(l_ref[row], axis=0, keepdims=True)
@@ -276,13 +297,14 @@
             out_ref[row] = result
 
 
-def unpack_kernel(table_ref, o_ref, out_hbm, out_ref, sem):
+def unpack_kernel(gather, table_ref, o_ref, out_hbm, out_ref, sem):
     groups = o_ref.shape[0]
     pairs = H // 2 // out_ref.shape[0]
+    turn = own_reversal(groups, gather)
 
     def fetch(head):
         place = table_ref[1, head]
-        return o_ref[place % groups, place // groups]
+        return o_ref[(place % groups) ^ turn, place // groups]
 
     copies = []
     for part in range(out_ref.shape[0]):
@@ -310,7 +332,7 @@
     packed_shape = pltpu.HBM((groups, 3, DH, BLK), BF16)
     held = [pltpu.VMEM(queries.shape, BF16)] * 3 + [pltpu.SemaphoreType.DMA((3, 4))]
     table, first = pl.pallas_call(
-        functools.partial(pack_first_kernel, groups),
+        functools.partial(pack_first_kernel, groups, gather),
         out_shape=(shape((8, 128), jnp.int32), packed_shape),
         in_specs=[VMEM] * 4,
         out_specs=(SMEM, VMEM),
@@ -322,7 +344,7 @@
     for slot in range(1, slots):
         packed.append(
             pl.pallas_call(
-                functools.partial(pack_rest_kernel, slot),
+                functools.partial(pack_rest_kernel, slot, gather),
                 out_shape=packed_shape,
                 in_specs=[SMEM] + [HBM] * 3,
                 out_specs=VMEM,
@@ -341,10 +363,11 @@
         name="plan",
     )(table, counts, layout)
 
-    members = [
-        [(part * gather + rest) * uly + mirror(at, uly) for part in range(parts) for at in range(uly)]
-        for rest in range(gather)
-    ]
+    def member(rest, at):
+        place = at ^ reversal(groups, gather, rest)
+        return ((place // uly) * gather + rest) * uly + mirror(place % uly, uly)
+
+    members = [[member(rest, at) for at in range(groups)] for rest in range(gather)]
     swap = functools.partial(
         lax.all_to_all,
         axis_name=("doc", "uly"),
@@ -394,7 +417,7 @@
             )(units, totals, *[hold(arrays[at]) for at in range(gather)], *[hold(result) for result in earlier])
         )
     return pl.pallas_call(
-        unpack_kernel,
+        functools.partial(unpack_kernel, gather),
         out_shape=pltpu.HBM(queries.shape, BF16),
         in_specs=[SMEM, VMEM],
         out_specs=HBM,

time: 83.4 us -> 84 us (level)
  transfers between devices with their start and end apart: 4 -> 4, of which waited for: 3 -> 3; matrix products, arithmetic and copies ran while one was open for 0% -> 0% of each run, Pallas kernels for 33% -> 34%
where the time goes in v12:
time: 84 us; the launch traced here: 83.6 us
  Pallas kernels  36.3 us (43%)
  blocking collectives  19.1 us (23%)
  waiting for transfers between devices  14.9 us (18%)
  starting transfers between devices  13.2 us (16%)
    all_to_all x1, blocking collectives, shards(): swap(results[-1])  19.1 us
    pallas_call x1, Pallas kernels, shards(): pl.pallas_call(functools.partial(plan_kernel, uly, gather), out_shape=(sh...  13.9 us
    pallas_call x2, Pallas kernels, shards(): pl.pallas_call(functools.partial(attend_kernel, slot, gather), out_shape=...  13.8 us
    all_to_all x1, waiting for transfers between devices, shards(): arrived, *results = lax.optimization_barrier((swap(packed[slot]), *results))  9.94 us
    all_to_all x1, starting transfers between devices, shards(): arrived = swap(packed[0])  8.32 us
    all_to_all x1, starting transfers between devices, shards(): arrived, *results = lax.optimization_barrier((swap(packed[slot]), *results))  4.84 us
    pallas_call x1, Pallas kernels, shards(): pl.pallas_call(functools.partial(pack_first_kernel, groups, gather), out_...  3.54 us
    pallas_call x1, Pallas kernels, shards(): pl.pallas_call(functools.partial(pack_rest_kernel, slot, gather), out_sha...  3.49 us
  transfers between devices with their start and end apart: 4, of which 3 were waited for; matrix products, arithmetic and copies ran while one was open for 0% of the time, Pallas kernels for 34%

profile of v12, /device:TPU:0, one launch (start us, length us, event | category | flops | bytes accessed | tf_op | source)
XLA Modules:
  0.0 83.6 jit_solution(5200516605004841308)
XLA Ops:
  0.0 3.5 %pack.2 = (s32[8,128]{1,0:T(8,128)S(1)}, bf16[16,3,64,128]{3,2,1,0:T(8,128)(2,1)}) custom-call(s32[32,32]{1,0:T(8,128)} %counts_ref.3, bf16[128,2048]{1,0:T(8,128)(2,1)} %q_hbm.1, bf16[128,2048]{1,0:T(8,128)(2,1)} %k_hbm.1, bf16[128,2048]{1,0:T(8,128)(2,1)} %v_hbm.1), custom_call_target="tpu_custom_call" | custom-call | tf_op jit(solution)/shard_map/pack/pallas_call | solution.py:334
  3.5 8.3 %all-to-all-start = ((bf16[16,3,64,128]{3,2,1,0:T(8,128)(2,1)}), bf16[16,3,64,128]{3,2,1,0:T(8,128)(2,1)S(1)}, u32[]{:S(2)}, u32[]{:S(2)}) async-start(bf16[16,3,64,128]{3,2,1,0:T(8,128)(2,1)} %get-tuple-element.16), calls=%async_computation | async-start | bytes 1572864 | tf_op jit(solution)/shard_map/all_to_all | solution.py:386
  11.9 0.0 copy-start
  11.9 0.0 copy-start.1
  11.9 3.5 %pack.3 = bf16[16,3,64,128]{3,2,1,0:T(8,128)(2,1)} custom-call(s32[8,128]{1,0:T(8,128)S(1)} %get-tuple-element.15.table_ref, bf16[128,2048]{1,0:T(8,128)(2,1)} %q_hbm.1, bf16[128,2048]{1,0:T(8,128)(2,1)} %k_hbm.1, bf16[128,2048]{1,0:T(8,128)(2,1)} %v_hbm.1), custom_call_target="tpu_custom_call" | custom-call | tf_op jit(solution)/shard_map/pack/pallas_call | solution.py:346
  15.4 0.0 copy-done
  15.4 0.0 copy-done.1
  15.4 13.9 %plan.1 = (s32[2,4,304]{2,1,0:T(4,128)S(1)}, s32[2]{0:T(128)S(1)}) custom-call(s32[8,128]{1,0:T(8,128)S(1)} %get-tuple-element.15.table_ref, s32[32,32]{1,0:T(8,128)S(1)} %copy-done.1, s32[32,32,32]{2,1,0:T(8,128)S(1)} %copy-done), custom_call_target="tpu_custom_call" | custom-call | tf_op jit(solution)/shard_map/plan/pallas_call | solution.py:356
  29.3 2.7 %all-to-all-done.refs_0_ = bf16[16,3,64,128]{3,2,1,0:T(8,128)(2,1)S(1)} async-done(((bf16[16,3,64,128]{3,2,1,0:T(8,128)(2,1)}), bf16[16,3,64,128]{3,2,1,0:T(8,128)(2,1)S(1)}, u32[]{:S(2)}, u32[]{:S(2)}) %all-to-all-start) | async-done | bytes 786464 | tf_op jit(solution)/shard_map/all_to_all | solution.py:386
  32.0 0.0 collective-permute-start
  32.0 4.8 %all-to-all-start.1 = ((bf16[16,3,64,128]{3,2,1,0:T(8,128)(2,1)}), bf16[16,3,64,128]{3,2,1,0:T(8,128)(2,1)S(1)}, u32[]{:S(2)}, u32[]{:S(2)}) async-start(bf16[16,3,64,128]{3,2,1,0:T(8,128)(2,1)} %pack.3), calls=%async_computation.1 | async-start | bytes 1572864 | tf_op jit(solution)/shard_map/all_to_all | solution.py:391
  36.9 0.0 collective-permute-done.refs_1_
  36.9 10.8 %attend.2.refs_2_ = bf16[16,64,128]{2,1,0:T(8,128)(2,1)S(1)} custom-call(s32[2,4,304]{2,1,0:T(4,128)S(1)} %get-tuple-element.19.unit_ref, s32[2]{0:T(128)S(1)} %get-tuple-element.20.total_ref, bf16[16,3,64,128]{3,2,1,0:T(8,128)(2,1)S(1)} %all-to-all-done.refs_0_, bf16[16,3,64,128]{3,2,1,0:T(8,128)(2,1)S(1)} %collective-permute-done.refs_1_), custom_call_target="tpu_custom_call" | custom-call | flops 10000000000 | bytes 6000000 | tf_op jit(solution)/shard_map/attend/pallas_call | solution.py:401
  47.7 9.9 %all-to-all-done.1.refs_0_ = bf16[16,3,64,128]{3,2,1,0:T(8,128)(2,1)S(1)} async-done(((bf16[16,3,64,128]{3,2,1,0:T(8,128)(2,1)}), bf16[16,3,64,128]{3,2,1,0:T(8,128)(2,1)S(1)}, u32[]{:S(2)}, u32[]{:S(2)}) %all-to-all-start.1) | async-done | bytes 786464 | tf_op jit(solution)/shard_map/all_to_all | solution.py:391
  57.7 0.0 collective-permute-start.1
  57.7 2.3 %collective-permute-done.1.refs_1_ = bf16[16,3,64,128]{3,2,1,0:T(8,128)(2,1)S(1)} collective-permute-done((bf16[16,3,64,128]{3,2,1,0:T(8,128)(2,1)S(1)}, bf16[16,3,64,128]{3,2,1,0:T(8,128)(2,1)S(1)}, u32[]{:S(2)}, u32[]{:S(2)}) %collective-permute-start.1) | collective-permute-done | bytes 786464 | tf_op jit(solution)/shard_map/ppermute | solution.py:384
  59.9 2.9 %attend.3 = bf16[16,2,64,128]{3,2,1,0:T(8,128)(2,1)S(1)} custom-call(s32[2,4,304]{2,1,0:T(4,128)S(1)} %get-tuple-element.19.unit_ref, s32[2]{0:T(128)S(1)} %get-tuple-element.20.total_ref, bf16[16,3,64,128]{3,2,1,0:T(8,128)(2,1)S(1)} %all-to-all-done.1.refs_0_, bf16[16,3,64,128]{3,2,1,0:T(8,128)(2,1)S(1)} %collective-permute-done.1.refs_1_, ...), custom_call_target="tpu_custom_call" | custom-call | flops 10000000000 | bytes 6000000 | tf_op jit(solution)/shard_map/attend/pallas_call | solution.py:401
  62.9 19.1 %all_to_all.15.o_ref = bf16[16,2,64,128]{3,2,1,0:T(8,128)(2,1)S(1)} all-to-all(bf16[16,2,64,128]{3,2,1,0:T(8,128)(2,1)S(1)} %attend.3), channel_id=1, replica_groups={{0,16,8,24,4,20,12,28,2,18,10,26,6,22,14,30},{31,15,23,7,27,11,19,3,29,..., dimensions={0} | all-to-all | bytes 1048576 | tf_op jit(solution)/shard_map/all_to_all | solution.py:427
  82.0 1.6 %unpack.1 = bf16[128,2048]{1,0:T(8,128)(2,1)} custom-call(s32[8,128]{1,0:T(8,128)S(1)} %get-tuple-element.15.table_ref, bf16[16,2,64,128]{3,2,1,0:T(8,128)(2,1)S(1)} %all_to_all.15.o_ref), custom_call_target="tpu_custom_call" | custom-call | tf_op jit(solution)/shard_map/unpack/pallas_call | solution.py:419
Async XLA Ops:
  3.5 28.5 %all-to-all-start = ((bf16[16,3,64,128]{3,2,1,0:T(8,128)(2,1)}), bf16[16,3,64,128]{3,2,1,0:T(8,128)(2,1)S(1)}, u32[]{:S(2)}, u32[]{:S(2)}) async-start(bf16[16,3,64,128]{3,2,1,0:T(8,128)(2,1)} %get-tuple-element.16), calls=%async_computation | async-start | bytes 1572864 | tf_op jit(solution)/shard_map/all_to_all | solution.py:386
  11.9 3.5 %copy-start = (s32[32,32,32]{2,1,0:T(8,128)S(1)}, s32[32,32,32]{2,1,0:T(8,128)}, u32[]{:S(2)}) copy-start(s32[32,32,32]{2,1,0:T(8,128)} %layout_ref.1) | copy-start | bytes 393220
  11.9 3.5 %copy-start.1 = (s32[32,32]{1,0:T(8,128)S(1)}, s32[32,32]{1,0:T(8,128)}, u32[]{:S(2)}) copy-start(s32[32,32]{1,0:T(8,128)} %counts_ref.3) | copy-start | bytes 12292
  32.0 4.9 %collective-permute-start = (bf16[16,3,64,128]{3,2,1,0:T(8,128)(2,1)S(1)}, bf16[16,3,64,128]{3,2,1,0:T(8,128)(2,1)S(1)}, u32[]{:S(2)}, u32[]{:S(2)}) collective-permute-start(bf16[16,3,64,128]{3,2,1,0:T(8,128)(2,1)S(1)} %all-to-all-done.refs_0_), channel_id=1, source_target_pairs={{0,1},{1,0},{2,3},{3,2},{4,5},{5,4},{6,7},{7,6},{8,9},{9,8},{10,11... | collective-permute-start | bytes 2359304 | tf_op jit(solution)/shard_map/ppermute | solution.py:384
  32.0 25.6 %all-to-all-start.1 = ((bf16[16,3,64,128]{3,2,1,0:T(8,128)(2,1)}), bf16[16,3,64,128]{3,2,1,0:T(8,128)(2,1)S(1)}, u32[]{:S(2)}, u32[]{:S(2)}) async-start(bf16[16,3,64,128]{3,2,1,0:T(8,128)(2,1)} %pack.3), calls=%async_computation.1 | async-start | bytes 1572864 | tf_op jit(solution)/shard_map/all_to_all | solution.py:391
  57.7 2.3 %collective-permute-start.1 = (bf16[16,3,64,128]{3,2,1,0:T(8,128)(2,1)S(1)}, bf16[16,3,64,128]{3,2,1,0:T(8,128)(2,1)S(1)}, u32[]{:S(2)}, u32[]{:S(2)}) collective-permute-start(bf16[16,3,64,128]{3,2,1,0:T(8,128)(2,1)S(1)} %all-to-all-done.1.refs_0_), channel_id=1, source_target_pairs={{0,1},{1,0},{2,3},{3,2},{4,5},{5,4},{6,7},{7,6},{8,9},{9,8},{10,11... | collective-permute-start | bytes 2359304 | tf_op jit(solution)/shard_map/ppermute | solution.py:384

commit v13 on v11

--- a/solution.py
+++ b/solution.py
@@ -175,8 +175,8 @@
             lax.fori_loop(0, units, place_unit, 0)
             return base + units
 
-        idle(0, 2 * UNROLL)
-        total = lax.fori_loop(0, groups, place_row, jnp.int32(2 * UNROLL))
+        idle(0, UNROLL)
+        total = lax.fori_loop(0, groups, place_row, jnp.int32(UNROLL))
         idle(total, 4 * UNROLL)
         total_ref[slot] = total
 
@@ -260,12 +260,21 @@
         advance(2 * index + 1, 1)
         return 0
 
-    chunks = (total_ref[slot] + UNROLL - 1) // UNROLL
+    chunks = (total_ref[slot] + UNROLL - 1) // UNROLL - 1
+    for lane in range(UNROLL):
+        make_scores(UNROLL + lane, lane, 1)
     lax.fori_loop(0, chunks // 2, step, 0)
 
     @pl.when(chunks % 2 == 1)
     def _():
         advance(chunks - 1, 0)
+        for lane in range(UNROLL):
+            merge(chunks * UNROLL + lane, lane, 1)
+
+    @pl.when(chunks % 2 == 0)
+    def _():
+        for lane in range(UNROLL):
+            merge(chunks * UNROLL + lane, lane, 0)
 
     for row in range(rows):
         total_w = jnp.sum(l_ref[row], axis=0, keepdims=True)

time: 83.4 us -> 83.3 us (level)
  no operation moved by 1% of the time
where the time goes in v13:
time: 83.3 us; the launch traced here: 82.9 us
  Pallas kernels  35.8 us (43%)
  blocking collectives  19.4 us (23%)
  waiting for transfers between devices  15.2 us (18%)
  starting transfers between devices  12.5 us (15%)
    all_to_all x1, blocking collectives, shards(): swap(results[-1])  19.4 us
    pallas_call x2, Pallas kernels, shards(): pl.pallas_call(functools.partial(attend_kernel, slot, gather), out_shape=...  13.8 us
    pallas_call x1, Pallas kernels, shards(): pl.pallas_call(functools.partial(plan_kernel, uly, gather), out_shape=(sh...  13.4 us
    all_to_all x1, waiting for transfers between devices, shards(): arrived, *results = lax.optimization_barrier((swap(packed[slot]), *results))  9.81 us
    all_to_all x1, starting transfers between devices, shards(): arrived = swap(packed[0])  8.32 us
    all_to_all x1, starting transfers between devices, shards(): arrived, *results = lax.optimization_barrier((swap(packed[slot]), *results))  4.12 us
    pallas_call x1, Pallas kernels, shards(): pl.pallas_call(functools.partial(pack_first_kernel, groups), out_shape=(s...  3.53 us
    pallas_call x1, Pallas kernels, shards(): pl.pallas_call(functools.partial(pack_rest_kernel, slot), out_shape=packe...  3.49 us
  transfers between devices with their start and end apart: 4, of which 3 were waited for; matrix products, arithmetic and copies ran while one was open for 0% of the time, Pallas kernels for 33%

profile of v13, /device:TPU:0, one launch (start us, length us, event | category | flops | bytes accessed | tf_op | source)
XLA Modules:
  0.0 82.9 jit_solution(17906823066210936624)
XLA Ops:
  0.0 3.5 %pack.2 = (s32[8,128]{1,0:T(8,128)S(1)}, bf16[16,3,64,128]{3,2,1,0:T(8,128)(2,1)}) custom-call(s32[32,32]{1,0:T(8,128)} %counts_ref.3, bf16[128,2048]{1,0:T(8,128)(2,1)} %q_hbm.1, bf16[128,2048]{1,0:T(8,128)(2,1)} %k_hbm.1, bf16[128,2048]{1,0:T(8,128)(2,1)} %v_hbm.1), custom_call_target="tpu_custom_call" | custom-call | tf_op jit(solution)/shard_map/pack/pallas_call | solution.py:321
  3.5 8.3 %all-to-all-start = ((bf16[16,3,64,128]{3,2,1,0:T(8,128)(2,1)}), bf16[16,3,64,128]{3,2,1,0:T(8,128)(2,1)S(1)}, u32[]{:S(2)}, u32[]{:S(2)}) async-start(bf16[16,3,64,128]{3,2,1,0:T(8,128)(2,1)} %get-tuple-element.16), calls=%async_computation | async-start | bytes 1572864 | tf_op jit(solution)/shard_map/all_to_all | solution.py:372
  11.9 0.0 copy-start
  11.9 0.0 copy-start.1
  11.9 3.5 %pack.3 = bf16[16,3,64,128]{3,2,1,0:T(8,128)(2,1)} custom-call(s32[8,128]{1,0:T(8,128)S(1)} %get-tuple-element.15.table_ref, bf16[128,2048]{1,0:T(8,128)(2,1)} %q_hbm.1, bf16[128,2048]{1,0:T(8,128)(2,1)} %k_hbm.1, bf16[128,2048]{1,0:T(8,128)(2,1)} %v_hbm.1), custom_call_target="tpu_custom_call" | custom-call | tf_op jit(solution)/shard_map/pack/pallas_call | solution.py:333
  15.4 0.0 copy-done
  15.4 0.0 copy-done.1
  15.4 13.4 %plan.1 = (s32[2,4,304]{2,1,0:T(4,128)S(1)}, s32[2]{0:T(128)S(1)}) custom-call(s32[8,128]{1,0:T(8,128)S(1)} %get-tuple-element.15.table_ref, s32[32,32]{1,0:T(8,128)S(1)} %copy-done.1, s32[32,32,32]{2,1,0:T(8,128)S(1)} %copy-done), custom_call_target="tpu_custom_call" | custom-call | tf_op jit(solution)/shard_map/plan/pallas_call | solution.py:343
  28.8 3.1 %all-to-all-done.refs_0_ = bf16[16,3,64,128]{3,2,1,0:T(8,128)(2,1)S(1)} async-done(((bf16[16,3,64,128]{3,2,1,0:T(8,128)(2,1)}), bf16[16,3,64,128]{3,2,1,0:T(8,128)(2,1)S(1)}, u32[]{:S(2)}, u32[]{:S(2)}) %all-to-all-start) | async-done | bytes 786464 | tf_op jit(solution)/shard_map/all_to_all | solution.py:372
  31.9 0.0 collective-permute-start
  31.9 4.1 %all-to-all-start.1 = ((bf16[16,3,64,128]{3,2,1,0:T(8,128)(2,1)}), bf16[16,3,64,128]{3,2,1,0:T(8,128)(2,1)S(1)}, u32[]{:S(2)}, u32[]{:S(2)}) async-start(bf16[16,3,64,128]{3,2,1,0:T(8,128)(2,1)} %pack.3), calls=%async_computation.1 | async-start | bytes 1572864 | tf_op jit(solution)/shard_map/all_to_all | solution.py:377
  36.0 0.0 collective-permute-done.refs_1_
  36.0 10.8 %attend.2.refs_2_ = bf16[16,64,128]{2,1,0:T(8,128)(2,1)S(1)} custom-call(s32[2,4,304]{2,1,0:T(4,128)S(1)} %get-tuple-element.19.unit_ref, s32[2]{0:T(128)S(1)} %get-tuple-element.20.total_ref, bf16[16,3,64,128]{3,2,1,0:T(8,128)(2,1)S(1)} %all-to-all-done.refs_0_, bf16[16,3,64,128]{3,2,1,0:T(8,128)(2,1)S(1)} %collective-permute-done.refs_1_), custom_call_target="tpu_custom_call" | custom-call | flops 10000000000 | bytes 6000000 | tf_op jit(solution)/shard_map/attend/pallas_call | solution.py:387
  46.9 9.8 %all-to-all-done.1.refs_0_ = bf16[16,3,64,128]{3,2,1,0:T(8,128)(2,1)S(1)} async-done(((bf16[16,3,64,128]{3,2,1,0:T(8,128)(2,1)}), bf16[16,3,64,128]{3,2,1,0:T(8,128)(2,1)S(1)}, u32[]{:S(2)}, u32[]{:S(2)}) %all-to-all-start.1) | async-done | bytes 786464 | tf_op jit(solution)/shard_map/all_to_all | solution.py:377
  56.7 0.0 collective-permute-start.1
  56.7 2.3 %collective-permute-done.1.refs_1_ = bf16[16,3,64,128]{3,2,1,0:T(8,128)(2,1)S(1)} collective-permute-done((bf16[16,3,64,128]{3,2,1,0:T(8,128)(2,1)S(1)}, bf16[16,3,64,128]{3,2,1,0:T(8,128)(2,1)S(1)}, u32[]{:S(2)}, u32[]{:S(2)}) %collective-permute-start.1) | collective-permute-done | bytes 786464 | tf_op jit(solution)/shard_map/ppermute | solution.py:370
  59.0 2.9 %attend.3 = bf16[16,2,64,128]{3,2,1,0:T(8,128)(2,1)S(1)} custom-call(s32[2,4,304]{2,1,0:T(4,128)S(1)} %get-tuple-element.19.unit_ref, s32[2]{0:T(128)S(1)} %get-tuple-element.20.total_ref, bf16[16,3,64,128]{3,2,1,0:T(8,128)(2,1)S(1)} %all-to-all-done.1.refs_0_, bf16[16,3,64,128]{3,2,1,0:T(8,128)(2,1)S(1)} %collective-permute-done.1.refs_1_, ...), custom_call_target="tpu_custom_call" | custom-call | flops 10000000000 | bytes 6000000 | tf_op jit(solution)/shard_map/attend/pallas_call | solution.py:387
  61.9 19.4 %all_to_all.15.o_ref = bf16[16,2,64,128]{3,2,1,0:T(8,128)(2,1)S(1)} all-to-all(bf16[16,2,64,128]{3,2,1,0:T(8,128)(2,1)S(1)} %attend.3), channel_id=1, replica_groups={{0,16,8,24,4,20,12,28,2,18,10,26,6,22,14,30},{1,17,9,25,5,21,13,29,3,19..., dimensions={0} | all-to-all | bytes 1048576 | tf_op jit(solution)/shard_map/all_to_all | solution.py:413
  81.3 1.6 %unpack.1 = bf16[128,2048]{1,0:T(8,128)(2,1)} custom-call(s32[8,128]{1,0:T(8,128)S(1)} %get-tuple-element.15.table_ref, bf16[16,2,64,128]{3,2,1,0:T(8,128)(2,1)S(1)} %all_to_all.15.o_ref), custom_call_target="tpu_custom_call" | custom-call | tf_op jit(solution)/shard_map/unpack/pallas_call | solution.py:405
Async XLA Ops:
  3.5 28.3 %all-to-all-start = ((bf16[16,3,64,128]{3,2,1,0:T(8,128)(2,1)}), bf16[16,3,64,128]{3,2,1,0:T(8,128)(2,1)S(1)}, u32[]{:S(2)}, u32[]{:S(2)}) async-start(bf16[16,3,64,128]{3,2,1,0:T(8,128)(2,1)} %get-tuple-element.16), calls=%async_computation | async-start | bytes 1572864 | tf_op jit(solution)/shard_map/all_to_all | solution.py:372
  11.9 3.5 %copy-start = (s32[32,32,32]{2,1,0:T(8,128)S(1)}, s32[32,32,32]{2,1,0:T(8,128)}, u32[]{:S(2)}) copy-start(s32[32,32,32]{2,1,0:T(8,128)} %layout_ref.1) | copy-start | bytes 393220
  11.9 3.5 %copy-start.1 = (s32[32,32]{1,0:T(8,128)S(1)}, s32[32,32]{1,0:T(8,128)}, u32[]{:S(2)}) copy-start(s32[32,32]{1,0:T(8,128)} %counts_ref.3) | copy-start | bytes 12292
  31.9 4.1 %collective-permute-start = (bf16[16,3,64,128]{3,2,1,0:T(8,128)(2,1)S(1)}, bf16[16,3,64,128]{3,2,1,0:T(8,128)(2,1)S(1)}, u32[]{:S(2)}, u32[]{:S(2)}) collective-permute-start(bf16[16,3,64,128]{3,2,1,0:T(8,128)(2,1)S(1)} %all-to-all-done.refs_0_), channel_id=1, source_target_pairs={{0,1},{1,0},{2,3},{3,2},{4,5},{5,4},{6,7},{7,6},{8,9},{9,8},{10,11... | collective-permute-start | bytes 2359304 | tf_op jit(solution)/shard_map/ppermute | solution.py:370
  31.9 24.8 %all-to-all-start.1 = ((bf16[16,3,64,128]{3,2,1,0:T(8,128)(2,1)}), bf16[16,3,64,128]{3,2,1,0:T(8,128)(2,1)S(1)}, u32[]{:S(2)}, u32[]{:S(2)}) async-start(bf16[16,3,64,128]{3,2,1,0:T(8,128)(2,1)} %pack.3), calls=%async_computation.1 | async-start | bytes 1572864 | tf_op jit(solution)/shard_map/all_to_all | solution.py:377
  56.7 2.3 %collective-permute-start.1 = (bf16[16,3,64,128]{3,2,1,0:T(8,128)(2,1)S(1)}, bf16[16,3,64,128]{3,2,1,0:T(8,128)(2,1)S(1)}, u32[]{:S(2)}, u32[]{:S(2)}) collective-permute-start(bf16[16,3,64,128]{3,2,1,0:T(8,128)(2,1)S(1)} %all-to-all-done.1.refs_0_), channel_id=1, source_target_pairs={{0,1},{1,0},{2,3},{3,2},{4,5},{5,4},{6,7},{7,6},{8,9},{9,8},{10,11... | collective-permute-start | bytes 2359304 | tf_op jit(solution)/shard_map/ppermute | solution.py:370

commit v14 on v13

--- a/solution.py
+++ b/solution.py
@@ -118,7 +118,7 @@
     return sum(((value >> at) & 1) << (bits - 1 - at) for at in range(bits)) if bits else value
 
 
-def plan_kernel(uly, gather, table_ref, counts_ref, layout_ref, unit_ref, total_ref, lay_ref, sem):
+def plan_kernel(uly, gather, table_ref, counts_ref, layout_ref, unit_ref, total_ref, lay_ref, index_ref, sem):
     slots = total_ref.shape[0]
     groups = H // slots
     parts = groups // uly
@@ -141,10 +141,12 @@
     for copy in copies:
         copy.start()
 
-    def local(block):
+    def place_block(block, _):
         its = block // uly
-        return ((its % gather) ^ rest) * groups + (its // gather) * uly + mirror(block % uly, uly)
-
+        index_ref[block] = ((its % gather) ^ rest) * groups + (its // gather) * uly + mirror(block % uly, uly)
+        return 0
+
+    lax.fori_loop(0, counts_ref.shape[1], place_block, 0)
     for copy in copies:
         copy.wait()
     for slot in range(slots):
@@ -166,8 +168,8 @@
                 whole = 2 * step + 1 < count
                 second = jnp.where(whole, lay_ref[slot, token, jnp.minimum(2 * step + 1, KMAX - 1)], first)
                 unit_ref[slot, 0, base + step] = row
-                unit_ref[slot, 1, base + step] = local(first)
-                unit_ref[slot, 2, base + step] = local(second)
+                unit_ref[slot, 1, base + step] = index_ref[first]
+                unit_ref[slot, 2, base + step] = index_ref[second]
                 unit_ref[slot, 3, base + step] = whole.astype(jnp.int32)
                 return 0
 
@@ -345,7 +347,7 @@
         out_shape=(shape((slots, 4, groups * KMAX // 2 + 8 * UNROLL), jnp.int32), shape((slots,), jnp.int32)),
         in_specs=[SMEM, SMEM, VMEM],
         out_specs=(SMEM, SMEM),
-        scratch_shapes=[pltpu.SMEM((slots, groups, KMAX), jnp.int32), pltpu.SemaphoreType.DMA((slots, parts))],
+        scratch_shapes=[pltpu.SMEM((slots, groups, KMAX), jnp.int32), pltpu.SMEM((counts.shape[1],), jnp.int32), pltpu.SemaphoreType.DMA((slots, parts))],
         compiler_params=PARAMS,
         name="plan",
     )(table, counts, layout)

time: 83.3 us -> 83.1 us (level)
  Pallas kernels: 35.8 us -> 29.5 us
  waiting for transfers between devices: 15.2 us -> 21.2 us
    pallas_call x1, Pallas kernels: 13.4 us -> 7.07 us  [shards(): pl.pallas_call(functools.partial(plan_kernel, uly, gather), out_shape=(sh...]
    all_to_all x1, waiting for transfers between devices: 3.07 us -> 9.38 us  [shards(): arrived = swap(packed[0])]
  transfers between devices with their start and end apart: 4 -> 4, of which waited for: 3 -> 3; matrix products, arithmetic and copies ran while one was open for 0% -> 0% of each run, Pallas kernels for 33% -> 26%
where the time goes in v14:
time: 83.1 us; the launch traced here: 82.9 us
  Pallas kernels  29.5 us (35%)
  waiting for transfers between devices  21.2 us (26%)
  blocking collectives  19.6 us (24%)
  starting transfers between devices  12.5 us (15%)
    all_to_all x1, blocking collectives, shards(): swap(results[-1])  19.6 us
    pallas_call x2, Pallas kernels, shards(): pl.pallas_call(functools.partial(attend_kernel, slot, gather), out_shape=...  13.8 us
    all_to_all x1, waiting for transfers between devices, shards(): arrived, *results = lax.optimization_barrier((swap(packed[slot]), *results))  9.54 us
    all_to_all x1, waiting for transfers between devices, shards(): arrived = swap(packed[0])  9.38 us
    all_to_all x1, starting transfers between devices, shards(): arrived = swap(packed[0])  8.32 us
    pallas_call x1, Pallas kernels, shards(): pl.pallas_call(functools.partial(plan_kernel, uly, gather), out_shape=(sh...  7.07 us
    all_to_all x1, starting transfers between devices, shards(): arrived, *results = lax.optimization_barrier((swap(packed[slot]), *results))  4.12 us
    pallas_call x1, Pallas kernels, shards(): pl.pallas_call(functools.partial(pack_first_kernel, groups), out_shape=(s...  3.53 us
  transfers between devices with their start and end apart: 4, of which 3 were waited for; matrix products, arithmetic and copies ran while one was open for 0% of the time, Pallas kernels for 26%

profile of v14, /device:TPU:0, one launch (start us, length us, event | category | flops | bytes accessed | tf_op | source)
XLA Modules:
  0.0 82.9 jit_solution(3912613802988893451)
XLA Ops:
  0.0 3.5 %pack.2 = (s32[8,128]{1,0:T(8,128)S(1)}, bf16[16,3,64,128]{3,2,1,0:T(8,128)(2,1)}) custom-call(s32[32,32]{1,0:T(8,128)} %counts_ref.3, bf16[128,2048]{1,0:T(8,128)(2,1)} %q_hbm.1, bf16[128,2048]{1,0:T(8,128)(2,1)} %k_hbm.1, bf16[128,2048]{1,0:T(8,128)(2,1)} %v_hbm.1), custom_call_target="tpu_custom_call" | custom-call | tf_op jit(solution)/shard_map/pack/pallas_call | solution.py:323
  3.5 8.3 %all-to-all-start = ((bf16[16,3,64,128]{3,2,1,0:T(8,128)(2,1)}), bf16[16,3,64,128]{3,2,1,0:T(8,128)(2,1)S(1)}, u32[]{:S(2)}, u32[]{:S(2)}) async-start(bf16[16,3,64,128]{3,2,1,0:T(8,128)(2,1)} %get-tuple-element.16), calls=%async_computation | async-start | bytes 1572864 | tf_op jit(solution)/shard_map/all_to_all | solution.py:374
  11.9 0.0 copy-start
  11.9 0.0 copy-start.1
  11.9 3.5 %pack.3 = bf16[16,3,64,128]{3,2,1,0:T(8,128)(2,1)} custom-call(s32[8,128]{1,0:T(8,128)S(1)} %get-tuple-element.15.table_ref, bf16[128,2048]{1,0:T(8,128)(2,1)} %q_hbm.1, bf16[128,2048]{1,0:T(8,128)(2,1)} %k_hbm.1, bf16[128,2048]{1,0:T(8,128)(2,1)} %v_hbm.1), custom_call_target="tpu_custom_call" | custom-call | tf_op jit(solution)/shard_map/pack/pallas_call | solution.py:335
  15.4 0.0 copy-done
  15.4 0.0 copy-done.1
  15.4 7.1 %plan.1 = (s32[2,4,304]{2,1,0:T(4,128)S(1)}, s32[2]{0:T(128)S(1)}) custom-call(s32[8,128]{1,0:T(8,128)S(1)} %get-tuple-element.15.table_ref, s32[32,32]{1,0:T(8,128)S(1)} %copy-done.1, s32[32,32,32]{2,1,0:T(8,128)S(1)} %copy-done), custom_call_target="tpu_custom_call" | custom-call | tf_op jit(solution)/shard_map/plan/pallas_call | solution.py:345
  22.5 9.4 %all-to-all-done.refs_0_ = bf16[16,3,64,128]{3,2,1,0:T(8,128)(2,1)S(1)} async-done(((bf16[16,3,64,128]{3,2,1,0:T(8,128)(2,1)}), bf16[16,3,64,128]{3,2,1,0:T(8,128)(2,1)S(1)}, u32[]{:S(2)}, u32[]{:S(2)}) %all-to-all-start) | async-done | bytes 786464 | tf_op jit(solution)/shard_map/all_to_all | solution.py:374
  31.9 0.0 collective-permute-start
  31.9 4.1 %all-to-all-start.1 = ((bf16[16,3,64,128]{3,2,1,0:T(8,128)(2,1)}), bf16[16,3,64,128]{3,2,1,0:T(8,128)(2,1)S(1)}, u32[]{:S(2)}, u32[]{:S(2)}) async-start(bf16[16,3,64,128]{3,2,1,0:T(8,128)(2,1)} %pack.3), calls=%async_computation.1 | async-start | bytes 1572864 | tf_op jit(solution)/shard_map/all_to_all | solution.py:379
  36.0 0.0 collective-permute-done.refs_1_
  36.0 11.1 %attend.2.refs_2_ = bf16[16,64,128]{2,1,0:T(8,128)(2,1)S(1)} custom-call(s32[2,4,304]{2,1,0:T(4,128)S(1)} %get-tuple-element.19.unit_ref, s32[2]{0:T(128)S(1)} %get-tuple-element.20.total_ref, bf16[16,3,64,128]{3,2,1,0:T(8,128)(2,1)S(1)} %all-to-all-done.refs_0_, bf16[16,3,64,128]{3,2,1,0:T(8,128)(2,1)S(1)} %collective-permute-done.refs_1_), custom_call_target="tpu_custom_call" | custom-call | flops 10000000000 | bytes 6000000 | tf_op jit(solution)/shard_map/attend/pallas_call | solution.py:389
  47.1 9.5 %all-to-all-done.1.refs_0_ = bf16[16,3,64,128]{3,2,1,0:T(8,128)(2,1)S(1)} async-done(((bf16[16,3,64,128]{3,2,1,0:T(8,128)(2,1)}), bf16[16,3,64,128]{3,2,1,0:T(8,128)(2,1)S(1)}, u32[]{:S(2)}, u32[]{:S(2)}) %all-to-all-start.1) | async-done | bytes 786464 | tf_op jit(solution)/shard_map/all_to_all | solution.py:379
  56.7 0.0 collective-permute-start.1
  56.7 2.3 %collective-permute-done.1.refs_1_ = bf16[16,3,64,128]{3,2,1,0:T(8,128)(2,1)S(1)} collective-permute-done((bf16[16,3,64,128]{3,2,1,0:T(8,128)(2,1)S(1)}, bf16[16,3,64,128]{3,2,1,0:T(8,128)(2,1)S(1)}, u32[]{:S(2)}, u32[]{:S(2)}) %collective-permute-start.1) | collective-permute-done | bytes 786464 | tf_op jit(solution)/shard_map/ppermute | solution.py:372
  59.0 2.7 %attend.3 = bf16[16,2,64,128]{3,2,1,0:T(8,128)(2,1)S(1)} custom-call(s32[2,4,304]{2,1,0:T(4,128)S(1)} %get-tuple-element.19.unit_ref, s32[2]{0:T(128)S(1)} %get-tuple-element.20.total_ref, bf16[16,3,64,128]{3,2,1,0:T(8,128)(2,1)S(1)} %all-to-all-done.1.refs_0_, bf16[16,3,64,128]{3,2,1,0:T(8,128)(2,1)S(1)} %collective-permute-done.1.refs_1_, ...), custom_call_target="tpu_custom_call" | custom-call | flops 10000000000 | bytes 6000000 | tf_op jit(solution)/shard_map/attend/pallas_call | solution.py:389
  61.7 19.6 %all_to_all.15.o_ref = bf16[16,2,64,128]{3,2,1,0:T(8,128)(2,1)S(1)} all-to-all(bf16[16,2,64,128]{3,2,1,0:T(8,128)(2,1)S(1)} %attend.3), channel_id=1, replica_groups={{0,16,8,24,4,20,12,28,2,18,10,26,6,22,14,30},{1,17,9,25,5,21,13,29,3,19..., dimensions={0} | all-to-all | bytes 1048576 | tf_op jit(solution)/shard_map/all_to_all | solution.py:415
  81.3 1.6 %unpack.1 = bf16[128,2048]{1,0:T(8,128)(2,1)} custom-call(s32[8,128]{1,0:T(8,128)S(1)} %get-tuple-element.15.table_ref, bf16[16,2,64,128]{3,2,1,0:T(8,128)(2,1)S(1)} %all_to_all.15.o_ref), custom_call_target="tpu_custom_call" | custom-call | tf_op jit(solution)/shard_map/unpack/pallas_call | solution.py:407
Async XLA Ops:
  3.5 28.3 %all-to-all-start = ((bf16[16,3,64,128]{3,2,1,0:T(8,128)(2,1)}), bf16[16,3,64,128]{3,2,1,0:T(8,128)(2,1)S(1)}, u32[]{:S(2)}, u32[]{:S(2)}) async-start(bf16[16,3,64,128]{3,2,1,0:T(8,128)(2,1)} %get-tuple-element.16), calls=%async_computation | async-start | bytes 1572864 | tf_op jit(solution)/shard_map/all_to_all | solution.py:374
  11.9 3.5 %copy-start = (s32[32,32,32]{2,1,0:T(8,128)S(1)}, s32[32,32,32]{2,1,0:T(8,128)}, u32[]{:S(2)}) copy-start(s32[32,32,32]{2,1,0:T(8,128)} %layout_ref.1) | copy-start | bytes 393220
  11.9 3.5 %copy-start.1 = (s32[32,32]{1,0:T(8,128)S(1)}, s32[32,32]{1,0:T(8,128)}, u32[]{:S(2)}) copy-start(s32[32,32]{1,0:T(8,128)} %counts_ref.3) | copy-start | bytes 12292
  31.9 4.1 %collective-permute-start = (bf16[16,3,64,128]{3,2,1,0:T(8,128)(2,1)S(1)}, bf16[16,3,64,128]{3,2,1,0:T(8,128)(2,1)S(1)}, u32[]{:S(2)}, u32[]{:S(2)}) collective-permute-start(bf16[16,3,64,128]{3,2,1,0:T(8,128)(2,1)S(1)} %all-to-all-done.refs_0_), channel_id=1, source_target_pairs={{0,1},{1,0},{2,3},{3,2},{4,5},{5,4},{6,7},{7,6},{8,9},{9,8},{10,11... | collective-permute-start | bytes 2359304 | tf_op jit(solution)/shard_map/ppermute | solution.py:372
  31.9 24.8 %all-to-all-start.1 = ((bf16[16,3,64,128]{3,2,1,0:T(8,128)(2,1)}), bf16[16,3,64,128]{3,2,1,0:T(8,128)(2,1)S(1)}, u32[]{:S(2)}, u32[]{:S(2)}) async-start(bf16[16,3,64,128]{3,2,1,0:T(8,128)(2,1)} %pack.3), calls=%async_computation.1 | async-start | bytes 1572864 | tf_op jit(solution)/shard_map/all_to_all | solution.py:379
  56.7 2.3 %collective-permute-start.1 = (bf16[16,3,64,128]{3,2,1,0:T(8,128)(2,1)S(1)}, bf16[16,3,64,128]{3,2,1,0:T(8,128)(2,1)S(1)}, u32[]{:S(2)}, u32[]{:S(2)}) collective-permute-start(bf16[16,3,64,128]{3,2,1,0:T(8,128)(2,1)S(1)} %all-to-all-done.1.refs_0_), channel_id=1, source_target_pairs={{0,1},{1,0},{2,3},{3,2},{4,5},{5,4},{6,7},{7,6},{8,9},{9,8},{10,11... | collective-permute-start | bytes 2359304 | tf_op jit(solution)/shard_map/ppermute | solution.py:372

commit v15 on v14

--- a/solution.py
+++ b/solution.py
@@ -11,7 +11,7 @@
 DH = 64
 BLK = 128
 KMAX = 32
-UNROLL = 6
+UNROLL = 7
 BIG = 1e30
 F32 = jnp.float32
 BF16 = jnp.bfloat16

time: 83.1 us -> 82.9 us (level)
  no operation moved by 1% of the time
where the time goes in v15:
time: 82.9 us; the launch traced here: 82.5 us
  Pallas kernels  29.7 us (36%)
  waiting for transfers between devices  21.1 us (25%)
  blocking collectives  19.1 us (23%)
  starting transfers between devices  12.5 us (15%)
    all_to_all x1, blocking collectives, shards(): swap(results[-1])  19.1 us
    pallas_call x2, Pallas kernels, shards(): pl.pallas_call(functools.partial(attend_kernel, slot, gather), out_shape=...  13.8 us
    all_to_all x1, waiting for transfers between devices, shards(): arrived, *results = lax.optimization_barrier((swap(packed[slot]), *results))  9.63 us
    all_to_all x1, waiting for transfers between devices, shards(): arrived = swap(packed[0])  9.15 us
    all_to_all x1, starting transfers between devices, shards(): arrived = swap(packed[0])  8.32 us
    pallas_call x1, Pallas kernels, shards(): pl.pallas_call(functools.partial(plan_kernel, uly, gather), out_shape=(sh...  7.31 us
    all_to_all x1, starting transfers between devices, shards(): arrived, *results = lax.optimization_barrier((swap(packed[slot]), *results))  4.12 us
    pallas_call x1, Pallas kernels, shards(): pl.pallas_call(functools.partial(pack_first_kernel, groups), out_shape=(s...  3.53 us
  transfers between devices with their start and end apart: 4, of which 3 were waited for; matrix products, arithmetic and copies ran while one was open for 0% of the time, Pallas kernels for 26%

profile of v15, /device:TPU:0, one launch (start us, length us, event | category | flops | bytes accessed | tf_op | source)
XLA Modules:
  0.0 82.5 jit_solution(800070560523593982)
XLA Ops:
  0.0 3.5 %pack.2 = (s32[8,128]{1,0:T(8,128)S(1)}, bf16[16,3,64,128]{3,2,1,0:T(8,128)(2,1)}) custom-call(s32[32,32]{1,0:T(8,128)} %counts_ref.3, bf16[128,2048]{1,0:T(8,128)(2,1)} %q_hbm.1, bf16[128,2048]{1,0:T(8,128)(2,1)} %k_hbm.1, bf16[128,2048]{1,0:T(8,128)(2,1)} %v_hbm.1), custom_call_target="tpu_custom_call" | custom-call | tf_op jit(solution)/shard_map/pack/pallas_call | solution.py:323
  3.5 8.3 %all-to-all-start = ((bf16[16,3,64,128]{3,2,1,0:T(8,128)(2,1)}), bf16[16,3,64,128]{3,2,1,0:T(8,128)(2,1)S(1)}, u32[]{:S(2)}, u32[]{:S(2)}) async-start(bf16[16,3,64,128]{3,2,1,0:T(8,128)(2,1)} %get-tuple-element.16), calls=%async_computation | async-start | bytes 1572864 | tf_op jit(solution)/shard_map/all_to_all | solution.py:374
  11.9 0.0 copy-start
  11.9 0.0 copy-start.1
  11.9 3.5 %pack.3 = bf16[16,3,64,128]{3,2,1,0:T(8,128)(2,1)} custom-call(s32[8,128]{1,0:T(8,128)S(1)} %get-tuple-element.15.table_ref, bf16[128,2048]{1,0:T(8,128)(2,1)} %q_hbm.1, bf16[128,2048]{1,0:T(8,128)(2,1)} %k_hbm.1, bf16[128,2048]{1,0:T(8,128)(2,1)} %v_hbm.1), custom_call_target="tpu_custom_call" | custom-call | tf_op jit(solution)/shard_map/pack/pallas_call | solution.py:335
  15.4 0.0 copy-done
  15.4 0.0 copy-done.1
  15.4 7.3 %plan.1 = (s32[2,4,312]{2,1,0:T(4,128)S(1)}, s32[2]{0:T(128)S(1)}) custom-call(s32[8,128]{1,0:T(8,128)S(1)} %get-tuple-element.15.table_ref, s32[32,32]{1,0:T(8,128)S(1)} %copy-done.1, s32[32,32,32]{2,1,0:T(8,128)S(1)} %copy-done), custom_call_target="tpu_custom_call" | custom-call | tf_op jit(solution)/shard_map/plan/pallas_call | solution.py:345
  22.7 9.1 %all-to-all-done.refs_0_ = bf16[16,3,64,128]{3,2,1,0:T(8,128)(2,1)S(1)} async-done(((bf16[16,3,64,128]{3,2,1,0:T(8,128)(2,1)}), bf16[16,3,64,128]{3,2,1,0:T(8,128)(2,1)S(1)}, u32[]{:S(2)}, u32[]{:S(2)}) %all-to-all-start) | async-done | bytes 786464 | tf_op jit(solution)/shard_map/all_to_all | solution.py:374
  31.9 0.0 collective-permute-start
  31.9 4.1 %all-to-all-start.1 = ((bf16[16,3,64,128]{3,2,1,0:T(8,128)(2,1)}), bf16[16,3,64,128]{3,2,1,0:T(8,128)(2,1)S(1)}, u32[]{:S(2)}, u32[]{:S(2)}) async-start(bf16[16,3,64,128]{3,2,1,0:T(8,128)(2,1)} %pack.3), calls=%async_computation.1 | async-start | bytes 1572864 | tf_op jit(solution)/shard_map/all_to_all | solution.py:379
  36.0 0.0 collective-permute-done.refs_1_
  36.0 11.0 %attend.2.refs_2_ = bf16[16,64,128]{2,1,0:T(8,128)(2,1)S(1)} custom-call(s32[2,4,312]{2,1,0:T(4,128)S(1)} %get-tuple-element.19.unit_ref, s32[2]{0:T(128)S(1)} %get-tuple-element.20.total_ref, bf16[16,3,64,128]{3,2,1,0:T(8,128)(2,1)S(1)} %all-to-all-done.refs_0_, bf16[16,3,64,128]{3,2,1,0:T(8,128)(2,1)S(1)} %collective-permute-done.refs_1_), custom_call_target="tpu_custom_call" | custom-call | flops 10000000000 | bytes 6000000 | tf_op jit(solution)/shard_map/attend/pallas_call | solution.py:389
  47.1 9.6 %all-to-all-done.1.refs_0_ = bf16[16,3,64,128]{3,2,1,0:T(8,128)(2,1)S(1)} async-done(((bf16[16,3,64,128]{3,2,1,0:T(8,128)(2,1)}), bf16[16,3,64,128]{3,2,1,0:T(8,128)(2,1)S(1)}, u32[]{:S(2)}, u32[]{:S(2)}) %all-to-all-start.1) | async-done | bytes 786464 | tf_op jit(solution)/shard_map/all_to_all | solution.py:379
  56.7 0.0 collective-permute-start.1
  56.7 2.3 %collective-permute-done.1.refs_1_ = bf16[16,3,64,128]{3,2,1,0:T(8,128)(2,1)S(1)} collective-permute-done((bf16[16,3,64,128]{3,2,1,0:T(8,128)(2,1)S(1)}, bf16[16,3,64,128]{3,2,1,0:T(8,128)(2,1)S(1)}, u32[]{:S(2)}, u32[]{:S(2)}) %collective-permute-start.1) | collective-permute-done | bytes 786464 | tf_op jit(solution)/shard_map/ppermute | solution.py:372
  59.0 2.8 %attend.3 = bf16[16,2,64,128]{3,2,1,0:T(8,128)(2,1)S(1)} custom-call(s32[2,4,312]{2,1,0:T(4,128)S(1)} %get-tuple-element.19.unit_ref, s32[2]{0:T(128)S(1)} %get-tuple-element.20.total_ref, bf16[16,3,64,128]{3,2,1,0:T(8,128)(2,1)S(1)} %all-to-all-done.1.refs_0_, bf16[16,3,64,128]{3,2,1,0:T(8,128)(2,1)S(1)} %collective-permute-done.1.refs_1_, ...), custom_call_target="tpu_custom_call" | custom-call | flops 10000000000 | bytes 6000000 | tf_op jit(solution)/shard_map/attend/pallas_call | solution.py:389
  61.8 19.1 %all_to_all.15.o_ref = bf16[16,2,64,128]{3,2,1,0:T(8,128)(2,1)S(1)} all-to-all(bf16[16,2,64,128]{3,2,1,0:T(8,128)(2,1)S(1)} %attend.3), channel_id=1, replica_groups={{0,16,8,24,4,20,12,28,2,18,10,26,6,22,14,30},{1,17,9,25,5,21,13,29,3,19..., dimensions={0} | all-to-all | bytes 1048576 | tf_op jit(solution)/shard_map/all_to_all | solution.py:415
  80.9 1.6 %unpack.1 = bf16[128,2048]{1,0:T(8,128)(2,1)} custom-call(s32[8,128]{1,0:T(8,128)S(1)} %get-tuple-element.15.table_ref, bf16[16,2,64,128]{3,2,1,0:T(8,128)(2,1)S(1)} %all_to_all.15.o_ref), custom_call_target="tpu_custom_call" | custom-call | tf_op jit(solution)/shard_map/unpack/pallas_call | solution.py:407
Async XLA Ops:
  3.5 28.3 %all-to-all-start = ((bf16[16,3,64,128]{3,2,1,0:T(8,128)(2,1)}), bf16[16,3,64,128]{3,2,1,0:T(8,128)(2,1)S(1)}, u32[]{:S(2)}, u32[]{:S(2)}) async-start(bf16[16,3,64,128]{3,2,1,0:T(8,128)(2,1)} %get-tuple-element.16), calls=%async_computation | async-start | bytes 1572864 | tf_op jit(solution)/shard_map/all_to_all | solution.py:374
  11.9 3.5 %copy-start = (s32[32,32,32]{2,1,0:T(8,128)S(1)}, s32[32,32,32]{2,1,0:T(8,128)}, u32[]{:S(2)}) copy-start(s32[32,32,32]{2,1,0:T(8,128)} %layout_ref.1) | copy-start | bytes 393220
  11.9 3.5 %copy-start.1 = (s32[32,32]{1,0:T(8,128)S(1)}, s32[32,32]{1,0:T(8,128)}, u32[]{:S(2)}) copy-start(s32[32,32]{1,0:T(8,128)} %counts_ref.3) | copy-start | bytes 12292
  31.9 4.1 %collective-permute-start = (bf16[16,3,64,128]{3,2,1,0:T(8,128)(2,1)S(1)}, bf16[16,3,64,128]{3,2,1,0:T(8,128)(2,1)S(1)}, u32[]{:S(2)}, u32[]{:S(2)}) collective-permute-start(bf16[16,3,64,128]{3,2,1,0:T(8,128)(2,1)S(1)} %all-to-all-done.refs_0_), channel_id=1, source_target_pairs={{0,1},{1,0},{2,3},{3,2},{4,5},{5,4},{6,7},{7,6},{8,9},{9,8},{10,11... | collective-permute-start | bytes 2359304 | tf_op jit(solution)/shard_map/ppermute | solution.py:372
  31.9 24.8 %all-to-all-start.1 = ((bf16[16,3,64,128]{3,2,1,0:T(8,128)(2,1)}), bf16[16,3,64,128]{3,2,1,0:T(8,128)(2,1)S(1)}, u32[]{:S(2)}, u32[]{:S(2)}) async-start(bf16[16,3,64,128]{3,2,1,0:T(8,128)(2,1)} %pack.3), calls=%async_computation.1 | async-start | bytes 1572864 | tf_op jit(solution)/shard_map/all_to_all | solution.py:379
  56.7 2.3 %collective-permute-start.1 = (bf16[16,3,64,128]{3,2,1,0:T(8,128)(2,1)S(1)}, bf16[16,3,64,128]{3,2,1,0:T(8,128)(2,1)S(1)}, u32[]{:S(2)}, u32[]{:S(2)}) collective-permute-start(bf16[16,3,64,128]{3,2,1,0:T(8,128)(2,1)S(1)} %all-to-all-done.1.refs_0_), channel_id=1, source_target_pairs={{0,1},{1,0},{2,3},{3,2},{4,5},{5,4},{6,7},{7,6},{8,9},{9,8},{10,11... | collective-permute-start | bytes 2359304 | tf_op jit(solution)/shard_map/ppermute | solution.py:372
